TPU v7x, 128 devices: a whole 4x4x4 slice. The times are simulated.
128 devices in a mesh: dp: 8 (over y_hi, z), seq: 16 (over x, y_lo, core).
Axes of the slice: x: 4, y: 4 (y_hi: 2, y_lo: 2; y = y_hi * 2 + y_lo), z: 4, core: 2. Of those that a mesh axis runs over, the one named last changes fastest.
Arguments:
- tokens: bfloat16 [8, 2048, 1024], P('dp', 'seq'), may hold values from -6 to 6
- positions: int32 [8, 2048], P('dp', 'seq'), may hold values from 0 to 2047, as said below
- in_gain: bfloat16 [1024], P(('dp', 'seq')), may hold values from 0.099609375 to 1.8984375
- q_gain: bfloat16 [128], P(('dp', 'seq')), may hold values from 0.099609375 to 1.8984375
- k_gain: bfloat16 [128], P(('dp', 'seq')), may hold values from 0.099609375 to 1.8984375
- w_query: bfloat16 [1024, 2048], P(('dp', 'seq')), may hold values from -0.1875 to 0.1875
- w_key: bfloat16 [1024, 1024], P(('dp', 'seq')), may hold values from -0.1875 to 0.1875
- w_value: bfloat16 [1024, 1024], P(('dp', 'seq')), may hold values from -0.1875 to 0.1875
- w_out: bfloat16 [2048, 1024], P(None, ('dp', 'seq')), may hold values from -4 to 4
- post_gain: bfloat16 [1024], P(('dp', 'seq')), may hold values from 0.099609375 to 1.8984375
- w_gate: bfloat16 [1024, 3072], P(('dp', 'seq')), may hold values from -0.1875 to 0.1875
- w_up: bfloat16 [1024, 3072], P(('dp', 'seq')), may hold values from -0.1875 to 0.1875
- w_down: bfloat16 [3072, 1024], P(None, ('dp', 'seq')), may hold values from -0.109375 to 0.109375
- cotangent: bfloat16 [8, 2048, 1024], P('dp', 'seq'), may hold values from -6 to 6
Outputs:
- output: bfloat16 [8, 2048, 1024], P('dp', 'seq')
- input_grad: bfloat16 [8, 2048, 1024], P('dp', 'seq')
- in_gain_grad: float32 [1024], P(('dp', 'seq'))
- q_gain_grad: float32 [128], P(('dp', 'seq'))
- k_gain_grad: float32 [128], P(('dp', 'seq'))
- query_grad: float32 [1024, 2048], P(('dp', 'seq'))
- key_grad: float32 [1024, 1024], P(('dp', 'seq'))
- value_grad: float32 [1024, 1024], P(('dp', 'seq'))
- out_grad: float32 [2048, 1024], P(None, ('dp', 'seq'))
- post_gain_grad: float32 [1024], P(('dp', 'seq'))
- gate_grad: float32 [1024, 3072], P(('dp', 'seq'))
- up_grad: float32 [1024, 3072], P(('dp', 'seq'))
- down_grad: float32 [3072, 1024], P(None, ('dp', 'seq'))
Inputs may be any that keep to these rules, and one draw needn't show every extreme that they name: `positions`: each sequence is a pack of documents and a token's position is its distance from the first token of its document; the first sequence is a single document.
All inputs are finite; a program needn't handle non-finite values.
Results may differ from a plain program's by a relative error of at most 0.035.
Values may be sent and summed in bfloat16 or wider, within the bound.
A program may use at most 256 MiB of HBM per device.

v0:
```python
import math

import jax
import jax.numpy as jnp
from jax import lax
from jax.sharding import PartitionSpec as P

HEADS = 16
KV_HEADS = 8
HEAD_DIM = 128
FF = 3072
BLOCK = 256


eps_norm = 1e-06
rope_base = 1000000.0
neg_big = -1e30


def contract(left_op, right_op, left_dim, right_dim):
    return lax.dot_general(
        left_op,
        right_op,
        (((left_dim,), (right_dim,)), ((), ())),
        preferred_element_type=jnp.float32,
    )


def rms_scale(values):
    return lax.rsqrt(jnp.mean(values * values, axis=-1, keepdims=True) + eps_norm)


def norm_back(grad_out, values, scale_factor, gain):
    weighted = grad_out * gain
    inner = jnp.mean(weighted * values, axis=-1, keepdims=True)
    grad_in = (
        scale_factor * weighted - values * (scale_factor * scale_factor * scale_factor) * inner
    )
    return (grad_in, grad_out * values * scale_factor)


def rope_tables(places):
    half_dim = HEAD_DIM // 2
    frequency = rope_base ** (-2.0 * jnp.arange(half_dim, dtype=jnp.float32) / HEAD_DIM)
    angles = places.astype(jnp.float32)[:, None] * frequency[None, :]
    cosine = jnp.cos(angles)
    sine_vals = jnp.sin(angles)
    return (
        jnp.concatenate([cosine, cosine], axis=-1),
        jnp.concatenate([sine_vals, sine_vals], axis=-1),
    )


def rotate(values, cosine, sine_vals):
    half_dim = values.shape[-1] // 2
    turned = jnp.concatenate([-values[..., half_dim:], values[..., :half_dim]], axis=-1)
    return values * cosine[:, None, :] + turned * sine_vals[:, None, :]


def rotate_back(grads, cosine, sine_vals):
    half_dim = grads.shape[-1] // 2
    moved = grads * sine_vals[:, None, :]
    return grads * cosine[:, None, :] + jnp.concatenate(
        [moved[..., half_dim:], -moved[..., :half_dim]], axis=-1
    )


def prepare_heads(normed_rows, query_mat, key_mat, value_mat, places_rows, gain_q, gain_k):
    rows = normed_rows.shape[0]
    query_pre = jnp.dot(normed_rows, query_mat, preferred_element_type=jnp.float32).reshape(
        rows, -1, HEAD_DIM
    )
    key_pre = jnp.dot(normed_rows, key_mat, preferred_element_type=jnp.float32).reshape(
        rows, -1, HEAD_DIM
    )
    value_low = jnp.dot(normed_rows, value_mat, preferred_element_type=jnp.float32).astype(
        jnp.bfloat16
    )
    query_scale = rms_scale(query_pre)
    key_scale = rms_scale(key_pre)
    cosine, sine_vals = rope_tables(places_rows)
    query_low = rotate(query_pre * query_scale * gain_q, cosine, sine_vals).astype(jnp.bfloat16)
    key_low = rotate(key_pre * key_scale * gain_k, cosine, sine_vals).astype(jnp.bfloat16)
    return (
        query_pre,
        key_pre,
        value_low,
        query_scale,
        key_scale,
        cosine,
        sine_vals,
        query_low,
        key_low,
    )


def heads_back(
    grad_query,
    key_sum,
    value_sum,
    query_pre,
    key_pre,
    query_scale,
    key_scale,
    cosine,
    sine_vals,
    gain_q,
    gain_k,
):
    rows = query_pre.shape[0]
    query_rot_grad = rotate_back(grad_query, cosine, sine_vals)
    query_pre_grad, q_terms = norm_back(query_rot_grad, query_pre, query_scale, gain_q)
    key_rot_grad = rotate_back(key_sum.reshape(key_pre.shape), cosine, sine_vals)
    key_pre_grad, k_terms = norm_back(key_rot_grad, key_pre, key_scale, gain_k)
    return (
        query_pre_grad.reshape(rows, -1).astype(jnp.bfloat16),
        key_pre_grad.reshape(rows, -1).astype(jnp.bfloat16),
        value_sum.astype(jnp.bfloat16),
        jnp.sum(q_terms, axis=(0, 1)),
        jnp.sum(k_terms, axis=(0, 1)),
    )


def feed_forward(hidden_rows, gate_mat, up_mat):
    gate_vals = jnp.dot(hidden_rows, gate_mat, preferred_element_type=jnp.float32)
    up_vals = jnp.dot(hidden_rows, up_mat, preferred_element_type=jnp.float32)
    act_low = (jax.nn.silu(gate_vals) * up_vals).astype(jnp.bfloat16)
    return (gate_vals, up_vals, act_low)


def feed_back(grad_act, gate_vals, up_vals):
    sigma = jax.nn.sigmoid(gate_vals)
    swish = gate_vals * sigma
    slope = sigma * (1.0 + gate_vals * (1.0 - sigma))
    return (
        (grad_act * up_vals * slope).astype(jnp.bfloat16),
        (grad_act * swish).astype(jnp.bfloat16),
    )


def block_plan(first_row, rows, length):
    key_block = min(512, length)
    query_marks = (first_row + jnp.arange(rows, dtype=jnp.int32)) // BLOCK
    key_end = (first_row + rows - 1) // BLOCK * BLOCK + BLOCK
    return (key_block, query_marks, (key_end + key_block - 1) // key_block)


def key_pieces(keys_all, values_all, block_num, key_block):
    offset = block_num * key_block
    kv_local = keys_all.shape[1] // HEAD_DIM
    key_piece = lax.dynamic_slice_in_dim(keys_all, offset, key_block, 0).reshape(
        key_block, kv_local, HEAD_DIM
    )
    value_piece = lax.dynamic_slice_in_dim(values_all, offset, key_block, 0).reshape(
        key_block, kv_local, HEAD_DIM
    )
    return (key_piece, value_piece)


def block_scores(query_grouped, key_piece, offset, query_marks):
    raw_scores = jnp.einsum(
        "tkgd,skd->kgts", query_grouped, key_piece, preferred_element_type=jnp.float32
    ) * (1.0 / math.sqrt(HEAD_DIM))
    key_marks = (offset + jnp.arange(key_piece.shape[0], dtype=jnp.int32)) // BLOCK
    allowed = key_marks[None, :] <= query_marks[:, None]
    return (jnp.where(allowed, raw_scores, neg_big), allowed)


def attend_forward(query_grouped, first_row, keys_all, values_all):
    rows = query_grouped.shape[0]
    kv_local = query_grouped.shape[1]
    group_local = query_grouped.shape[2]
    key_block, query_marks, block_count = block_plan(first_row, rows, keys_all.shape[0])

    def max_step(block_num, running):
        run_max, run_sum = running
        key_piece, value_piece = key_pieces(keys_all, values_all, block_num, key_block)
        scores, allowed = block_scores(query_grouped, key_piece, block_num * key_block, query_marks)
        new_max = jnp.maximum(run_max, jnp.max(scores, axis=-1))
        terms = jnp.where(allowed, jnp.exp(scores - new_max[..., None]), 0.0)
        return (new_max, run_sum * jnp.exp(run_max - new_max) + jnp.sum(terms, axis=-1))

    start_max = jnp.full((kv_local, group_local, rows), neg_big, jnp.float32)
    start_sum = jnp.zeros((kv_local, group_local, rows), jnp.float32)
    run_max, run_sum = lax.fori_loop(0, block_count, max_step, (start_max, start_sum))
    log_total = run_max + jnp.log(run_sum)

    def value_step(block_num, partial_value):
        key_piece, value_piece = key_pieces(keys_all, values_all, block_num, key_block)
        scores, allowed = block_scores(query_grouped, key_piece, block_num * key_block, query_marks)
        weights_low = jnp.where(allowed, jnp.exp(scores - log_total[..., None]), 0.0).astype(
            jnp.bfloat16
        )
        return partial_value + jnp.einsum(
            "kgts,skd->tkgd", weights_low, value_piece, preferred_element_type=jnp.float32
        )

    mixed = lax.fori_loop(
        0, block_count, value_step, jnp.zeros((rows, kv_local, group_local, HEAD_DIM), jnp.float32)
    )
    return (mixed, log_total)


def attend_backward(
    query_grouped,
    grad_grouped,
    mixed,
    log_total,
    first_row,
    keys_all,
    values_all,
    grad_keys,
    grad_values,
):
    rows = query_grouped.shape[0]
    kv_width = keys_all.shape[1]
    key_block, query_marks, block_count = block_plan(first_row, rows, keys_all.shape[0])
    delta = jnp.transpose(jnp.sum(grad_grouped.astype(jnp.float32) * mixed, axis=-1), (1, 2, 0))

    def back_step(block_num, running):
        grad_query, key_acc, value_acc = running
        key_piece, value_piece = key_pieces(keys_all, values_all, block_num, key_block)
        offset = block_num * key_block
        scores, allowed = block_scores(query_grouped, key_piece, offset, query_marks)
        probs = jnp.where(allowed, jnp.exp(scores - log_total[..., None]), 0.0)
        grad_probs = jnp.einsum(
            "tkgd,skd->kgts", grad_grouped, value_piece, preferred_element_type=jnp.float32
        )
        grad_scores = (probs * (grad_probs - delta[..., None])).astype(jnp.bfloat16)
        grad_query = grad_query + jnp.einsum(
            "kgts,skd->tkgd", grad_scores, key_piece, preferred_element_type=jnp.float32
        )
        key_term = jnp.einsum(
            "kgts,tkgd->skd", grad_scores, query_grouped, preferred_element_type=jnp.float32
        ).reshape(key_block, kv_width)
        value_term = jnp.einsum(
            "kgts,tkgd->skd",
            probs.astype(jnp.bfloat16),
            grad_grouped,
            preferred_element_type=jnp.float32,
        ).reshape(key_block, kv_width)
        key_old = lax.dynamic_slice_in_dim(key_acc, offset, key_block, 0)
        value_old = lax.dynamic_slice_in_dim(value_acc, offset, key_block, 0)
        key_acc = lax.dynamic_update_slice_in_dim(key_acc, key_old + key_term, offset, 0)
        value_acc = lax.dynamic_update_slice_in_dim(value_acc, value_old + value_term, offset, 0)
        return (grad_query, key_acc, value_acc)

    start_query = jnp.zeros(query_grouped.shape, jnp.float32)
    return lax.fori_loop(0, block_count, back_step, (start_query, grad_keys, grad_values))


def body(
    tokens,
    positions,
    in_gain,
    q_gain,
    k_gain,
    w_query,
    w_key,
    w_value,
    w_out,
    post_gain,
    w_gate,
    w_up,
    w_down,
    cotangent,
):
    seq_count = lax.axis_size("seq")
    seq_index = lax.axis_index("seq")
    tok_rows = tokens.shape[1]
    group_size = HEADS // KV_HEADS
    kv_width = KV_HEADS * HEAD_DIM
    length = tok_rows * seq_count
    score_scale = 1.0 / math.sqrt(HEAD_DIM)
    inputs = tokens[0].astype(jnp.float32)
    places = positions[0]
    grad_low = cotangent[0]
    scale_in = rms_scale(inputs)
    (
        full_in,
        full_q,
        full_k,
        full_post,
        query_full,
        key_full,
        value_full,
        out_full,
        gate_full,
        up_full,
        down_full,
    ) = (
        lax.all_gather(in_gain, ("dp", "seq"), axis=0, tiled=True),
        lax.all_gather(q_gain, ("dp", "seq"), axis=0, tiled=True),
        lax.all_gather(k_gain, ("dp", "seq"), axis=0, tiled=True),
        lax.all_gather(post_gain, ("dp", "seq"), axis=0, tiled=True),
        lax.all_gather(w_query, ("dp", "seq"), axis=0, tiled=True),
        lax.all_gather(w_key, ("dp", "seq"), axis=0, tiled=True),
        lax.all_gather(w_value, ("dp", "seq"), axis=0, tiled=True),
        lax.all_gather(w_out, ("dp", "seq"), axis=1, tiled=True),
        lax.all_gather(w_gate, ("dp", "seq"), axis=0, tiled=True),
        lax.all_gather(w_up, ("dp", "seq"), axis=0, tiled=True),
        lax.all_gather(w_down, ("dp", "seq"), axis=1, tiled=True),
    )
    gain_in = full_in.astype(jnp.float32)
    gain_q = full_q.astype(jnp.float32)
    gain_k = full_k.astype(jnp.float32)
    gain_post = full_post.astype(jnp.float32)
    normed = (inputs * scale_in * gain_in).astype(jnp.bfloat16)
    query_pre, key_pre, value_low, query_scale, key_scale, cosine, sine_vals, query_low, key_low = (
        prepare_heads(normed, query_full, key_full, value_full, places, gain_q, gain_k)
    )
    keys_all, values_all = (
        lax.all_gather(key_low.reshape(tok_rows, kv_width), "seq", axis=0, tiled=True),
        lax.all_gather(value_low, "seq", axis=0, tiled=True),
    )
    query_grouped = query_low.reshape(tok_rows, KV_HEADS, group_size, HEAD_DIM)
    first_row = seq_index * tok_rows
    mixed, log_total = attend_forward(query_grouped, first_row, keys_all, values_all)
    attended_low = mixed.reshape(tok_rows, HEADS * HEAD_DIM).astype(jnp.bfloat16)
    middle = inputs + jnp.dot(attended_low, out_full, preferred_element_type=jnp.float32)
    scale_post = rms_scale(middle)
    hidden_in = (middle * scale_post * gain_post).astype(jnp.bfloat16)
    gate_vals, up_vals, act_low = feed_forward(hidden_in, gate_full, up_full)
    output = (middle + jnp.dot(act_low, down_full, preferred_element_type=jnp.float32)).astype(
        jnp.bfloat16
    )
    query_again, key_again, value_again, out_again, gate_again, up_again, down_again = (
        lax.all_gather(w_query, ("dp", "seq"), axis=0, tiled=True),
        lax.all_gather(w_key, ("dp", "seq"), axis=0, tiled=True),
        lax.all_gather(w_value, ("dp", "seq"), axis=0, tiled=True),
        lax.all_gather(w_out, ("dp", "seq"), axis=1, tiled=True),
        lax.all_gather(w_gate, ("dp", "seq"), axis=0, tiled=True),
        lax.all_gather(w_up, ("dp", "seq"), axis=0, tiled=True),
        lax.all_gather(w_down, ("dp", "seq"), axis=1, tiled=True),
    )
    grad_act = contract(grad_low, down_again, 1, 1)
    grad_gate, grad_up = feed_back(grad_act, gate_vals, up_vals)
    grad_hidden = contract(grad_gate, gate_again, 1, 1) + contract(grad_up, up_again, 1, 1)
    summed = lax.psum_scatter(
        jnp.concatenate(
            [
                contract(hidden_in, grad_gate, 0, 0),
                contract(hidden_in, grad_up, 0, 0),
                contract(grad_low, act_low, 0, 0),
            ],
            axis=1,
        ),
        ("dp", "seq"),
        scatter_dimension=0,
        tiled=True,
    )
    gate_grad = summed[:, :FF]
    up_grad = summed[:, FF : 2 * FF]
    down_grad = jnp.transpose(summed[:, 2 * FF :])
    grad_mid_in, post_terms = norm_back(grad_hidden, middle, scale_post, gain_post)
    grad_middle = grad_low.astype(jnp.float32) + grad_mid_in
    branch_grad = grad_middle.astype(jnp.bfloat16)
    grad_att = contract(branch_grad, out_again, 1, 1).astype(jnp.bfloat16)
    out_weight_grad = contract(attended_low, branch_grad, 0, 0)
    grad_grouped = grad_att.reshape(tok_rows, KV_HEADS, group_size, HEAD_DIM)
    start_keys = jnp.zeros((length, kv_width), jnp.float32)
    grad_query, grad_keys, grad_values = attend_backward(
        query_grouped,
        grad_grouped,
        mixed,
        log_total,
        first_row,
        keys_all,
        values_all,
        start_keys,
        start_keys,
    )
    key_sum, value_sum = (
        lax.psum_scatter(
            (grad_keys * score_scale).astype(jnp.bfloat16), "seq", scatter_dimension=0, tiled=True
        ).astype(jnp.float32),
        lax.psum_scatter(
            grad_values.astype(jnp.bfloat16), "seq", scatter_dimension=0, tiled=True
        ).astype(jnp.float32),
    )
    query_grad_low, key_grad_low, value_grad_low, q_gain_part, k_gain_part = heads_back(
        grad_query.reshape(tok_rows, HEADS, HEAD_DIM) * score_scale,
        key_sum,
        value_sum,
        query_pre,
        key_pre,
        query_scale,
        key_scale,
        cosine,
        sine_vals,
        gain_q,
        gain_k,
    )
    query_weight_grad = contract(normed, query_grad_low, 0, 0)
    key_weight_grad = contract(normed, key_grad_low, 0, 0)
    value_weight_grad = contract(normed, value_grad_low, 0, 0)
    grad_normed = (
        contract(query_grad_low, query_again, 1, 1)
        + contract(key_grad_low, key_again, 1, 1)
        + contract(value_grad_low, value_again, 1, 1)
    )
    grad_in_part, in_terms = norm_back(grad_normed, inputs, scale_in, gain_in)
    input_grad = (grad_middle + grad_in_part).astype(jnp.bfloat16)
    (
        in_gain_grad,
        q_gain_grad,
        k_gain_grad,
        post_gain_grad,
        query_grad,
        key_grad,
        value_grad,
        out_grad,
    ) = (
        lax.psum_scatter(jnp.sum(in_terms, axis=0), ("dp", "seq"), scatter_dimension=0, tiled=True),
        lax.psum_scatter(q_gain_part, ("dp", "seq"), scatter_dimension=0, tiled=True),
        lax.psum_scatter(k_gain_part, ("dp", "seq"), scatter_dimension=0, tiled=True),
        lax.psum_scatter(
            jnp.sum(post_terms, axis=0), ("dp", "seq"), scatter_dimension=0, tiled=True
        ),
        lax.psum_scatter(query_weight_grad, ("dp", "seq"), scatter_dimension=0, tiled=True),
        lax.psum_scatter(key_weight_grad, ("dp", "seq"), scatter_dimension=0, tiled=True),
        lax.psum_scatter(value_weight_grad, ("dp", "seq"), scatter_dimension=0, tiled=True),
        lax.psum_scatter(out_weight_grad, ("dp", "seq"), scatter_dimension=1, tiled=True),
    )
    return (
        output[None],
        input_grad[None],
        in_gain_grad,
        q_gain_grad,
        k_gain_grad,
        query_grad,
        key_grad,
        value_grad,
        out_grad,
        post_gain_grad,
        gate_grad,
        up_grad,
        down_grad,
    )


def solution(mesh):
    placed = (
        P("dp", "seq", None),
        P("dp", "seq"),
        P(("dp", "seq")),
        P(("dp", "seq")),
        P(("dp", "seq")),
        P(("dp", "seq"), None),
        P(("dp", "seq"), None),
        P(("dp", "seq"), None),
        P(None, ("dp", "seq")),
        P(("dp", "seq")),
        P(("dp", "seq"), None),
        P(("dp", "seq"), None),
        P(None, ("dp", "seq")),
        P("dp", "seq", None),
    )
    return jax.shard_map(
        body,
        mesh=mesh,
        in_specs=placed,
        out_specs=(
            P("dp", "seq", None),
            P("dp", "seq", None),
            P(("dp", "seq")),
            P(("dp", "seq")),
            P(("dp", "seq")),
            P(("dp", "seq"), None),
            P(("dp", "seq"), None),
            P(("dp", "seq"), None),
            P(None, ("dp", "seq")),
            P(("dp", "seq")),
            P(("dp", "seq"), None),
            P(("dp", "seq"), None),
            P(None, ("dp", "seq")),
        ),
        check_vma=False,
    )
```

profile of v0, /device:TPU:1, one launch (start us, length us, event | category | flops | bytes accessed | tf_op | source)
XLA Modules:
  0.0 4986.3 jit_solution(4410123356168087583)
XLA Ops:
  12.7 68.9 %all-reduce.9 = (bf16[1024]{0:T(1024)(128)(2,1)S(1)}, bf16[128]{0:T(256)(128)(2,1)S(1)}, bf16[128]{0:T(256)(128)(2,1)S(1)}, bf16[1024]{0:T(1024)(128)(2,1)S(1)}) all-reduce(bf16[1024]{0:T(1024)(128)(2,1)S(1)} %dynamic-update-slice, bf16[128]{0:T(256)(128)(2,1)S(1)} %dynamic-update-slice.1, ...), channel_id=1, replica_groups=mesh['dp'=8,'seq'=16] {'dp','seq'}, use_global_device_ids=true, to_apply=%add | all-reduce | flops 2304 | bytes 9216
  83.2 123.8 %all-gather.10.cloned.1.call-done = bf16[1024,1024]{1,0:T(8,128)(2,1)} async-done(((bf16[8,1024]{1,0:T(8,128)(2,1)}), bf16[1024,1024]{1,0:T(8,128)(2,1)}) %all-gather.10.cloned.1.call-update) | async-done | bytes 2097168 | tf_op jit(solution)/shard_map/all_gather | solution.py:298
  211.6 190.0 %all-gather.14.cloned.1.call-done = bf16[1024,1024]{1,0:T(8,128)(2,1)} async-done(((bf16[8,1024]{1,0:T(8,128)(2,1)}), bf16[1024,1024]{1,0:T(8,128)(2,1)}) %all-gather.14.cloned.1.call-update) | async-done | bytes 2097168 | tf_op jit(solution)/shard_map/all_gather | solution.py:297
  409.9 189.9 %all-gather.18.cloned.1.call-done = bf16[1024,2048]{1,0:T(8,128)(2,1)} async-done(((bf16[8,2048]{1,0:T(8,128)(2,1)}), bf16[1024,2048]{1,0:T(8,128)(2,1)}) %all-gather.18.cloned.1.call-update) | async-done | bytes 4194320 | tf_op jit(solution)/shard_map/all_gather | solution.py:296
  599.8 6.4 copy.90
  611.4 27.1 all-gather.12.cloned.1.call-done
  638.5 6.5 copy.92
  645.0 40.6 all-gather.16.cloned.1.call-done
  697.3 187.3 %all-gather.20.cloned.1.call-done = bf16[2048,1024]{0,1:T(8,128)(2,1)} async-done(((bf16[2048,8]{0,1:T(8,128)(2,1)}), bf16[2048,1024]{0,1:T(8,128)(2,1)}) %all-gather.20.cloned.1.call-update) | async-done | bytes 4194320 | tf_op jit(solution)/shard_map/all_gather | solution.py:299
  888.6 197.6 %all-gather.24.cloned.1.call-done = bf16[1024,3072]{1,0:T(8,128)(2,1)} async-done(((bf16[8,3072]{1,0:T(8,128)(2,1)}), bf16[1024,3072]{1,0:T(8,128)(2,1)}) %all-gather.24.cloned.1.call-update) | async-done | bytes 6291472 | tf_op jit(solution)/shard_map/all_gather | solution.py:301
  1090.0 197.7 %all-gather.22.cloned.1.call-done = bf16[1024,3072]{1,0:T(8,128)(2,1)} async-done(((bf16[8,3072]{1,0:T(8,128)(2,1)}), bf16[1024,3072]{1,0:T(8,128)(2,1)}) %all-gather.22.cloned.1.call-update) | async-done | bytes 6291472 | tf_op jit(solution)/shard_map/all_gather | solution.py:300
  1292.7 196.6 %all-gather.26.cloned.1.call-done = bf16[3072,1024]{0,1:T(8,128)(2,1)} async-done(((bf16[3072,8]{0,1:T(8,128)(2,1)}), bf16[3072,1024]{0,1:T(8,128)(2,1)}) %all-gather.26.cloned.1.call-update) | async-done | bytes 6291472 | tf_op jit(solution)/shard_map/all_gather | solution.py:302
  1514.3 13.1 while.47
  1539.9 6.6 multiply_convert_fusion
  1560.4 6.4 fusion.100
  1573.2 26.4 pad_maximum_fusion
  1605.3 34.9 reduce-scatter.24.cloned.1.call-done
  1644.1 64.8 %reduce-scatter.22.cloned.1.call-done = bf16[128,1024]{1,0:T(8,128)(2,1)} async-done(((bf16[2048,1024]{1,0:T(8,128)(2,1)}), bf16[128,1024]{1,0:T(8,128)(2,1)}) %reduce-scatter.22.cloned.1.call-update) | async-done | bytes 262160
  1731.5 70.1 %all-reduce.8 = (f32[1024]{0:T(1024)S(1)}, f32[128]{0:T(128)S(1)}, f32[128]{0:T(128)S(1)}, f32[1024]{0:T(1024)S(1)}) all-reduce(f32[1024]{0:T(1024)S(1)} %get-tuple-element.553, f32[128]{0:T(128)S(1)} %get-tuple-element.547, f32[128]{0:T(128)S(1)} %get-tuple-element.549, ...), channel_id=4, replica_groups=mesh['dp'=8,'seq'=16] {'dp','seq'}, use_global_device_ids=true, to_apply=%region_20.21.clone | all-reduce | flops 2304 | bytes 18432
  1804.9 602.5 %reduce-scatter.20.cloned.1.call-done = f32[8,9216]{1,0:T(8,128)} async-done(((f32[1024,9216]{1,0:T(8,128)}), f32[8,9216]{1,0:T(8,128)}) %reduce-scatter.20.cloned.1.call-update) | async-done | bytes 294928 | tf_op jit(solution)/shard_map/reduce_scatter | solution.py:339
  2409.1 645.4 %reduce-scatter.18.cloned.1.call-done = f32[2048,8]{0,1:T(8,128)} async-done(((f32[2048,1024]{0,1:T(8,128)}), f32[2048,8]{0,1:T(8,128)}) %reduce-scatter.18.cloned.1.call-update) | async-done | bytes 65552 | tf_op jit(solution)/shard_map/reduce_scatter | solution.py:423
  3054.5 639.2 %reduce-scatter.16.cloned.1.call-done = f32[8,1024]{1,0:T(8,128)} async-done(((f32[1024,1024]{1,0:T(8,128)}), f32[8,1024]{1,0:T(8,128)}) %reduce-scatter.16.cloned.1.call-update) | async-done | bytes 32784 | tf_op jit(solution)/shard_map/reduce_scatter | solution.py:422
  3693.7 639.0 %reduce-scatter.14.cloned.1.call-done = f32[8,1024]{1,0:T(8,128)} async-done(((f32[1024,1024]{1,0:T(8,128)}), f32[8,1024]{1,0:T(8,128)}) %reduce-scatter.14.cloned.1.call-update) | async-done | bytes 32784 | tf_op jit(solution)/shard_map/reduce_scatter | solution.py:421
  4332.8 646.8 %reduce-scatter.12.cloned.1.call-done = f32[8,2048]{1,0:T(8,128)} async-done(((f32[1024,2048]{1,0:T(8,128)}), f32[8,2048]{1,0:T(8,128)}) %reduce-scatter.12.cloned.1.call-update) | async-done | bytes 65552 | tf_op jit(solution)/shard_map/reduce_scatter | solution.py:420
  (246 shorter events, 163.9 us)
Async XLA Ops:
  7.2 397.2 %copy-start.1 = (bf16[1,128,1024]{2,1,0:T(8,128)(2,1)S(1)}, bf16[1,128,1024]{2,1,0:T(8,128)(2,1)}, u32[]{:S(2)}) copy-start(bf16[1,128,1024]{2,1,0:T(8,128)(2,1)} %param.20) | copy-start | bytes 786436
  7.2 199.8 %all-gather.10.cloned.1.call-start = ((), (), s32[]{:S(2)}) async-start(), calls=%async_computation.7 | async-start | bytes 2113536 | tf_op jit(solution)/shard_map/all_gather | solution.py:298
  7.9 393.6 %all-gather.14.cloned.1.call-start = ((), (), s32[]{:S(2)}) async-start(), calls=%async_computation.9 | async-start | bytes 2113536 | tf_op jit(solution)/shard_map/all_gather | solution.py:297
  8.7 591.1 %all-gather.18.cloned.1.call-start = ((), (), s32[]{:S(2)}) async-start(), calls=%async_computation.11 | async-start | bytes 4227072 | tf_op jit(solution)/shard_map/all_gather | solution.py:296
  9.4 629.0 %all-gather.12.cloned.1.call-start = ((), (), s32[]{:S(2)}) async-start(), calls=%async_computation.8 | async-start | bytes 4456448 | tf_op jit(solution)/shard_map/all_gather | solution.py:314
  81.5 524.7 %copy-start.34 = (f32[1024]{0:T(1024)}, f32[1024]{0:T(1024)S(1)}, u32[]{:S(2)}) copy-start(f32[1024]{0:T(1024)S(1)} %convert_element_type.133) | copy-start | bytes 12292
  83.2 523.0 %copy-start.42 = (f32[128]{0:T(128)}, f32[128]{0:T(128)S(1)}, u32[]{:S(2)}) copy-start(f32[128]{0:T(128)S(1)} %get-tuple-element.649) | copy-start | bytes 1540
  209.9 475.6 %all-gather.16.cloned.1.call-start = ((), (), s32[]{:S(2)}) async-start(), calls=%async_computation.10 | async-start | bytes 4456448 | tf_op jit(solution)/shard_map/all_gather | solution.py:313
  211.6 399.2 %copy-start.27 = (f32[128,128]{0,1:T(8,128)}, f32[128,128]{0,1:T(8,128)S(1)}, u32[]{:S(2)}) copy-start(f32[128,128]{0,1:T(8,128)S(1)} %get-tuple-element.660) | copy-start | bytes 196612
  211.6 399.2 %copy-start.32 = (f32[128,128]{0,1:T(8,128)}, f32[128,128]{0,1:T(8,128)S(1)}, u32[]{:S(2)}) copy-start(f32[128,128]{0,1:T(8,128)S(1)} %get-tuple-element.641) | copy-start | bytes 196612
  407.0 477.7 %all-gather.20.cloned.1.call-start = ((), (), s32[]{:S(2)}) async-start(), calls=%async_computation.12 | async-start | bytes 4227072 | tf_op jit(solution)/shard_map/all_gather | solution.py:299
  407.6 678.7 %all-gather.24.cloned.1.call-start = ((), (), s32[]{:S(2)}) async-start(), calls=%async_computation.14 | async-start | bytes 6340608 | tf_op jit(solution)/shard_map/all_gather | solution.py:301
  408.3 879.4 %all-gather.22.cloned.1.call-start = ((), (), s32[]{:S(2)}) async-start(), calls=%async_computation.13 | async-start | bytes 6340608 | tf_op jit(solution)/shard_map/all_gather | solution.py:300
  409.1 1080.2 %all-gather.26.cloned.1.call-start = ((), (), s32[]{:S(2)}) async-start(), calls=%async_computation.15 | async-start | bytes 6340608 | tf_op jit(solution)/shard_map/all_gather | solution.py:302
  409.8 1230.4 %reduce-scatter.24.cloned.1.call-start = ((), (), s32[]{:S(2)}) async-start(), calls=%async_computation.22 | async-start | bytes 4456448
  409.9 200.9 %copy-start.49 = (f32[128]{0:T(128)}, f32[128]{0:T(128)S(1)}, u32[]{:S(2)}) copy-start(f32[128]{0:T(128)S(1)} %convert_element_type.143) | copy-start | bytes 1540
  888.5 615.0 %copy-start.9 = (f32[128,1024]{1,0:T(8,128)}, f32[128,1024]{1,0:T(8,128)S(1)}, u32[]{:S(2)}) copy-start(f32[128,1024]{1,0:T(8,128)S(1)} %get-tuple-element.657) | copy-start | bytes 1572868
  1090.0 399.3 %copy-start.29 = (bf16[1,128,1024]{2,1,0:T(8,128)(2,1)S(1)}, bf16[1,128,1024]{2,1,0:T(8,128)(2,1)}, u32[]{:S(2)}) copy-start(bf16[1,128,1024]{2,1,0:T(8,128)(2,1)} %param.33) | copy-start | bytes 786436
  1539.8 169.1 %reduce-scatter.22.cloned.1.call-start = ((), (), s32[]{:S(2)}) async-start(), calls=%async_computation.21 | async-start | bytes 4456448
  1552.9 854.5 %reduce-scatter.20.cloned.1.call-start = ((), (), s32[]{:S(2)}) async-start(), calls=%async_computation.20 | async-start | bytes 38043648 | tf_op jit(solution)/shard_map/reduce_scatter | solution.py:339
  1599.6 1454.9 %reduce-scatter.18.cloned.1.call-start = ((), (), s32[]{:S(2)}) async-start(), calls=%async_computation.19 | async-start | bytes 8454144 | tf_op jit(solution)/shard_map/reduce_scatter | solution.py:423
  1605.2 2088.5 %reduce-scatter.16.cloned.1.call-start = ((), (), s32[]{:S(2)}) async-start(), calls=%async_computation.18 | async-start | bytes 4227072 | tf_op jit(solution)/shard_map/reduce_scatter | solution.py:422
  1644.0 2688.8 %reduce-scatter.14.cloned.1.call-start = ((), (), s32[]{:S(2)}) async-start(), calls=%async_computation.17 | async-start | bytes 4227072 | tf_op jit(solution)/shard_map/reduce_scatter | solution.py:421
  1713.5 3266.0 %reduce-scatter.12.cloned.1.call-start = ((), (), s32[]{:S(2)}) async-start(), calls=%async_computation.16 | async-start | bytes 8454144 | tf_op jit(solution)/shard_map/reduce_scatter | solution.py:420
  (44 other events, 1316.2 us)
Sparse Core Ops, SparseCore 0:
  9.7 197.2 all-gather.9
  208.7 192.7 all-gather.13
  403.3 196.4 all-gather.17
  601.9 36.4 all-gather.11
  640.5 45.0 all-gather.15
  687.2 197.4 all-gather.19
  886.4 199.7 all-gather.23
  1087.9 199.7 all-gather.21
  1289.5 199.7 all-gather.25
  1540.0 100.1 reduce-scatter.23
  1642.6 66.2 reduce-scatter.21
  1711.2 696.2 reduce-scatter.19
  2410.4 644.1 reduce-scatter.17
  3057.4 636.2 reduce-scatter.15
  3696.5 636.2 reduce-scatter.13
  4335.7 643.7 reduce-scatter.11
where the time goes:
time: 5000 us; the launch traced here: 4990 us
  waiting for transfers between devices  4630 us (93%)
  blocking collectives  139 us (3%)
  matrix products  88.8 us (2%)
  local copies, waits for them, and re-layouts  56.7 us (1%)
  other arithmetic  55.7 us (1%)
    reduce_scatter x1, waiting for transfers between devices, body(): lax.psum_scatter(query_weight_grad, ('dp', 'seq'), scatter_dimension=0, t...  647 us
    reduce_scatter x1, waiting for transfers between devices, body(): lax.psum_scatter(out_weight_grad, ('dp', 'seq'), scatter_dimension=1, til...  645 us
    reduce_scatter x1, waiting for transfers between devices, body(): lax.psum_scatter(value_weight_grad, ('dp', 'seq'), scatter_dimension=0, t...  639 us
    reduce_scatter x1, waiting for transfers between devices, body(): lax.psum_scatter(key_weight_grad, ('dp', 'seq'), scatter_dimension=0, til...  639 us
    reduce_scatter x1, waiting for transfers between devices, body(): lax.psum_scatter(jnp.concatenate([contract(hidden_in, grad_gate, 0, 0), c...  602 us
    all_gather x1, waiting for transfers between devices, body(): lax.all_gather(w_gate, ('dp', 'seq'), axis=0, tiled=True)  198 us
    all_gather x1, waiting for transfers between devices, body(): lax.all_gather(w_up, ('dp', 'seq'), axis=0, tiled=True)  198 us
    all_gather x1, waiting for transfers between devices, body(): lax.all_gather(w_down, ('dp', 'seq'), axis=1, tiled=True)  197 us
  transfers between devices with their start and end apart: 16, of which 16 were waited for; matrix products, arithmetic and copies ran while one was open for 3% of the time, Pallas kernels for 0%

commit v1 on v0

v1 whole, which is shorter than its diff:
```python
import functools
import math

import jax
import jax.numpy as jnp
from jax import lax
from jax.experimental import pallas as pl
from jax.experimental.pallas import tpu as pltpu
from jax.sharding import PartitionSpec as P

HEADS = 16
KV_HEADS = 8
HEAD_DIM = 128
D = 1024
FF = 3072
BLOCK = 256
CORES = 2

WIDTHS = (1024, 512, 512, 1024, 1536, 1536, 1536)
TILE = 128

eps_norm = 1e-06
rope_base = 1000000.0
score_scale = 1.0 / math.sqrt(HEAD_DIM)
log2e = math.log2(math.e)


def place():
    dp = lax.axis_index("dp")
    seq = lax.axis_index("seq")
    return dp // 4, dp % 4, seq // 4, (seq // 2) % 2, seq % 2


def device(yh, z, x, yl, c):
    return {"dp": yh * 4 + z, "seq": x * 4 + yl * 2 + c}


def sibling():
    yh, z, x, yl, c = place()
    return device(yh, z, x, yl, 1 - c)


def neighbour(axis, step):
    yh, z, x, yl, c = place()
    if axis == "x":
        return device(yh, z, (x + step + 4) % 4, yl, c)
    if axis == "z":
        return device(yh, (z + step + 4) % 4, x, yl, c)
    y = (yh * 2 + yl + step + 4) % 4
    return device(y // 2, z, x, y % 2, c)


ORDERS = (("x", "y", "z"), ("y", "z", "x"), ("z", "x", "y"))


def chip_set(whole_axes, axis, step):
    yh, z, x, yl, _ = place()
    iz, ix, iyh, iyl = z, x, yh, yl
    if axis == "x":
        ix = (x + step + 4) % 4
    elif axis == "z":
        iz = (z + step + 4) % 4
    else:
        y = (yh * 2 + yl + step + 4) % 4
        iyh, iyl = y // 2, y % 2
    every = slice(None)
    if "x" in whole_axes:
        ix = every
    if "z" in whole_axes:
        iz = every
    if "y" in whole_axes:
        iyh, iyl = every, every
    return (iyh, iz, ix, iyl)


def set_dims(whole_axes):
    dims = ()
    if "y" in whole_axes:
        dims += (2,)
    if "z" in whole_axes:
        dims += (4,)
    if "x" in whole_axes:
        dims += (4,)
    if "y" in whole_axes:
        dims += (2,)
    return dims


FULL_PIECES = (
    (((4, 0, 10),), ((5, 0, 10),)),
    (((6, 0, 10),), ((0, 0, 8), (4, 10, 2))),
    (((3, 0, 8), (5, 10, 2)), ((1, 0, 4), (2, 0, 4), (6, 10, 2), (7, 0, 1))),
)


def flat_pieces(pieces):
    out = []
    for colour in range(3):
        for half in range(2):
            for array, first, tiles in pieces[colour][half]:
                out.append((colour, half, array, pl.ds(first * TILE, tiles * TILE), tiles * TILE))
    return out


def greet(others):
    barrier = pltpu.get_barrier_semaphore()
    for other in others:
        pl.semaphore_signal(barrier, inc=1, device_id=other)
    pl.semaphore_wait(barrier, len(others))


def torus_neighbours():
    return [neighbour(axis, step) for axis in ("x", "y", "z") for step in (1, -1)]


def gather_kernel(n_w, n_p, pieces, *refs):
    shards, pairs_in = refs[:n_w], refs[n_w : n_w + n_p]
    outs = refs[n_w + n_p : 2 * n_w + n_p]
    pairs = refs[2 * n_w + n_p : 2 * (n_w + n_p)]
    send, recv, pair_send, pair_recv, local = refs[2 * (n_w + n_p) :]
    yh, z, x, yl, c = place()
    sib = sibling()
    greet(torus_neighbours() + [sib])
    first, later = [], []
    for k in range(n_w):
        mine = outs[k].at[yh, z, x, yl, c]
        own = pltpu.make_async_copy(shards[k].at[c], mine, local.at[k])
        own.start()
        away = pltpu.make_async_remote_copy(
            shards[k].at[1 - c], mine, pair_send.at[k], pair_recv.at[k], device_id=sib
        )
        away.start()
        first += [own, away]
    for k in range(n_p):
        own = pltpu.make_async_copy(pairs_in[k], pairs[k].at[c], local.at[n_w + k])
        own.start()
        away = pltpu.make_async_remote_copy(
            pairs_in[k], pairs[k].at[c], pair_send.at[n_w + k], pair_recv.at[n_w + k], device_id=sib
        )
        away.start()
        later += [own, away]
    for copy in first:
        copy.wait()
    flat = flat_pieces(pieces)
    for phase in range(3):
        copies = {}

        def send_block(n, step, offset, which):
            colour, half, array, cols, _ = flat[n]
            axis, whole = ORDERS[colour][phase], ORDERS[colour][:phase]
            ref = outs[array].at[(*chip_set(whole, axis, offset), slice(None), slice(None), cols)]
            copy = pltpu.make_async_remote_copy(
                ref, ref, send.at[phase, n, which], recv.at[phase, n, which],
                device_id=neighbour(axis, step),
            )
            copy.start()
            copies[n, which] = copy

        for n, piece in enumerate(flat):
            send_block(n, 1 if piece[1] == 0 else -1, 0, 0)
        for n, piece in enumerate(flat):
            send_block(n, -1 if piece[1] == 0 else 1, 0, 1)
        for n, piece in enumerate(flat):
            copies[n, 0].wait_recv()
            step = 1 if piece[1] == 0 else -1
            send_block(n, step, -step, 2)
        for n in range(len(flat)):
            copies[n, 1].wait_recv()
            copies[n, 2].wait_recv()
        for n in range(len(flat)):
            for which in range(3):
                copies[n, which].wait_send()
    for copy in later:
        copy.wait()


def gather_weights(shards, pairs):
    n_w, n_p = len(shards), len(pairs)
    n_pieces = len(flat_pieces(FULL_PIECES))
    any_space = pl.BlockSpec(memory_space=pl.ANY)
    return pl.pallas_call(
        functools.partial(gather_kernel, n_w, n_p, FULL_PIECES),
        out_shape=[jax.ShapeDtypeStruct((2, 4, 4, 2, 2, 8, s.shape[-1]), s.dtype) for s in shards]
        + [jax.ShapeDtypeStruct((2, *p.shape), p.dtype) for p in pairs],
        in_specs=[any_space] * (n_w + n_p),
        out_specs=[any_space] * (n_w + n_p),
        scratch_shapes=[
            pltpu.SemaphoreType.DMA((3, n_pieces, 3)),
            pltpu.SemaphoreType.DMA((3, n_pieces, 3)),
            pltpu.SemaphoreType.DMA((n_w + n_p,)),
            pltpu.SemaphoreType.DMA((n_w + n_p,)),
            pltpu.SemaphoreType.DMA((n_w + n_p,)),
        ],
        compiler_params=pltpu.CompilerParams(collective_id=0, has_side_effects=True),
        name="gather_weights",
    )(*shards, *pairs)


def scatter_kernel(n_w, pieces, *refs):
    grads, outs = refs[:n_w], refs[n_w : 2 * n_w]
    flat = flat_pieces(pieces)
    n_pieces = len(flat)
    scratch = refs[2 * n_w :]
    held, scratch = scratch[:n_w], scratch[n_w:]
    fin, scratch = scratch[:n_w], scratch[n_w:]
    landing, scratch = scratch[: 9 * n_pieces], scratch[9 * n_pieces :]
    send, recv, pair_send, pair_recv, local = scratch
    yh, z, x, yl, c = place()
    sib = sibling()
    loads = [pltpu.make_async_copy(grads[k], held[k], local.at[k]) for k in range(n_w)]
    for load in loads:
        load.start()
    greet(torus_neighbours() + [sib])
    for load in loads:
        load.wait()
    for phase in range(3):
        copies = {}

        def spot(n, offset):
            colour, _, array, cols, _ = flat[n]
            order = ORDERS[colour]
            return held[array].at[
                (*chip_set(order[: 2 - phase], order[2 - phase], offset), slice(None), cols)
            ]

        def send_block(n, offset, step, which):
            axis = ORDERS[flat[n][0]][2 - phase]
            copy = pltpu.make_async_remote_copy(
                spot(n, offset), landing[(phase * n_pieces + n) * 3 + which],
                send.at[phase, n, which], recv.at[phase, n, which],
                device_id=neighbour(axis, step),
            )
            copy.start()
            copies[n, which] = copy

        def add_sets(n, offset, whichs):
            colour, _, _, _, width = flat[n]
            dims = set_dims(ORDERS[colour][: 2 - phase])
            target = spot(n, offset)
            terms = [landing[(phase * n_pieces + n) * 3 + w] for w in whichs]

            def one(flat_index, _):
                index, rest = [], flat_index
                for size in reversed(dims):
                    index.insert(0, rest % size)
                    rest = rest // size
                at = tuple(index)
                total = target[at].astype(jnp.float32)
                for term in terms:
                    total = total + term[at].astype(jnp.float32)
                target[at] = total.astype(jnp.bfloat16)
                return 0

            if dims:
                lax.fori_loop(0, math.prod(dims), one, 0)
            else:
                total = target[...].astype(jnp.float32)
                for term in terms:
                    total = total + term[...].astype(jnp.float32)
                target[...] = total.astype(jnp.bfloat16)

        ways = [1 if piece[1] == 0 else -1 for piece in flat]
        for n in range(n_pieces):
            send_block(n, 2, ways[n], 0)
        for n in range(n_pieces):
            send_block(n, -ways[n], -ways[n], 1)
        for n in range(n_pieces):
            copies[n, 0].wait_recv()
            add_sets(n, ways[n], (0,))
            send_block(n, ways[n], ways[n], 2)
        for n in range(n_pieces):
            copies[n, 1].wait_recv()
            copies[n, 2].wait_recv()
            add_sets(n, 0, (1, 2))
        for n in range(n_pieces):
            for which in range(3):
                copies[n, which].wait_send()
    copies = []
    for k in range(n_w):
        unit = held[k][yh, z, x, yl].astype(jnp.float32)
        fin[k][0] = unit[:8]
        fin[k][1] = unit[8:]
        away = pltpu.make_async_remote_copy(
            fin[k].at[1 - c], outs[k].at[c], pair_send.at[k], pair_recv.at[k], device_id=sib
        )
        away.start()
        outs_own = pltpu.make_async_copy(fin[k].at[c], outs[k].at[c], local.at[k])
        outs_own.start()
        copies += [away, outs_own]
    for copy in copies:
        copy.wait()


def scatter_grads(grads):
    n_w = len(grads)
    flat = flat_pieces(FULL_PIECES)
    n_pieces = len(flat)
    any_space = pl.BlockSpec(memory_space=pl.ANY)
    vmem = pl.BlockSpec(memory_space=pltpu.VMEM)
    landing = []
    for phase in range(3):
        for colour, _, _, _, width in flat:
            dims = set_dims(ORDERS[colour][: 2 - phase])
            landing += [pltpu.VMEM((*dims, 16, width), jnp.bfloat16)] * 3
    return pl.pallas_call(
        functools.partial(scatter_kernel, n_w, FULL_PIECES),
        out_shape=[jax.ShapeDtypeStruct((2, 8, g.shape[-1]), jnp.float32) for g in grads],
        in_specs=[any_space] * n_w,
        out_specs=[vmem] * n_w,
        scratch_shapes=[pltpu.VMEM(g.shape, g.dtype) for g in grads]
        + [pltpu.VMEM((2, 8, g.shape[-1]), jnp.float32) for g in grads]
        + landing
        + [
            pltpu.SemaphoreType.DMA((3, n_pieces, 3)),
            pltpu.SemaphoreType.DMA((3, n_pieces, 3)),
            pltpu.SemaphoreType.DMA((n_w,)),
            pltpu.SemaphoreType.DMA((n_w,)),
            pltpu.SemaphoreType.DMA((n_w,)),
        ],
        compiler_params=pltpu.CompilerParams(
            collective_id=1, has_side_effects=True, vmem_limit_bytes=56 << 20
        ),
        name="scatter_grads",
    )(*grads)


def exchange_kernel(n_in, n_out, items, *refs):
    ins, outs = refs[:n_in], refs[n_in : n_in + n_out]
    send, recv, local = refs[n_in + n_out :]
    yh, z, x, yl, c = place()
    me = x * 2 + yl

    def chip(number):
        return device(yh, z, number // 2, number % 2, c)

    greet([chip((me + step) % 8) for step in range(1, 8)])
    copies = []
    for step in range(1, 8):
        there = (me + step) % 8
        for n, (source, target) in enumerate(items):
            copy = pltpu.make_async_remote_copy(
                source(ins, there), target(outs, me), send.at[step, n], recv.at[step, n],
                device_id=chip(there),
            )
            copy.start()
            copies.append(copy)
    for n, (source, target) in enumerate(items):
        copy = pltpu.make_async_copy(source(ins, me), target(outs, me), local.at[n])
        copy.start()
        copies.append(copy)
    for copy in copies:
        copy.wait()


def exchange(arrays, out_shapes, items, number, name):
    any_space = pl.BlockSpec(memory_space=pl.ANY)
    return pl.pallas_call(
        functools.partial(exchange_kernel, len(arrays), len(out_shapes), items),
        out_shape=[jax.ShapeDtypeStruct(s, jnp.bfloat16) for s in out_shapes],
        in_specs=[any_space] * len(arrays),
        out_specs=[any_space] * len(out_shapes),
        scratch_shapes=[
            pltpu.SemaphoreType.DMA((8, len(items))),
            pltpu.SemaphoreType.DMA((8, len(items))),
            pltpu.SemaphoreType.DMA((len(items),)),
        ],
        compiler_params=pltpu.CompilerParams(collective_id=number, has_side_effects=True),
        name=name,
    )(*arrays)


def columns(head):
    return pl.ds(pl.multiple_of(head * HEAD_DIM, HEAD_DIM), HEAD_DIM)


def head_source(n, share=1):
    return lambda ins, there: ins[n].at[:, columns(there // share)]


def block_target(n):
    return lambda outs, me: outs[n].at[me]


def block_source(n):
    return lambda ins, there: ins[n].at[there]


def head_target(n):
    return lambda outs, me: outs[n].at[:, columns(me)]


def part_target(n):
    return lambda outs, me: outs[n].at[me % 2, :, columns(me // 2)]


def nt(left, right):
    return lax.dot_general(left, right, (((1,), (1,)), ((), ())), preferred_element_type=jnp.float32)


def attend_kernel(q_ref, k_ref, v_ref, o_ref, o32_ref, lse_ref, scores, vt):
    for j in range(8):
        vt[j] = v_ref[j].T

    def one_block(i, _):
        q = q_ref[i]

        def score(j, top):
            s = nt(k_ref[j], q) * (score_scale * log2e)
            scores[j] = s
            return jnp.maximum(top, jnp.max(s, axis=0, keepdims=True))

        top = lax.fori_loop(0, i + 1, score, jnp.full((1, BLOCK), -1e30, jnp.float32))

        def weigh(j, carry):
            total, mixed = carry
            p = jnp.exp2(scores[j] - top)
            total = total + jnp.sum(p, axis=0, keepdims=True)
            mixed = mixed + jnp.dot(vt[j], p.astype(jnp.bfloat16), preferred_element_type=jnp.float32)
            return total, mixed

        total, mixed = lax.fori_loop(
            0, i + 1, weigh,
            (jnp.zeros((1, BLOCK), jnp.float32), jnp.zeros((HEAD_DIM, BLOCK), jnp.float32)),
        )
        out = (mixed / total).T
        o32_ref[i] = out
        o_ref[i] = out.astype(jnp.bfloat16)
        lse_ref[i] = top + jnp.log2(total)
        return 0

    lax.fori_loop(0, 8, one_block, 0)


def attend(q, k, v):
    vmem = pl.BlockSpec(memory_space=pltpu.VMEM)
    return pl.pallas_call(
        attend_kernel,
        out_shape=[
            jax.ShapeDtypeStruct(q.shape, jnp.bfloat16),
            jax.ShapeDtypeStruct(q.shape, jnp.float32),
            jax.ShapeDtypeStruct((8, 1, BLOCK), jnp.float32),
        ],
        in_specs=[vmem] * 3,
        out_specs=[vmem] * 3,
        scratch_shapes=[
            pltpu.VMEM((8, BLOCK, BLOCK), jnp.float32),
            pltpu.VMEM((8, HEAD_DIM, BLOCK), jnp.bfloat16),
        ],
        compiler_params=pltpu.CompilerParams(vmem_limit_bytes=32 << 20),
        name="attend",
    )(q, k, v)


def attend_back_kernel(
    q_ref, k_ref, v_ref, do_ref, o32_ref, lse_ref, dq_ref, dk_ref, dv_ref, kt, dk_acc, dv_acc
):
    for j in range(8):
        kt[j] = k_ref[j].T
    dk_acc[...] = jnp.zeros_like(dk_acc)
    dv_acc[...] = jnp.zeros_like(dv_acc)

    def one_block(i, _):
        q, do, lse = q_ref[i], do_ref[i], lse_ref[i]
        delta = jnp.sum((do.astype(jnp.float32) * o32_ref[i]).T, axis=0, keepdims=True)

        def one_pair(j, dqt):
            p = jnp.exp2(nt(k_ref[j], q) * (score_scale * log2e) - lse)
            dp = nt(v_ref[j], do)
            ds = (p * (dp - delta)).astype(jnp.bfloat16)
            dv_acc[j] += jnp.dot(p.astype(jnp.bfloat16), do, preferred_element_type=jnp.float32)
            dk_acc[j] += jnp.dot(ds, q, preferred_element_type=jnp.float32)
            return dqt + jnp.dot(kt[j], ds, preferred_element_type=jnp.float32)

        dqt = lax.fori_loop(0, i + 1, one_pair, jnp.zeros((HEAD_DIM, BLOCK), jnp.float32))
        dq_ref[i] = (dqt * score_scale).T.astype(jnp.bfloat16)
        return 0

    lax.fori_loop(0, 8, one_block, 0)
    dk_ref[...] = (dk_acc[...] * score_scale).astype(jnp.bfloat16)
    dv_ref[...] = dv_acc[...].astype(jnp.bfloat16)


def attend_back(q, k, v, do, o32, lse):
    vmem = pl.BlockSpec(memory_space=pltpu.VMEM)
    return pl.pallas_call(
        attend_back_kernel,
        out_shape=[jax.ShapeDtypeStruct(q.shape, jnp.bfloat16)] * 3,
        in_specs=[vmem] * 6,
        out_specs=[vmem] * 3,
        scratch_shapes=[
            pltpu.VMEM((8, HEAD_DIM, BLOCK), jnp.bfloat16),
            pltpu.VMEM((8, BLOCK, HEAD_DIM), jnp.float32),
            pltpu.VMEM((8, BLOCK, HEAD_DIM), jnp.float32),
        ],
        compiler_params=pltpu.CompilerParams(vmem_limit_bytes=32 << 20),
        name="attend_back",
    )(q, k, v, do, o32, lse)


def contract(left_op, right_op, left_dim, right_dim):
    return lax.dot_general(
        left_op,
        right_op,
        (((left_dim,), (right_dim,)), ((), ())),
        preferred_element_type=jnp.float32,
    )


def rms_scale(values):
    return lax.rsqrt(jnp.mean(values * values, axis=-1, keepdims=True) + eps_norm)


def norm_back(grad_out, values, scale_factor, gain):
    weighted = grad_out * gain
    inner = jnp.mean(weighted * values, axis=-1, keepdims=True)
    grad_in = (
        scale_factor * weighted - values * (scale_factor * scale_factor * scale_factor) * inner
    )
    return (grad_in, grad_out * values * scale_factor)


def rope_tables(places):
    half_dim = HEAD_DIM // 2
    frequency = rope_base ** (-2.0 * jnp.arange(half_dim, dtype=jnp.float32) / HEAD_DIM)
    angles = places.astype(jnp.float32)[:, None] * frequency[None, :]
    cosine = jnp.cos(angles)
    sine_vals = jnp.sin(angles)
    return (
        jnp.concatenate([cosine, cosine], axis=-1),
        jnp.concatenate([sine_vals, sine_vals], axis=-1),
    )


def rotate(values, cosine, sine_vals):
    half_dim = values.shape[-1] // 2
    turned = jnp.concatenate([-values[..., half_dim:], values[..., :half_dim]], axis=-1)
    return values * cosine[:, None, :] + turned * sine_vals[:, None, :]


def rotate_back(grads, cosine, sine_vals):
    half_dim = grads.shape[-1] // 2
    moved = grads * sine_vals[:, None, :]
    return grads * cosine[:, None, :] + jnp.concatenate(
        [moved[..., half_dim:], -moved[..., :half_dim]], axis=-1
    )


def split_columns(shard):
    rows, width = shard.shape
    return jnp.transpose(shard.reshape(rows, CORES, width // CORES), (1, 0, 2))


def other_core(values):
    return lax.ppermute(values, "seq", [(s, s ^ 1) for s in range(16)])


def body(
    tokens,
    positions,
    in_gain,
    q_gain,
    k_gain,
    w_query,
    w_key,
    w_value,
    w_out,
    post_gain,
    w_gate,
    w_up,
    w_down,
    cotangent,
):
    core = lax.axis_index("seq") % 2
    rows = tokens.shape[1]
    both = 2 * rows

    gain_tile = jnp.zeros((8, TILE), jnp.bfloat16)
    gain_tile = gain_tile.at[:, 0].set(in_gain).at[:, 1].set(post_gain)
    gain_tile = gain_tile.at[0, 2].set(q_gain[0]).at[1, 2].set(k_gain[0])
    shards = [
        split_columns(w)
        for w in (w_query, w_key, w_value, w_out.T, w_gate, w_up, w_down.T)
    ] + [jnp.broadcast_to(gain_tile[None], (2, 8, TILE))]
    gathered = gather_weights(shards, [tokens[0], cotangent[0], positions])
    wq, wk, wv, wo, wg, wu, wd, gains = [w.reshape(D, w.shape[-1]) for w in gathered[:8]]
    inputs = gathered[8].reshape(both, D).astype(jnp.float32)
    grad_low = gathered[9].reshape(both, D)
    places = gathered[10].reshape(both)
    gains = gains[:, :4].astype(jnp.float32)
    gain_in = gains[:, 0]
    gain_post = gains[:, 1]
    gain_qk = gains[:, 2].reshape(HEAD_DIM, 8)
    gain_q, gain_k = gain_qk[:, 0], gain_qk[:, 1]

    def own_rows(values):
        return lax.dynamic_slice_in_dim(values, core * rows, rows, 0)

    def sum_cores_own(values):
        away = lax.dynamic_slice_in_dim(values, (1 - core) * rows, rows, 0)
        return own_rows(values) + other_core(away)

    scale_in = rms_scale(inputs)
    normed = (inputs * scale_in * gain_in).astype(jnp.bfloat16)
    query_pre = jnp.dot(normed, wq, preferred_element_type=jnp.float32).reshape(both, -1, HEAD_DIM)
    key_pre = jnp.dot(normed, wk, preferred_element_type=jnp.float32).reshape(both, -1, HEAD_DIM)
    value_low = jnp.dot(normed, wv, preferred_element_type=jnp.float32).astype(jnp.bfloat16)
    query_scale, key_scale = rms_scale(query_pre), rms_scale(key_pre)
    cosine, sine_vals = rope_tables(places)
    query_low = rotate(query_pre * query_scale * gain_q, cosine, sine_vals).astype(jnp.bfloat16)
    key_low = rotate(key_pre * key_scale * gain_k, cosine, sine_vals).astype(jnp.bfloat16)

    head_blocks = (8, BLOCK, HEAD_DIM)
    q_all, k_all, v_all = exchange(
        [query_low.reshape(both, -1), key_low.reshape(both, -1), value_low],
        [head_blocks] * 3,
        [
            (head_source(0), block_target(0)),
            (head_source(1, 2), block_target(1)),
            (head_source(2, 2), block_target(2)),
        ],
        2,
        "heads_out",
    )
    mixed_low, mixed, log_total = attend(q_all, k_all, v_all)
    (attended_low,) = exchange(
        [mixed_low], [(both, 1024)], [(block_source(0), head_target(0))], 3, "heads_back"
    )
    branch = contract(attended_low, wo, 1, 1)
    middle = inputs + (branch + other_core(branch))
    scale_post = rms_scale(middle)
    hidden_in = (middle * scale_post * gain_post).astype(jnp.bfloat16)
    gate_vals = jnp.dot(hidden_in, wg, preferred_element_type=jnp.float32)
    up_vals = jnp.dot(hidden_in, wu, preferred_element_type=jnp.float32)
    sigma = jax.nn.sigmoid(gate_vals)
    swish = gate_vals * sigma
    act_low = (swish * up_vals).astype(jnp.bfloat16)
    output = (own_rows(middle) + sum_cores_own(contract(act_low, wd, 1, 1))).astype(jnp.bfloat16)

    grad_act = jnp.dot(grad_low, wd, preferred_element_type=jnp.float32)
    slope = sigma * (1.0 + gate_vals * (1.0 - sigma))
    grad_gate = (grad_act * up_vals * slope).astype(jnp.bfloat16)
    grad_up = (grad_act * swish).astype(jnp.bfloat16)
    grad_hidden = contract(grad_gate, wg, 1, 1) + contract(grad_up, wu, 1, 1)
    grad_hidden = grad_hidden + other_core(grad_hidden)
    grad_mid_in, post_terms = norm_back(grad_hidden, middle, scale_post, gain_post)
    grad_middle = grad_low.astype(jnp.float32) + grad_mid_in
    branch_grad = grad_middle.astype(jnp.bfloat16)
    grad_att = jnp.dot(branch_grad, wo, preferred_element_type=jnp.float32).astype(jnp.bfloat16)
    (do_all,) = exchange(
        [grad_att], [head_blocks], [(head_source(0), block_target(0))], 4, "grads_out"
    )
    dq_all, dk_all, dv_all = attend_back(q_all, k_all, v_all, do_all, mixed, log_total)
    grad_query, key_parts, value_parts = exchange(
        [dq_all, dk_all, dv_all],
        [(both, 1024), (2, both, 512), (2, both, 512)],
        [
            (block_source(0), head_target(0)),
            (block_source(1), part_target(1)),
            (block_source(2), part_target(2)),
        ],
        5,
        "grads_back",
    )
    query_rot_grad = rotate_back(
        grad_query.reshape(query_pre.shape).astype(jnp.float32), cosine, sine_vals
    )
    query_pre_grad, q_terms = norm_back(query_rot_grad, query_pre, query_scale, gain_q)
    key_sum = key_parts[0].astype(jnp.float32) + key_parts[1].astype(jnp.float32)
    key_rot_grad = rotate_back(key_sum.reshape(key_pre.shape), cosine, sine_vals)
    key_pre_grad, k_terms = norm_back(key_rot_grad, key_pre, key_scale, gain_k)
    query_grad_low = query_pre_grad.reshape(both, -1).astype(jnp.bfloat16)
    key_grad_low = key_pre_grad.reshape(both, -1).astype(jnp.bfloat16)
    value_grad_low = (
        value_parts[0].astype(jnp.float32) + value_parts[1].astype(jnp.float32)
    ).astype(jnp.bfloat16)
    grad_normed = sum_cores_own(
        contract(query_grad_low, wq, 1, 1)
        + contract(key_grad_low, wk, 1, 1)
        + contract(value_grad_low, wv, 1, 1)
    )
    grad_in_part, in_terms = norm_back(
        grad_normed, own_rows(inputs), own_rows(scale_in), gain_in
    )
    input_grad = (own_rows(grad_middle) + grad_in_part).astype(jnp.bfloat16)

    qk_part = jnp.stack([jnp.sum(q_terms, axis=(0, 1)), jnp.sum(k_terms, axis=(0, 1))], axis=1)
    qk_part = jnp.pad(qk_part, ((0, 0), (0, 6))).reshape(D)
    gain_part = jnp.stack(
        [jnp.sum(in_terms, axis=0), jnp.sum(own_rows(post_terms), axis=0), qk_part], axis=1
    )
    gain_part = jnp.pad(gain_part, ((0, 0), (0, TILE - 3)))
    grads = [
        contract(normed, query_grad_low, 0, 0),
        contract(normed, key_grad_low, 0, 0),
        contract(normed, value_grad_low, 0, 0),
        contract(branch_grad, attended_low, 0, 0),
        contract(hidden_in, grad_gate, 0, 0),
        contract(hidden_in, grad_up, 0, 0),
        contract(grad_low, act_low, 0, 0),
        gain_part,
    ]
    sums = scatter_grads(
        [g.astype(jnp.bfloat16).reshape(2, 4, 4, 2, 16, g.shape[-1]) for g in grads]
    )
    wide = [jnp.concatenate([s[0], s[1]], axis=1) for s in sums[:7]]
    gain_sum = sums[7][0] + sums[7][1]
    return (
        output[None],
        input_grad[None],
        gain_sum[:, 0],
        gain_sum[0:1, 2],
        gain_sum[1:2, 2],
        wide[0],
        wide[1],
        wide[2],
        wide[3].T,
        gain_sum[:, 1],
        wide[4],
        wide[5],
        wide[6].T,
    )


def solution(mesh):
    placed = (
        P("dp", "seq", None),
        P("dp", "seq"),
        P(("dp", "seq")),
        P(("dp", "seq")),
        P(("dp", "seq")),
        P(("dp", "seq"), None),
        P(("dp", "seq"), None),
        P(("dp", "seq"), None),
        P(None, ("dp", "seq")),
        P(("dp", "seq")),
        P(("dp", "seq"), None),
        P(("dp", "seq"), None),
        P(None, ("dp", "seq")),
        P("dp", "seq", None),
    )
    return jax.shard_map(
        body,
        mesh=mesh,
        in_specs=placed,
        out_specs=(
            P("dp", "seq", None),
            P("dp", "seq", None),
            P(("dp", "seq")),
            P(("dp", "seq")),
            P(("dp", "seq")),
            P(("dp", "seq"), None),
            P(("dp", "seq"), None),
            P(("dp", "seq"), None),
            P(None, ("dp", "seq")),
            P(("dp", "seq")),
            P(("dp", "seq"), None),
            P(("dp", "seq"), None),
            P(None, ("dp", "seq")),
        ),
        check_vma=False,
    )
```

time: 5000 us -> 363 us (0.07)
  waiting for transfers between devices: 4630 us -> 0.01 us
  Pallas kernels: 0 us -> 253 us
  blocking collectives: 139 us -> 0 us
  matrix products: 88.8 us -> 34.4 us
    reduce_scatter x5 -> x0, waiting for transfers between devices: 3170 us -> none  [the longest x1 647 us: body(): lax.psum_scatter(query_weight_grad, ('dp', 'seq'), scatter_dimension=0, t...]
    all_gather x9 -> x0, waiting for transfers between devices: 1350 us -> none  [the longest x1 198 us: body(): lax.all_gather(w_gate, ('dp', 'seq'), axis=0, tiled=True)]
    pallas_call x0 -> x8, Pallas kernels: none -> 253 us  [the longest x1 85.6 us: scatter_grads(): pl.pallas_call(functools.partial(scatter_kernel, n_w, FULL_PIECES), out_s...]
    unnamed x2 -> x0, blocking collectives: 139 us -> none
    unnamed x18 -> x0, waiting for transfers between devices: 105 us -> none
  transfers between devices with their start and end apart: 16 -> 4, of which waited for: 16 -> 0; matrix products, arithmetic and copies ran while one was open for 3% -> 9% of each run, Pallas kernels for 0% -> 14%
where the time goes in v1:
time: 363 us; the launch traced here: 361 us
  Pallas kernels  253 us (70%)
  local copies, waits for them, and re-layouts  36.3 us (10%)
  matrix products  34.4 us (9%)
  other arithmetic  26.3 us (7%)
  starting transfers between devices  7.08 us (2%)
  between operations  4.06 us (1%)
    pallas_call x1, Pallas kernels, scatter_grads(): pl.pallas_call(functools.partial(scatter_kernel, n_w, FULL_PIECES), out_s...  85.6 us
    pallas_call x1, Pallas kernels, gather_weights(): pl.pallas_call(functools.partial(gather_kernel, n_w, n_p, FULL_PIECES), o...  75.4 us
    pallas_call x4, Pallas kernels, exchange(): pl.pallas_call(functools.partial(exchange_kernel, len(arrays), len(out_sh...  59.7 us
    dot_general x14, matrix products, contract(): lax.dot_general(left_op, right_op, (((left_dim,), (right_dim,)), ((), ())...  23.5 us
    pallas_call x1, Pallas kernels, attend_back(): pl.pallas_call(attend_back_kernel, out_shape=[jax.ShapeDtypeStruct(q.shap...  17.6 us
    unnamed x95, local copies, waits for them, and re-layouts  15.5 us
    pallas_call x1, Pallas kernels, attend(): pl.pallas_call(attend_kernel, out_shape=[jax.ShapeDtypeStruct(q.shape, jn...  14.8 us
  transfers between devices with their start and end apart: 4, of which 0 were waited for; matrix products, arithmetic and copies ran while one was open for 9% of the time, Pallas kernels for 14%

profile of v1, /device:TPU:1, one launch (start us, length us, event | category | flops | bytes accessed | tf_op | source)
XLA Modules:
  0.0 361.3 jit_solution(3078028203807689600)
XLA Ops:
  6.5 1.9 dynamic-slice.31
  12.5 75.4 %gather_weights.1 = (bf16[2,4,4,2,2,8,1024]{6,5,4,3,2,1,0:T(8,128)(2,1)}, bf16[2,4,4,2,2,8,512]{6,5,4,3,2,1,0:T(8,128)(2,1)}, bf16[2,4,4,2,2,8,512]{6,5,4,3,2,1,...) custom-call(bf16[2,8,1024]{2,1,0:T(8,128)(2,1)} %bitcast.225, ...), custom_call_target="tpu_custom_call" | custom-call | tf_op jit(solution)/shard_map/gather_weights/pallas_call | solution.py:181
  94.2 1.8 copy.61.refs_1_
  96.0 2.5 copy.50
  98.6 2.3 multiply_reduce_fusion.4
  104.4 18.8 %heads_out.1 = (bf16[8,256,128]{2,1,0:T(8,128)(2,1)}, bf16[8,256,128]{2,1,0:T(8,128)(2,1)}, bf16[8,256,128]{2,1,0:T(8,128)(2,1)}) custom-call(bf16[256,1024]{1,0:T(8,128)(2,1)} %copy.60.refs_0_, bf16[256,512]{1,0:T(8,128)(2,1)} %copy.61.refs_1_, bf16[256,512]{1,0:T(8,128)(2,1)} %convolution_convert_fusion.8.refs_2_), custom_call_target="tpu_custom_call" | custom-call | tf_op jit(solution)/shard_map/heads_out/pallas_call | solution.py:357
  126.4 14.8 %attend.1 = (bf16[8,256,128]{2,1,0:T(8,128)(2,1)S(1)}, f32[8,256,128]{2,1,0:T(8,128)S(1)}, f32[8,1,256]{2,1,0:T(1,128)S(1)}) custom-call(bf16[8,256,128]{2,1,0:T(8,128)(2,1)S(1)} %copy-done, bf16[8,256,128]{2,1,0:T(8,128)(2,1)S(1)} %copy-done.2, bf16[8,256,128]{2,1,0:T(8,128)(2,1)S(1)} %copy-done.4), custom_call_target="tpu_custom_call" | custom-call | tf_op jit(solution)/shard_map/attend/pallas_call | solution.py:436
  142.0 9.4 %heads_back.1 = bf16[256,1024]{1,0:T(8,128)(2,1)} custom-call(bf16[8,256,128]{2,1,0:T(8,128)(2,1)} %copy-done.10), custom_call_target="tpu_custom_call" | custom-call | tf_op jit(solution)/shard_map/heads_back/pallas_call | solution.py:357
  151.4 3.5 fusion.23
  155.0 4.1 %collective-permute-start = (f32[256,1024]{1,0:T(8,128)}, f32[256,1024]{1,0:T(8,128)}, u32[]{:S(2)}, u32[]{:S(2)}) collective-permute-start(f32[256,1024]{1,0:T(8,128)} %fusion.23), channel_id=1, source_target_pairs={{0,1},{1,0},{2,3},{3,2},{4,5},{5,4},{6,7},{7,6},{8,9},{9,8},{10,11... | collective-permute-start | bytes 3145736 | tf_op jit(solution)/shard_map/ppermute | solution.py:554
  160.2 2.9 fusion.26
  163.1 2.0 multiply_reduce_fusion.3
  173.9 2.7 convolution_convert_fusion.1
  176.6 2.6 convolution_convert_fusion.2
  179.2 2.7 convolution_convert_fusion
  185.7 9.5 %grads_out.1.do_ref = bf16[8,256,128]{2,1,0:T(8,128)(2,1)} custom-call(bf16[256,1024]{1,0:T(8,128)(2,1)} %convolution_convert_fusion.7.refs_0_), custom_call_target="tpu_custom_call" | custom-call | tf_op jit(solution)/shard_map/grads_out/pallas_call | solution.py:357
  196.3 17.6 %attend_back.1 = (bf16[8,256,128]{2,1,0:T(8,128)(2,1)S(1)}, bf16[8,256,128]{2,1,0:T(8,128)(2,1)S(1)}, bf16[8,256,128]{2,1,0:T(8,128)(2,1)S(1)}) custom-call(bf16[8,256,128]{2,1,0:T(8,128)(2,1)S(1)} %copy-done.1, bf16[8,256,128]{2,1,0:T(8,128)(2,1)S(1)} %copy-done.3, bf16[8,256,128]{2,1,0:T(8,128)(2,1)S(1)} %copy-done.5, bf16[8,256,128]{2,1,0:T(8,128)(2,1)S(1)} %copy-done.6, ...), custom_call_target="tpu_custom_call" | custom-call | tf_op jit(solution)/shard_map/attend_back/pallas_call | solution.py:485
  216.3 22.0 %grads_back.1 = (bf16[256,1024]{1,0:T(8,128)(2,1)}, bf16[2,256,512]{2,1,0:T(8,128)(2,1)}, bf16[2,256,512]{2,1,0:T(8,128)(2,1)}) custom-call(bf16[8,256,128]{2,1,0:T(8,128)(2,1)} %copy-done.7, bf16[8,256,128]{2,1,0:T(8,128)(2,1)} %copy-done.8, bf16[8,256,128]{2,1,0:T(8,128)(2,1)} %copy-done.9), custom_call_target="tpu_custom_call" | custom-call | tf_op jit(solution)/shard_map/grads_back/pallas_call | solution.py:357
  244.7 1.6 subtract_convert_fusion
  249.4 2.9 collective-permute-start.3
  253.8 2.1 convolution_convert_fusion.4
  255.9 2.0 fusion.4
  259.4 2.2 convolution_convert_fusion.3
  262.8 85.6 %scatter_grads.1 = (f32[2,8,1024]{2,1,0:T(8,128)}, f32[2,8,512]{2,1,0:T(8,128)}, f32[2,8,512]{2,1,0:T(8,128)}, f32[2,8,1024]{2,1,0:T(8,128)}, f32[2,8,1536]{2,1,...) custom-call(bf16[2,4,4,2,16,1024]{5,4,3,2,1,0:T(8,128)(2,1)} %bitcast.188, ...), custom_call_target="tpu_custom_call" | custom-call | tf_op jit(solution)/shard_map/scatter_grads/pallas_call | solution.py:305
  (198 shorter events, 64.3 us)
Async XLA Ops:
  87.9 3.9 %copy-start.23 = (bf16[2,128,1024]{2,1,0:T(8,128)(2,1)S(1)}, bf16[2,128,1024]{2,1,0:T(8,128)(2,1)}, u32[]{:S(2)}) copy-start(bf16[2,128,1024]{2,1,0:T(8,128)(2,1)} %get-tuple-element.92) | copy-start | bytes 1572868
  93.0 3.1 copy-start.21
  101.2 2.0 copy-start.31
  151.4 7.7 %copy-start.24 = (bf16[2,128,1024]{2,1,0:T(8,128)(2,1)S(1)}, bf16[2,128,1024]{2,1,0:T(8,128)(2,1)}, u32[]{:S(2)}) copy-start(bf16[2,128,1024]{2,1,0:T(8,128)(2,1)} %get-tuple-element.92) | copy-start | bytes 1572868
  151.4 8.8 %copy-start.27 = (bf16[2,128,1024]{2,1,0:T(8,128)(2,1)S(1)}, bf16[2,128,1024]{2,1,0:T(8,128)(2,1)}, u32[]{:S(2)}) copy-start(bf16[2,128,1024]{2,1,0:T(8,128)(2,1)} %get-tuple-element.106) | copy-start | bytes 1572868
  155.0 8.1 %collective-permute-start = (f32[256,1024]{1,0:T(8,128)}, f32[256,1024]{1,0:T(8,128)}, u32[]{:S(2)}, u32[]{:S(2)}) collective-permute-start(f32[256,1024]{1,0:T(8,128)} %fusion.23), channel_id=1, source_target_pairs={{0,1},{1,0},{2,3},{3,2},{4,5},{5,4},{6,7},{7,6},{8,9},{9,8},{10,11... | collective-permute-start | bytes 3145736 | tf_op jit(solution)/shard_map/ppermute | solution.py:554
  163.0 2.5 copy-start.19
  165.0 17.2 %copy-start.13 = (f32[256,1024]{1,0:T(8,128)}, f32[256,1024]{1,0:T(8,128)S(1)}, u32[]{:S(2)}) copy-start(f32[256,1024]{1,0:T(8,128)S(1)} %get-tuple-element.138) | copy-start | bytes 3145732
  171.0 10.9 %collective-permute-start.2 = (f32[256,1024]{1,0:T(8,128)S(1)}, f32[256,1024]{1,0:T(8,128)S(1)}, u32[]{:S(2)}, u32[]{:S(2)}) collective-permute-start(f32[256,1024]{1,0:T(8,128)S(1)} %convolution_add_fusion.2), channel_id=1, source_target_pairs={{0,1},{1,0},{2,3},{3,2},{4,5},{5,4},{6,7},{7,6},{8,9},{9,8},{10,11... | collective-permute-start | bytes 3145736 | tf_op jit(solution)/shard_map/ppermute | solution.py:554
  172.9 3.7 %copy-start.38 = (f32[256,1024]{1,0:T(8,128)}, f32[256,1024]{1,0:T(8,128)S(1)}, u32[]{:S(2)}) copy-start(f32[256,1024]{1,0:T(8,128)S(1)} %fusion.25) | copy-start | bytes 3145732
  173.9 82.0 %collective-permute-start.1 = (f32[128,1024]{1,0:T(8,128)}, f32[128,1024]{1,0:T(8,128)}, u32[]{:S(2)}, u32[]{:S(2)}) collective-permute-start(f32[128,1024]{1,0:T(8,128)} %constant_dynamic-slice_fusion.2), channel_id=1, source_target_pairs={{0,1},{1,0},{2,3},{3,2},{4,5},{5,4},{6,7},{7,6},{8,9},{9,8},{10,11... | collective-permute-start | bytes 1572872 | tf_op jit(solution)/shard_map/ppermute | solution.py:554
  184.2 11.0 %copy-start.1 = (bf16[8,256,128]{2,1,0:T(8,128)(2,1)S(1)}, bf16[8,256,128]{2,1,0:T(8,128)(2,1)}, u32[]{:S(2)}) copy-start(bf16[8,256,128]{2,1,0:T(8,128)(2,1)} %get-tuple-element.98.q_ref) | copy-start | bytes 1572868
  184.2 11.0 %copy-start.3 = (bf16[8,256,128]{2,1,0:T(8,128)(2,1)S(1)}, bf16[8,256,128]{2,1,0:T(8,128)(2,1)}, u32[]{:S(2)}) copy-start(bf16[8,256,128]{2,1,0:T(8,128)(2,1)} %get-tuple-element.99.k_ref) | copy-start | bytes 1572868
  184.2 11.0 %copy-start.5 = (bf16[8,256,128]{2,1,0:T(8,128)(2,1)S(1)}, bf16[8,256,128]{2,1,0:T(8,128)(2,1)}, u32[]{:S(2)}) copy-start(bf16[8,256,128]{2,1,0:T(8,128)(2,1)} %get-tuple-element.100.v_ref) | copy-start | bytes 1572868
  238.3 2.3 copy-start.42
  241.0 2.1 copy-start.12
  249.4 6.5 %copy-start.14 = (f32[256,1024]{1,0:T(8,128)S(1)}, f32[256,1024]{1,0:T(8,128)}, u32[]{:S(2)}) copy-start(f32[256,1024]{1,0:T(8,128)} %copy-done.13) | copy-start | bytes 3145732
  249.4 6.5 %copy-start.26 = (f32[256,1024]{1,0:T(8,128)S(1)}, f32[256,1024]{1,0:T(8,128)}, u32[]{:S(2)}) copy-start(f32[256,1024]{1,0:T(8,128)} %copy-done.25) | copy-start | bytes 3145732
  249.4 6.5 %copy-start.39 = (f32[256,1024]{1,0:T(8,128)S(1)}, f32[256,1024]{1,0:T(8,128)}, u32[]{:S(2)}) copy-start(f32[256,1024]{1,0:T(8,128)} %copy-done.38) | copy-start | bytes 3145732
  249.4 12.2 %collective-permute-start.3 = (f32[128,1024]{1,0:T(8,128)S(1)}, f32[128,1024]{1,0:T(8,128)S(1)}, u32[]{:S(2)}, u32[]{:S(2)}) collective-permute-start(f32[128,1024]{1,0:T(8,128)S(1)} %constant_dynamic-slice_fusion), channel_id=1, source_target_pairs={{0,1},{1,0},{2,3},{3,2},{4,5},{5,4},{6,7},{7,6},{8,9},{9,8},{10,11... | collective-permute-start | bytes 1572872 | tf_op jit(solution)/shard_map/ppermute | solution.py:554
  255.9 3.5 copy-start.18
  255.9 3.5 copy-start.28
  259.4 2.2 copy-start.33
  348.4 12.0 %copy-start.34 = (f32[256,1024]{1,0:T(8,128)S(1)}, f32[256,1024]{1,0:T(8,128)}, u32[]{:S(2)}) copy-start(f32[256,1024]{1,0:T(8,128)} %convert.30) | copy-start | bytes 3145732
  (26 other events, 31.6 us)

commit v2 on v1

v2 whole, which is shorter than its diff:
```python
import functools
import math

import jax
import jax.numpy as jnp
from jax import lax
from jax.experimental import pallas as pl
from jax.experimental.pallas import tpu as pltpu
from jax.sharding import PartitionSpec as P

HEADS = 16
KV_HEADS = 8
HEAD_DIM = 128
D = 1024
FF = 3072
BLOCK = 256
CORES = 2

TILE = 128

eps_norm = 1e-06
rope_base = 1000000.0
score_scale = 1.0 / math.sqrt(HEAD_DIM)
log2e = math.log2(math.e)


def place():
    dp = lax.axis_index("dp")
    seq = lax.axis_index("seq")
    return dp // 4, dp % 4, seq // 4, (seq // 2) % 2, seq % 2


def device(yh, z, x, yl, c):
    return {"dp": yh * 4 + z, "seq": x * 4 + yl * 2 + c}


def sibling():
    yh, z, x, yl, c = place()
    return device(yh, z, x, yl, 1 - c)


def neighbour(axis, step):
    yh, z, x, yl, c = place()
    if axis == "x":
        return device(yh, z, (x + step + 4) % 4, yl, c)
    if axis == "z":
        return device(yh, (z + step + 4) % 4, x, yl, c)
    y = (yh * 2 + yl + step + 4) % 4
    return device(y // 2, z, x, y % 2, c)


ORDERS = (("x", "y", "z"), ("y", "z", "x"), ("z", "x", "y"))


def chip_set(whole_axes, axis, step):
    yh, z, x, yl, _ = place()
    iz, ix, iyh, iyl = z, x, yh, yl
    if axis == "x":
        ix = (x + step + 4) % 4
    elif axis == "z":
        iz = (z + step + 4) % 4
    else:
        y = (yh * 2 + yl + step + 4) % 4
        iyh, iyl = y // 2, y % 2
    every = slice(None)
    if "x" in whole_axes:
        ix = every
    if "z" in whole_axes:
        iz = every
    if "y" in whole_axes:
        iyh, iyl = every, every
    return (iyh, iz, ix, iyl)


def set_dims(whole_axes):
    dims = ()
    if "y" in whole_axes:
        dims += (2,)
    if "z" in whole_axes:
        dims += (4,)
    if "x" in whole_axes:
        dims += (4,)
    if "y" in whole_axes:
        dims += (2,)
    return dims


NEAR_PIECES = (
    (((0, 0, 3),), ((0, 3, 3),)),
    (((1, 0, 3),), ((2, 0, 3),)),
    (((0, 6, 2), (1, 3, 1)), ((2, 3, 1), (3, 0, 1))),
)
FAR_PIECES = (
    (((4, 0, 8),), ((5, 0, 7),)),
    (((5, 7, 5), (6, 0, 2)), ((6, 2, 8),)),
    (((6, 10, 2), (7, 0, 5)), ((7, 5, 7),)),
)
NEAR = 4


class Piece:
    def __init__(self, colour, half, array, first, tiles):
        self.order = ORDERS[colour]
        self.way = 1 if half == 0 else -1
        self.array = array
        self.width = tiles * TILE
        self.cols = pl.ds(first * TILE, self.width)


def flat_pieces(pieces):
    return [
        Piece(colour, half, *piece)
        for colour in range(3)
        for half in range(2)
        for piece in pieces[colour][half]
    ]


def greet(others):
    barrier = pltpu.get_barrier_semaphore()
    for other in others:
        pl.semaphore_signal(barrier, inc=1, device_id=other)
    pl.semaphore_wait(barrier, len(others))


def torus_neighbours():
    return [neighbour(axis, step) for axis in ("x", "y", "z") for step in (1, -1)]


def sequence_chip(number):
    yh, z, x, yl, c = place()
    return device(yh, z, number // 2, number % 2, c)


def sequence_others():
    yh, z, x, yl, c = place()
    me = x * 2 + yl
    return [sequence_chip((me + step) % 8) for step in range(1, 8)]


ANY = pl.BlockSpec(memory_space=pl.ANY)
VMEM = pl.BlockSpec(memory_space=pltpu.VMEM)


class Gather:
    def __init__(self, outs, send, recv):
        self.outs, self.send, self.recv = outs, send, recv
        self.copies = {}

    def start(self, n, piece, phase, which):
        axis, whole = piece.order[phase], piece.order[:phase]
        step, offset = ((piece.way, 0), (-piece.way, 0), (piece.way, -piece.way))[which]
        ref = self.outs[piece.array].at[
            (*chip_set(whole, axis, offset), slice(None), slice(None), piece.cols)
        ]
        copy = pltpu.make_async_remote_copy(
            ref, ref, self.send.at[n, which], self.recv.at[n, which],
            device_id=neighbour(axis, step),
        )
        copy.start()
        self.copies[n, which] = copy

    def begin(self, active):
        for which in (0, 1):
            for n, piece, phase in active:
                self.start(n, piece, phase, which)

    def forward(self, active):
        for n, piece, phase in active:
            self.copies[n, 0].wait_recv()
            self.start(n, piece, phase, 2)

    def arrive(self, active):
        for n, _, _ in active:
            self.copies[n, 1].wait_recv()
            self.copies[n, 2].wait_recv()

    def drain(self):
        for copy in self.copies.values():
            copy.wait_send()


def gather_kernel(n_w, n_p, *refs):
    shards, pairs_in = refs[:n_w], refs[n_w : n_w + n_p]
    outs = refs[n_w + n_p : 2 * n_w + n_p]
    pairs = refs[2 * n_w + n_p : 2 * (n_w + n_p)]
    send, recv, pair_send, pair_recv, local = refs[2 * (n_w + n_p) :]
    yh, z, x, yl, c = place()
    sib = sibling()
    greet(torus_neighbours() + [sib])
    units, others = [], []
    for k in range(n_w):
        mine = outs[k].at[yh, z, x, yl, c]
        own = pltpu.make_async_copy(shards[k].at[c], mine, local.at[k])
        own.start()
        away = pltpu.make_async_remote_copy(
            shards[k].at[1 - c], mine, pair_send.at[k], pair_recv.at[k], device_id=sib
        )
        away.start()
        units.append((own, away))
    for k in range(n_p):
        own = pltpu.make_async_copy(pairs_in[k], pairs[k].at[c], local.at[n_w + k])
        own.start()
        away = pltpu.make_async_remote_copy(
            pairs_in[k], pairs[k].at[c], pair_send.at[n_w + k], pair_recv.at[n_w + k], device_id=sib
        )
        away.start()
        others.append((own, away))
    near, far = flat_pieces(NEAR_PIECES), flat_pieces(FAR_PIECES)
    gather = Gather(outs, send, recv)
    for own, away in units[:NEAR]:
        own.wait()
        away.wait_recv()
    base = 3 * len(near)
    for stage in range(3):
        active = [(stage * len(near) + n, piece, stage) for n, piece in enumerate(near)]
        if stage == 1:
            for own, away in units[NEAR:]:
                own.wait()
                away.wait_recv()
        if stage >= 1:
            active += [
                (base + (stage - 1) * len(far) + n, piece, stage - 1) for n, piece in enumerate(far)
            ]
        gather.begin(active)
        gather.forward(active)
        gather.arrive(active)
    gather.drain()
    for own, away in units:
        away.wait_send()
    for own, away in others:
        own.wait()
        away.wait()


def gather_weights(shards, pairs):
    n_w, n_p = len(shards), len(pairs)
    count = 3 * len(flat_pieces(NEAR_PIECES)) + 2 * len(flat_pieces(FAR_PIECES))
    return pl.pallas_call(
        functools.partial(gather_kernel, n_w, n_p),
        out_shape=[jax.ShapeDtypeStruct((2, 4, 4, 2, 2, 8, s.shape[-1]), s.dtype) for s in shards]
        + [jax.ShapeDtypeStruct((2, *p.shape), p.dtype) for p in pairs],
        in_specs=[ANY] * (n_w + n_p),
        out_specs=[ANY] * (n_w + n_p),
        scratch_shapes=[
            pltpu.SemaphoreType.DMA((count, 3)),
            pltpu.SemaphoreType.DMA((count, 3)),
            pltpu.SemaphoreType.DMA((n_w + n_p,)),
            pltpu.SemaphoreType.DMA((n_w + n_p,)),
            pltpu.SemaphoreType.DMA((n_w + n_p,)),
        ],
        compiler_params=pltpu.CompilerParams(collective_id=0, has_side_effects=True),
        name="gather_weights",
    )(*shards, *pairs)


def kept_index(kept, axis, step):
    iyh, iz, ix, iyl = chip_set(tuple(a for a in kept if a != axis), axis, step)
    index = ()
    if "y" in kept:
        index += (iyh,)
    if "z" in kept:
        index += (iz,)
    if "x" in kept:
        index += (ix,)
    if "y" in kept:
        index += (iyl,)
    return index


def add_sets(dims, target, terms):
    def one(flat_index, _):
        index, rest = [], flat_index
        for size in reversed(dims):
            index.insert(0, rest % size)
            rest = rest // size
        at = tuple(index)
        total = terms[0][at].astype(jnp.float32)
        for term in terms[1:]:
            total = total + term[at].astype(jnp.float32)
        target[at] = total.astype(jnp.bfloat16)
        return 0

    if dims:
        lax.fori_loop(0, math.prod(dims), one, 0)
    else:
        total = terms[0][...].astype(jnp.float32)
        for term in terms[1:]:
            total = total + term[...].astype(jnp.float32)
        target[...] = total.astype(jnp.bfloat16)


class Scatter:
    def __init__(self, landing, send, recv):
        self.landing, self.send, self.recv = landing, send, recv
        self.copies = {}

    def start(self, n, axis, step, source, which):
        copy = pltpu.make_async_remote_copy(
            source, self.landing[3 * n + which], self.send.at[n, which], self.recv.at[n, which],
            device_id=neighbour(axis, step),
        )
        copy.start()
        self.copies[n, which] = copy

    def drain(self):
        for copy in self.copies.values():
            copy.wait_send()


def scatter_dims(piece, phase):
    return set_dims(piece.order[: 2 - phase])


def landing_shapes(steps):
    return [
        pltpu.VMEM((*scatter_dims(piece, phase), 16, piece.width), jnp.bfloat16)
        for piece, phase in steps
        for _ in range(3)
    ]


def mid_shapes(steps):
    return [
        pltpu.VMEM((*scatter_dims(piece, phase), 16, piece.width), jnp.bfloat16)
        for piece, phase in steps
    ]


def grad_spot(grads, piece, offset):
    return grads[piece.array].at[
        (*chip_set(piece.order[:2], piece.order[2], offset), slice(None), piece.cols)
    ]


def scatter_kernel(n_near, n_planes, n_w, *refs):
    near, far = flat_pieces(NEAR_PIECES), flat_pieces(FAR_PIECES)
    grads, refs = refs[:n_near], refs[n_near:]
    far_planes, refs = refs[:n_planes], refs[n_planes:]
    outs, refs = refs[:n_w], refs[n_w:]
    steps = [(p, ph) for ph in range(3) for p in near] + [(p, ph) for ph in (1, 2) for p in far]
    fin, refs = refs[:n_w], refs[n_w:]
    landing, refs = refs[: 3 * len(steps)], refs[3 * len(steps) :]
    mids, refs = refs[: len(steps)], refs[len(steps) :]
    bases, refs = refs[: len(near)], refs[len(near) :]
    results, refs = refs[: len(steps)], refs[len(steps) :]
    send, recv, pair_send, pair_recv, local, load = refs
    yh, z, x, yl, c = place()
    sib = sibling()
    loads = {}
    for n, piece in enumerate(near):
        for m, (offset, target) in enumerate(((piece.way, mids[n]), (0, bases[n]))):
            loads[n, m] = pltpu.make_async_copy(grad_spot(grads, piece, offset), target, load.at[n, m])
            loads[n, m].start()
    greet(torus_neighbours() + [sib])
    scatter = Scatter(landing, send, recv)
    number = {}
    for n, (piece, phase) in enumerate(steps):
        number[id(piece), phase] = n

    def source(piece, phase, offset):
        if phase == 0:
            return grad_spot(grads, piece, offset)
        axis = piece.order[2 - phase]
        kept = piece.order[: 3 - phase]
        if phase == 1 and (id(piece), 0) not in number:
            held = far_planes[far.index(piece)]
        else:
            held = results[number[id(piece), phase - 1]]
        return held.at[(*kept_index(kept, axis, offset), slice(None), slice(None))]

    for stage in range(3):
        active = [(piece, stage) for piece in near]
        if stage < 2:
            active += [(piece, stage + 1) for piece in far]
        for which in (0, 1):
            for piece, phase in active:
                axis = piece.order[2 - phase]
                offset, step = ((2, piece.way), (-piece.way, -piece.way))[which]
                scatter.start(
                    number[id(piece), phase], axis, step, source(piece, phase, offset), which
                )
        for piece, phase in active:
            n = number[id(piece), phase]
            scatter.copies[n, 0].wait_recv()
            if phase == 0:
                loads[n, 0].wait()
                terms = [mids[n], landing[3 * n]]
            else:
                terms = [source(piece, phase, piece.way), landing[3 * n]]
            add_sets(scatter_dims(piece, phase), mids[n], terms)
            scatter.start(n, piece.order[2 - phase], piece.way, mids[n], 2)
        for piece, phase in active:
            n = number[id(piece), phase]
            scatter.copies[n, 1].wait_recv()
            scatter.copies[n, 2].wait_recv()
            if phase == 0:
                loads[n, 1].wait()
                base = bases[n]
            else:
                base = source(piece, phase, 0)
            if phase < 2:
                add_sets(
                    scatter_dims(piece, phase), results[n], [base, landing[3 * n + 1], landing[3 * n + 2]]
                )
            else:
                total = (
                    base[...].astype(jnp.float32)
                    + landing[3 * n + 1][...].astype(jnp.float32)
                    + landing[3 * n + 2][...].astype(jnp.float32)
                )
                fin[piece.array][0, :, piece.cols] = total[:8]
                fin[piece.array][1, :, piece.cols] = total[8:]
    copies = []
    for k in range(n_w):
        away = pltpu.make_async_remote_copy(
            fin[k].at[1 - c], outs[k].at[c], pair_send.at[k], pair_recv.at[k], device_id=sib
        )
        away.start()
        own = pltpu.make_async_copy(fin[k].at[c], outs[k].at[c], local.at[k])
        own.start()
        copies += [away, own]
    scatter.drain()
    for copy in copies:
        copy.wait()


def scatter_grads(grads, planes, widths):
    near, far = flat_pieces(NEAR_PIECES), flat_pieces(FAR_PIECES)
    steps = [(p, ph) for ph in range(3) for p in near] + [(p, ph) for ph in (1, 2) for p in far]
    n_w = len(widths)
    return pl.pallas_call(
        functools.partial(scatter_kernel, len(grads), len(planes), n_w),
        out_shape=[jax.ShapeDtypeStruct((2, 8, w), jnp.float32) for w in widths],
        in_specs=[ANY] * len(grads) + [VMEM] * len(planes),
        out_specs=[VMEM] * n_w,
        scratch_shapes=[pltpu.VMEM((2, 8, w), jnp.float32) for w in widths]
        + landing_shapes(steps)
        + mid_shapes(steps)
        + mid_shapes([(p, 0) for p in near])
        + mid_shapes(steps)
        + [
            pltpu.SemaphoreType.DMA((len(steps), 3)),
            pltpu.SemaphoreType.DMA((len(steps), 3)),
            pltpu.SemaphoreType.DMA((n_w,)),
            pltpu.SemaphoreType.DMA((n_w,)),
            pltpu.SemaphoreType.DMA((n_w,)),
            pltpu.SemaphoreType.DMA((len(near), 2)),
        ],
        compiler_params=pltpu.CompilerParams(
            collective_id=1, has_side_effects=True, vmem_limit_bytes=56 << 20
        ),
        name="scatter_grads",
    )(*grads, *planes)


def columns(head):
    return pl.ds(pl.multiple_of(head * HEAD_DIM, HEAD_DIM), HEAD_DIM)


def exchange_start(moves, me, send, recv, local, first):
    copies = []
    for step in range(1, 8):
        there = (me + step) % 8
        for n, (source, target) in enumerate(moves):
            copy = pltpu.make_async_remote_copy(
                source(there), target(me), send.at[first + n, step], recv.at[first + n, step],
                device_id=sequence_chip(there),
            )
            copy.start()
            copies.append(copy)
    for n, (source, target) in enumerate(moves):
        copy = pltpu.make_async_copy(source(me), target(me), local.at[first + n])
        copy.start()
        copies.append(copy)
    return copies


def nt(left, right):
    return lax.dot_general(left, right, (((1,), (1,)), ((), ())), preferred_element_type=jnp.float32)


def forward_kernel(*refs):
    q_in, k_in, v_in = refs[:3]
    weights = refs[7:11]
    q_ref, k_ref, v_ref, o32_ref, lse_ref, attended = refs[11:17]
    o_low, scores, vt, send, recv, head_send, head_recv, local = refs[17:]
    yh, z, x, yl, c = place()
    me = x * 2 + yl
    far = flat_pieces(FAR_PIECES)
    greet(torus_neighbours() + sequence_others())
    arriving = exchange_start(
        [
            (lambda j: q_in.at[:, columns(j)], lambda i: q_ref.at[i]),
            (lambda j: k_in.at[:, columns(j // 2)], lambda i: k_ref.at[i]),
            (lambda j: v_in.at[:, columns(j // 2)], lambda i: v_ref.at[i]),
        ],
        me, head_send, head_recv, local, 0,
    )
    gather = Gather([None] * NEAR + list(weights), send, recv)
    active = [(n, piece, 2) for n, piece in enumerate(far)]
    gather.begin(active)
    for copy in arriving:
        copy.wait()
    for j in range(8):
        vt[j] = v_ref[j].T

    def one_block(i, _):
        q = q_ref[i]

        def score(j, top):
            s = nt(k_ref[j], q) * (score_scale * log2e)
            scores[j] = s
            return jnp.maximum(top, jnp.max(s, axis=0, keepdims=True))

        top = lax.fori_loop(0, i + 1, score, jnp.full((1, BLOCK), -1e30, jnp.float32))

        def weigh(j, carry):
            total, mixed = carry
            p = jnp.exp2(scores[j] - top)
            total = total + jnp.sum(p, axis=0, keepdims=True)
            mixed = mixed + jnp.dot(vt[j], p.astype(jnp.bfloat16), preferred_element_type=jnp.float32)
            return total, mixed

        total, mixed = lax.fori_loop(
            0, i + 1, weigh,
            (jnp.zeros((1, BLOCK), jnp.float32), jnp.zeros((HEAD_DIM, BLOCK), jnp.float32)),
        )
        out = (mixed / total).T
        o32_ref[i] = out
        o_low[i] = out.astype(jnp.bfloat16)
        lse_ref[i] = top + jnp.log2(total)
        return 0

    lax.fori_loop(0, 6, one_block, 0)
    gather.forward(active)
    lax.fori_loop(6, 8, one_block, 0)
    leaving = exchange_start(
        [(lambda j: o_low.at[j], lambda i: attended.at[:, columns(i)])],
        me, head_send, head_recv, local, 3,
    )
    gather.arrive(active)
    gather.drain()
    for copy in leaving:
        copy.wait()


def attend(q, k, v, weights):
    blocks = (8, BLOCK, HEAD_DIM)
    n_far = len(flat_pieces(FAR_PIECES))
    return pl.pallas_call(
        forward_kernel,
        out_shape=[jax.ShapeDtypeStruct(w.shape, w.dtype) for w in weights]
        + [jax.ShapeDtypeStruct(blocks, jnp.bfloat16)] * 3
        + [
            jax.ShapeDtypeStruct(blocks, jnp.float32),
            jax.ShapeDtypeStruct((8, 1, BLOCK), jnp.float32),
            jax.ShapeDtypeStruct((BLOCK, 1024), jnp.bfloat16),
        ],
        in_specs=[ANY] * 7,
        out_specs=[ANY] * 4 + [VMEM] * 5 + [ANY],
        input_output_aliases={3: 0, 4: 1, 5: 2, 6: 3},
        scratch_shapes=[
            pltpu.VMEM(blocks, jnp.bfloat16),
            pltpu.VMEM((8, BLOCK, BLOCK), jnp.float32),
            pltpu.VMEM((8, HEAD_DIM, BLOCK), jnp.bfloat16),
            pltpu.SemaphoreType.DMA((n_far, 3)),
            pltpu.SemaphoreType.DMA((n_far, 3)),
            pltpu.SemaphoreType.DMA((4, 8)),
            pltpu.SemaphoreType.DMA((4, 8)),
            pltpu.SemaphoreType.DMA((4,)),
        ],
        compiler_params=pltpu.CompilerParams(
            collective_id=2, has_side_effects=True, vmem_limit_bytes=40 << 20
        ),
        name="attend",
    )(q, k, v, *weights)


def backward_kernel(*refs):
    far = flat_pieces(FAR_PIECES)
    n_far = len(far)
    q_ref, k_ref, v_ref, o32_ref, lse_ref, do_in = refs[:6]
    grads = [None] * NEAR + list(refs[6:10])
    dq_out, dk_out, dv_out = refs[10:13]
    planes, refs = refs[13 : 13 + n_far], refs[13 + n_far :]
    do_ref, dq_low, dk_low, dv_low, kt, dk_acc, dv_acc = refs[:7]
    refs = refs[7:]
    landing, refs = refs[: 3 * n_far], refs[3 * n_far :]
    mids, bases, refs = refs[:n_far], refs[n_far : 2 * n_far], refs[2 * n_far :]
    send, recv, load, head_send, head_recv, local = refs
    yh, z, x, yl, c = place()
    me = x * 2 + yl
    loads = {}
    for n, piece in enumerate(far):
        for m, (offset, target) in enumerate(((piece.way, mids[n]), (0, bases[n]))):
            loads[n, m] = pltpu.make_async_copy(grad_spot(grads, piece, offset), target, load.at[n, m])
            loads[n, m].start()
    greet(torus_neighbours() + sequence_others())
    arriving = exchange_start(
        [(lambda j: do_in.at[:, columns(j)], lambda i: do_ref.at[i])],
        me, head_send, head_recv, local, 0,
    )
    scatter = Scatter(landing, send, recv)
    for which in (0, 1):
        for n, piece in enumerate(far):
            offset, step = ((2, piece.way), (-piece.way, -piece.way))[which]
            scatter.start(n, piece.order[2], step, grad_spot(grads, piece, offset), which)
    for j in range(8):
        kt[j] = k_ref[j].T
    dk_acc[...] = jnp.zeros_like(dk_acc)
    dv_acc[...] = jnp.zeros_like(dv_acc)
    for copy in arriving:
        copy.wait()

    def one_block(i, _):
        q, do, lse = q_ref[i], do_ref[i], lse_ref[i]
        delta = jnp.sum((do.astype(jnp.float32) * o32_ref[i]).T, axis=0, keepdims=True)

        def one_pair(j, dqt):
            p = jnp.exp2(nt(k_ref[j], q) * (score_scale * log2e) - lse)
            dp = nt(v_ref[j], do)
            ds = (p * (dp - delta)).astype(jnp.bfloat16)
            dv_acc[j] += jnp.dot(p.astype(jnp.bfloat16), do, preferred_element_type=jnp.float32)
            dk_acc[j] += jnp.dot(ds, q, preferred_element_type=jnp.float32)
            return dqt + jnp.dot(kt[j], ds, preferred_element_type=jnp.float32)

        dqt = lax.fori_loop(0, i + 1, one_pair, jnp.zeros((HEAD_DIM, BLOCK), jnp.float32))
        dq_low[i] = (dqt * score_scale).T.astype(jnp.bfloat16)
        return 0

    lax.fori_loop(0, 6, one_block, 0)
    for n, piece in enumerate(far):
        scatter.copies[n, 0].wait_recv()
        loads[n, 0].wait()
        add_sets(scatter_dims(piece, 0), mids[n], [mids[n], landing[3 * n]])
        scatter.start(n, piece.order[2], piece.way, mids[n], 2)
    lax.fori_loop(6, 8, one_block, 0)
    dk_low[...] = (dk_acc[...] * score_scale).astype(jnp.bfloat16)
    dv_low[...] = dv_acc[...].astype(jnp.bfloat16)
    leaving = exchange_start(
        [
            (lambda j: dq_low.at[j], lambda i: dq_out.at[:, columns(i)]),
            (lambda j: dk_low.at[j], lambda i: dk_out.at[i % 2, :, columns(i // 2)]),
            (lambda j: dv_low.at[j], lambda i: dv_out.at[i % 2, :, columns(i // 2)]),
        ],
        me, head_send, head_recv, local, 1,
    )
    for n, piece in enumerate(far):
        scatter.copies[n, 1].wait_recv()
        scatter.copies[n, 2].wait_recv()
        loads[n, 1].wait()
        add_sets(scatter_dims(piece, 0), planes[n], [bases[n], landing[3 * n + 1], landing[3 * n + 2]])
    scatter.drain()
    for copy in leaving:
        copy.wait()


def attend_back(saved, grad_att, grads):
    far = flat_pieces(FAR_PIECES)
    n_far = len(far)
    steps = [(p, 0) for p in far]
    blocks = (8, BLOCK, HEAD_DIM)
    return pl.pallas_call(
        backward_kernel,
        out_shape=[
            jax.ShapeDtypeStruct((BLOCK, 1024), jnp.bfloat16),
            jax.ShapeDtypeStruct((2, BLOCK, 512), jnp.bfloat16),
            jax.ShapeDtypeStruct((2, BLOCK, 512), jnp.bfloat16),
        ]
        + [
            jax.ShapeDtypeStruct((*scatter_dims(p, 0), 16, p.width), jnp.bfloat16) for p in far
        ],
        in_specs=[VMEM] * 5 + [ANY] * 5,
        out_specs=[ANY] * 3 + [VMEM] * n_far,
        scratch_shapes=[pltpu.VMEM(blocks, jnp.bfloat16)] * 4
        + [
            pltpu.VMEM((8, HEAD_DIM, BLOCK), jnp.bfloat16),
            pltpu.VMEM(blocks, jnp.float32),
            pltpu.VMEM(blocks, jnp.float32),
        ]
        + landing_shapes(steps)
        + mid_shapes(steps)
        + mid_shapes(steps)
        + [
            pltpu.SemaphoreType.DMA((n_far, 3)),
            pltpu.SemaphoreType.DMA((n_far, 3)),
            pltpu.SemaphoreType.DMA((n_far, 2)),
            pltpu.SemaphoreType.DMA((4, 8)),
            pltpu.SemaphoreType.DMA((4, 8)),
            pltpu.SemaphoreType.DMA((4,)),
        ],
        compiler_params=pltpu.CompilerParams(
            collective_id=3, has_side_effects=True, vmem_limit_bytes=52 << 20
        ),
        name="attend_back",
    )(*saved, grad_att, *grads)


def contract(left_op, right_op, left_dim, right_dim):
    return lax.dot_general(
        left_op,
        right_op,
        (((left_dim,), (right_dim,)), ((), ())),
        preferred_element_type=jnp.float32,
    )


def rms_scale(values):
    return lax.rsqrt(jnp.mean(values * values, axis=-1, keepdims=True) + eps_norm)


def norm_back(grad_out, values, scale_factor, gain):
    weighted = grad_out * gain
    inner = jnp.mean(weighted * values, axis=-1, keepdims=True)
    grad_in = (
        scale_factor * weighted - values * (scale_factor * scale_factor * scale_factor) * inner
    )
    return (grad_in, grad_out * values * scale_factor)


def rope_tables(places):
    half_dim = HEAD_DIM // 2
    frequency = rope_base ** (-2.0 * jnp.arange(half_dim, dtype=jnp.float32) / HEAD_DIM)
    angles = places.astype(jnp.float32)[:, None] * frequency[None, :]
    cosine = jnp.cos(angles)
    sine_vals = jnp.sin(angles)
    return (
        jnp.concatenate([cosine, cosine], axis=-1),
        jnp.concatenate([sine_vals, sine_vals], axis=-1),
    )


def rotate(values, cosine, sine_vals):
    half_dim = values.shape[-1] // 2
    turned = jnp.concatenate([-values[..., half_dim:], values[..., :half_dim]], axis=-1)
    return values * cosine[:, None, :] + turned * sine_vals[:, None, :]


def rotate_back(grads, cosine, sine_vals):
    half_dim = grads.shape[-1] // 2
    moved = grads * sine_vals[:, None, :]
    return grads * cosine[:, None, :] + jnp.concatenate(
        [moved[..., half_dim:], -moved[..., :half_dim]], axis=-1
    )


def split_columns(shard):
    rows, width = shard.shape
    return jnp.transpose(shard.reshape(rows, CORES, width // CORES), (1, 0, 2))


def other_core(values):
    return lax.ppermute(values, "seq", [(s, s ^ 1) for s in range(16)])


def body(
    tokens,
    positions,
    in_gain,
    q_gain,
    k_gain,
    w_query,
    w_key,
    w_value,
    w_out,
    post_gain,
    w_gate,
    w_up,
    w_down,
    cotangent,
):
    core = lax.axis_index("seq") % 2
    rows = tokens.shape[1]
    both = 2 * rows

    gain_tile = jnp.zeros((8, TILE), jnp.bfloat16)
    gain_tile = gain_tile.at[:, 0].set(in_gain).at[:, 1].set(post_gain)
    gain_tile = gain_tile.at[0, 2].set(q_gain[0]).at[1, 2].set(k_gain[0])
    gain_shard = jnp.broadcast_to(gain_tile[None], (2, 8, TILE))
    shards = (
        [split_columns(w) for w in (w_query, w_key, w_value)]
        + [gain_shard]
        + [split_columns(w) for w in (w_out.T, w_gate, w_up, w_down.T)]
    )
    gathered = gather_weights(shards, [tokens[0], cotangent[0], positions])
    wq, wk, wv, gains = [w.reshape(D, w.shape[-1]) for w in gathered[:4]]
    inputs = gathered[8].reshape(both, D).astype(jnp.float32)
    grad_low = gathered[9].reshape(both, D)
    places = gathered[10].reshape(both)
    gains = gains[:, :4].astype(jnp.float32)
    gain_in = gains[:, 0]
    gain_post = gains[:, 1]
    gain_qk = gains[:, 2].reshape(HEAD_DIM, 8)
    gain_q, gain_k = gain_qk[:, 0], gain_qk[:, 1]

    def own_rows(values):
        return lax.dynamic_slice_in_dim(values, core * rows, rows, 0)

    def sum_cores_own(values):
        away = lax.dynamic_slice_in_dim(values, (1 - core) * rows, rows, 0)
        return own_rows(values) + other_core(away)

    scale_in = rms_scale(inputs)
    normed = (inputs * scale_in * gain_in).astype(jnp.bfloat16)
    query_pre = jnp.dot(normed, wq, preferred_element_type=jnp.float32).reshape(both, -1, HEAD_DIM)
    key_pre = jnp.dot(normed, wk, preferred_element_type=jnp.float32).reshape(both, -1, HEAD_DIM)
    value_low = jnp.dot(normed, wv, preferred_element_type=jnp.float32).astype(jnp.bfloat16)
    query_scale, key_scale = rms_scale(query_pre), rms_scale(key_pre)
    cosine, sine_vals = rope_tables(places)
    query_low = rotate(query_pre * query_scale * gain_q, cosine, sine_vals).astype(jnp.bfloat16)
    key_low = rotate(key_pre * key_scale * gain_k, cosine, sine_vals).astype(jnp.bfloat16)

    *far_weights, q_all, k_all, v_all, mixed, log_total, attended_low = attend(
        query_low.reshape(both, -1), key_low.reshape(both, -1), value_low, gathered[4:8]
    )
    saved = (q_all, k_all, v_all, mixed, log_total)
    wo, wg, wu, wd = [w.reshape(D, w.shape[-1]) for w in far_weights]
    branch = contract(attended_low, wo, 1, 1)
    middle = inputs + (branch + other_core(branch))
    scale_post = rms_scale(middle)
    hidden_in = (middle * scale_post * gain_post).astype(jnp.bfloat16)
    gate_vals = jnp.dot(hidden_in, wg, preferred_element_type=jnp.float32)
    up_vals = jnp.dot(hidden_in, wu, preferred_element_type=jnp.float32)
    sigma = jax.nn.sigmoid(gate_vals)
    swish = gate_vals * sigma
    act_low = (swish * up_vals).astype(jnp.bfloat16)
    output = (own_rows(middle) + sum_cores_own(contract(act_low, wd, 1, 1))).astype(jnp.bfloat16)

    grad_act = jnp.dot(grad_low, wd, preferred_element_type=jnp.float32)
    slope = sigma * (1.0 + gate_vals * (1.0 - sigma))
    grad_gate = (grad_act * up_vals * slope).astype(jnp.bfloat16)
    grad_up = (grad_act * swish).astype(jnp.bfloat16)
    grad_hidden = contract(grad_gate, wg, 1, 1) + contract(grad_up, wu, 1, 1)
    grad_hidden = grad_hidden + other_core(grad_hidden)
    grad_mid_in, post_terms = norm_back(grad_hidden, middle, scale_post, gain_post)
    grad_middle = grad_low.astype(jnp.float32) + grad_mid_in
    branch_grad = grad_middle.astype(jnp.bfloat16)
    grad_att = jnp.dot(branch_grad, wo, preferred_element_type=jnp.float32).astype(jnp.bfloat16)
    far_grads = [
        contract(branch_grad, attended_low, 0, 0),
        contract(hidden_in, grad_gate, 0, 0),
        contract(hidden_in, grad_up, 0, 0),
        contract(grad_low, act_low, 0, 0),
    ]

    def by_chip(grad):
        return grad.astype(jnp.bfloat16).reshape(2, 4, 4, 2, 16, grad.shape[-1])

    grad_query, key_parts, value_parts, *planes = attend_back(
        saved, grad_att, [by_chip(g) for g in far_grads]
    )
    query_rot_grad = rotate_back(
        grad_query.reshape(query_pre.shape).astype(jnp.float32), cosine, sine_vals
    )
    query_pre_grad, q_terms = norm_back(query_rot_grad, query_pre, query_scale, gain_q)
    key_sum = key_parts[0].astype(jnp.float32) + key_parts[1].astype(jnp.float32)
    key_rot_grad = rotate_back(key_sum.reshape(key_pre.shape), cosine, sine_vals)
    key_pre_grad, k_terms = norm_back(key_rot_grad, key_pre, key_scale, gain_k)
    query_grad_low = query_pre_grad.reshape(both, -1).astype(jnp.bfloat16)
    key_grad_low = key_pre_grad.reshape(both, -1).astype(jnp.bfloat16)
    value_grad_low = (
        value_parts[0].astype(jnp.float32) + value_parts[1].astype(jnp.float32)
    ).astype(jnp.bfloat16)
    grad_normed = sum_cores_own(
        contract(query_grad_low, wq, 1, 1)
        + contract(key_grad_low, wk, 1, 1)
        + contract(value_grad_low, wv, 1, 1)
    )
    grad_in_part, in_terms = norm_back(
        grad_normed, own_rows(inputs), own_rows(scale_in), gain_in
    )
    input_grad = (own_rows(grad_middle) + grad_in_part).astype(jnp.bfloat16)

    qk_part = jnp.stack([jnp.sum(q_terms, axis=(0, 1)), jnp.sum(k_terms, axis=(0, 1))], axis=1)
    qk_part = jnp.pad(qk_part, ((0, 0), (0, 6))).reshape(D)
    gain_part = jnp.stack(
        [jnp.sum(in_terms, axis=0), jnp.sum(own_rows(post_terms), axis=0), qk_part], axis=1
    )
    gain_part = jnp.pad(gain_part, ((0, 0), (0, TILE - 3)))
    near_grads = [
        contract(normed, query_grad_low, 0, 0),
        contract(normed, key_grad_low, 0, 0),
        contract(normed, value_grad_low, 0, 0),
        gain_part,
    ]
    sums = scatter_grads(
        [by_chip(g) for g in near_grads], planes, [1024, 512, 512, TILE, 1024, 1536, 1536, 1536]
    )
    wide = [jnp.concatenate([s[0], s[1]], axis=1) for s in sums[:3] + sums[4:]]
    gain_sum = sums[3][0] + sums[3][1]
    return (
        output[None],
        input_grad[None],
        gain_sum[:, 0],
        gain_sum[0:1, 2],
        gain_sum[1:2, 2],
        wide[0],
        wide[1],
        wide[2],
        wide[3].T,
        gain_sum[:, 1],
        wide[4],
        wide[5],
        wide[6].T,
    )


def solution(mesh):
    placed = (
        P("dp", "seq", None),
        P("dp", "seq"),
        P(("dp", "seq")),
        P(("dp", "seq")),
        P(("dp", "seq")),
        P(("dp", "seq"), None),
        P(("dp", "seq"), None),
        P(("dp", "seq"), None),
        P(None, ("dp", "seq")),
        P(("dp", "seq")),
        P(("dp", "seq"), None),
        P(("dp", "seq"), None),
        P(None, ("dp", "seq")),
        P("dp", "seq", None),
    )
    return jax.shard_map(
        body,
        mesh=mesh,
        in_specs=placed,
        out_specs=(
            P("dp", "seq", None),
            P("dp", "seq", None),
            P(("dp", "seq")),
            P(("dp", "seq")),
            P(("dp", "seq")),
            P(("dp", "seq"), None),
            P(("dp", "seq"), None),
            P(("dp", "seq"), None),
            P(None, ("dp", "seq")),
            P(("dp", "seq")),
            P(("dp", "seq"), None),
            P(("dp", "seq"), None),
            P(None, ("dp", "seq")),
        ),
        check_vma=False,
    )
```

time: 363 us -> 336 us (0.926)
  Pallas kernels: 253 us -> 216 us
  local copies, waits for them, and re-layouts: 36.3 us -> 45.3 us
  other arithmetic: 26.3 us -> 31.5 us
    pallas_call x8 -> x4, Pallas kernels: 253 us -> 216 us  [the longest x1 62.2 us: attend_back(): pl.pallas_call(backward_kernel, out_shape=[jax.ShapeDtypeStruct((BLOCK, 1...]
    unnamed x95 -> x143, local copies, waits for them, and re-layouts: 15.5 us -> 20.4 us
  transfers between devices with their start and end apart: 4 -> 4, of which waited for: 0 -> 0; matrix products, arithmetic and copies ran while one was open for 9% -> 12% of each run, Pallas kernels for 14% -> 19%
where the time goes in v2:
time: 336 us; the launch traced here: 335 us
  Pallas kernels  216 us (64%)
  local copies, waits for them, and re-layouts  45.3 us (13%)
  matrix products  31.9 us (9%)
  other arithmetic  31.5 us (9%)
  starting transfers between devices  6.16 us (2%)
  between operations  4.17 us (1%)
    pallas_call x1, Pallas kernels, attend_back(): pl.pallas_call(backward_kernel, out_shape=[jax.ShapeDtypeStruct((BLOCK, 1...  62.2 us
    pallas_call x1, Pallas kernels, attend(): pl.pallas_call(forward_kernel, out_shape=[jax.ShapeDtypeStruct(w.shape, w...  57 us
    pallas_call x1, Pallas kernels, scatter_grads(): pl.pallas_call(functools.partial(scatter_kernel, len(grads), len(planes),...  51.1 us
    pallas_call x1, Pallas kernels, gather_weights(): pl.pallas_call(functools.partial(gather_kernel, n_w, n_p), out_shape=[jax...  45.5 us
    dot_general x14, matrix products, contract(): lax.dot_general(left_op, right_op, (((left_dim,), (right_dim,)), ((), ())...  21.7 us
    unnamed x143, local copies, waits for them, and re-layouts  20.4 us
  transfers between devices with their start and end apart: 4, of which 0 were waited for; matrix products, arithmetic and copies ran while one was open for 12% of the time, Pallas kernels for 19%

profile of v2, /device:TPU:1, one launch (start us, length us, event | category | flops | bytes accessed | tf_op | source)
XLA Modules:
  0.0 334.8 jit_solution(6509116274343251793)
XLA Ops:
  6.5 1.9 dynamic-slice.31
  12.5 45.5 %gather_weights.1 = (bf16[2,4,4,2,2,8,1024]{6,5,4,3,2,1,0:T(8,128)(2,1)}, bf16[2,4,4,2,2,8,512]{6,5,4,3,2,1,0:T(8,128)(2,1)}, bf16[2,4,4,2,2,8,512]{6,5,4,3,2,1,...) custom-call(bf16[2,8,1024]{2,1,0:T(8,128)(2,1)} %bitcast.227, ...), custom_call_target="tpu_custom_call" | custom-call | tf_op jit(solution)/shard_map/gather_weights/pallas_call | solution.py:239
  61.0 2.9 copy.54
  72.3 1.9 convolution_convert_fusion.8.refs_2_
  74.2 1.6 copy-done.1
  75.8 1.9 copy-done.4
  77.7 57.0 %attend.1 = (bf16[2,4,4,2,2,8,1024]{6,5,4,3,2,1,0:T(8,128)(2,1)S(1)}, bf16[2,4,4,2,2,8,1536]{6,5,4,3,2,1,0:T(8,128)(2,1)S(1)}, bf16[2,4,4,2,2,8,1536]{6,5,4,3,2,...) custom-call(bf16[256,1024]{1,0:T(8,128)(2,1)S(1)} %copy-done.9, ...), custom_call_target="tpu_custom_call", output_to_operand_aliasing={{0}: (3, {}), {1}: (4, {}), {2}: (5, {}), {3}: (6, {})} | custom-call | tf_op jit(solution)/shard_map/attend/pallas_call | solution.py:551
  139.5 1.7 fusion.23
  141.2 3.9 %collective-permute-start = (f32[256,1024]{1,0:T(8,128)}, f32[256,1024]{1,0:T(8,128)}, u32[]{:S(2)}, u32[]{:S(2)}) collective-permute-start(f32[256,1024]{1,0:T(8,128)} %fusion.23), channel_id=1, source_target_pairs={{0,1},{1,0},{2,3},{3,2},{4,5},{5,4},{6,7},{7,6},{8,9},{9,8},{10,11... | collective-permute-start | bytes 3145736 | tf_op jit(solution)/shard_map/ppermute | solution.py:754
  145.1 2.1 convert.30
  147.8 3.1 fusion.26
  151.0 1.8 multiply_reduce_fusion.3
  162.1 2.6 convolution_convert_fusion.2
  164.7 2.7 convolution_convert_fusion.1
  167.4 2.7 convolution_convert_fusion
  173.9 2.1 convolution_convert_fusion.4
  176.0 62.2 %attend_back.1 = (bf16[256,1024]{1,0:T(8,128)(2,1)}, bf16[2,256,512]{2,1,0:T(8,128)(2,1)}, bf16[2,256,512]{2,1,0:T(8,128)(2,1)}, bf16[2,4,2,16,1024]{4,3,2,1,0:T...) custom-call(bf16[8,256,128]{2,1,0:T(8,128)(2,1)} %copy-done.11, ...), custom_call_target="tpu_custom_call" | custom-call | tf_op jit(solution)/shard_map/attend_back/pallas_call | solution.py:664
  242.6 2.3 copy.66
  246.7 1.7 multiply_reduce_fusion
  257.7 2.1 collective-permute-start.3
  261.7 2.1 fusion.4
  265.3 2.1 convolution_convert_fusion.3
  269.7 51.1 %scatter_grads.1 = (f32[2,8,1024]{2,1,0:T(8,128)}, f32[2,8,512]{2,1,0:T(8,128)}, f32[2,8,512]{2,1,0:T(8,128)}, f32[2,8,128]{2,1,0:T(8,128)}, f32[2,8,1024]{2,1,0...) custom-call(bf16[2,4,4,2,16,1024]{5,4,3,2,1,0:T(8,128)(2,1)} %bitcast.192, ...), custom_call_target="tpu_custom_call" | custom-call | tf_op jit(solution)/shard_map/scatter_grads/pallas_call | solution.py:432
  332.9 2.0 fusion.9
  (242 shorter events, 69.5 us)
Async XLA Ops:
  59.7 4.5 %copy-start.52 = (f32[1024,1]{0,1:T(1,128)}, f32[1024,1]{0,1:T(1,128)S(1)}, u32[]{:S(2)}) copy-start(f32[1024,1]{0,1:T(1,128)S(1)} %get-tuple-element.187) | copy-start | bytes 12292
  64.2 5.9 %copy-start.58 = (f32[128]{0:T(128)}, f32[128]{0:T(128)S(1)}, u32[]{:S(2)}) copy-start(f32[128]{0:T(128)S(1)} %get-tuple-element.147) | copy-start | bytes 1540
  64.5 4.3 %copy-start.24 = (bf16[2,128,1024]{2,1,0:T(8,128)(2,1)}, bf16[2,128,1024]{2,1,0:T(8,128)(2,1)S(1)}, u32[]{:S(2)}) copy-start(bf16[2,128,1024]{2,1,0:T(8,128)(2,1)S(1)} %multiply_convert_fusion.4) | copy-start | bytes 1572868
  70.1 4.0 %copy-start = (bf16[2,4,4,2,2,8,1536]{6,5,4,3,2,1,0:T(8,128)(2,1)S(1)}, bf16[2,4,4,2,2,8,1536]{6,5,4,3,2,1,0:T(8,128)(2,1)}, u32[]{:S(2)}) copy-start(bf16[2,4,4,2,2,8,1536]{6,5,4,3,2,1,0:T(8,128)(2,1)} %get-tuple-element.109.refs_5_) | copy-start | bytes 9437188
  138.1 7.0 %copy-start.7 = (bf16[256,1024]{1,0:T(8,128)(2,1)}, bf16[256,1024]{1,0:T(8,128)(2,1)S(1)}, u32[]{:S(2)}) copy-start(bf16[256,1024]{1,0:T(8,128)(2,1)S(1)} %get-tuple-element.111) | copy-start | bytes 1572868
  139.5 7.8 %copy-start.64 = (f32[2,128]{1,0:T(2,128)S(1)}, f32[2,128]{1,0:T(2,128)}, u32[]{:S(2)}) copy-start(f32[2,128]{1,0:T(2,128)} %copy-done.63) | copy-start | bytes 3076
  141.2 9.7 %collective-permute-start = (f32[256,1024]{1,0:T(8,128)}, f32[256,1024]{1,0:T(8,128)}, u32[]{:S(2)}, u32[]{:S(2)}) collective-permute-start(f32[256,1024]{1,0:T(8,128)} %fusion.23), channel_id=1, source_target_pairs={{0,1},{1,0},{2,3},{3,2},{4,5},{5,4},{6,7},{7,6},{8,9},{9,8},{10,11... | collective-permute-start | bytes 3145736 | tf_op jit(solution)/shard_map/ppermute | solution.py:754
  152.8 17.6 %copy-start.22 = (f32[256,1024]{1,0:T(8,128)}, f32[256,1024]{1,0:T(8,128)S(1)}, u32[]{:S(2)}) copy-start(f32[256,1024]{1,0:T(8,128)S(1)} %get-tuple-element.156) | copy-start | bytes 3145732
  158.6 11.5 %collective-permute-start.2 = (f32[256,1024]{1,0:T(8,128)S(1)}, f32[256,1024]{1,0:T(8,128)S(1)}, u32[]{:S(2)}, u32[]{:S(2)}) collective-permute-start(f32[256,1024]{1,0:T(8,128)S(1)} %convolution_add_fusion.2), channel_id=1, source_target_pairs={{0,1},{1,0},{2,3},{3,2},{4,5},{5,4},{6,7},{7,6},{8,9},{9,8},{10,11... | collective-permute-start | bytes 3145736 | tf_op jit(solution)/shard_map/ppermute | solution.py:754
  160.5 4.2 %copy-start.46 = (f32[256,1024]{1,0:T(8,128)}, f32[256,1024]{1,0:T(8,128)S(1)}, u32[]{:S(2)}) copy-start(f32[256,1024]{1,0:T(8,128)S(1)} %fusion.25) | copy-start | bytes 3145732
  162.0 99.7 %collective-permute-start.1 = (f32[128,1024]{1,0:T(8,128)}, f32[128,1024]{1,0:T(8,128)}, u32[]{:S(2)}, u32[]{:S(2)}) collective-permute-start(f32[128,1024]{1,0:T(8,128)} %constant_dynamic-slice_fusion.2), channel_id=1, source_target_pairs={{0,1},{1,0},{2,3},{3,2},{4,5},{5,4},{6,7},{7,6},{8,9},{9,8},{10,11... | collective-permute-start | bytes 1572872 | tf_op jit(solution)/shard_map/ppermute | solution.py:754
  176.0 68.8 %copy-start.45 = (f32[256,128]{0,1:T(8,128)S(1)}, f32[256,128]{0,1:T(8,128)}, u32[]{:S(2)}) copy-start(f32[256,128]{0,1:T(8,128)} %copy-done.44) | copy-start | bytes 393220
  255.4 4.4 %copy-start.69 = (bf16[128]{0:T(256)(128)(2,1)S(1)}, bf16[128]{0:T(256)(128)(2,1)}, u32[]{:S(2)}) copy-start(bf16[128]{0:T(256)(128)(2,1)} %get-tuple-element.143) | copy-start | bytes 772
  255.4 4.7 %copy-start.25 = (bf16[2,128,1024]{2,1,0:T(8,128)(2,1)S(1)}, bf16[2,128,1024]{2,1,0:T(8,128)(2,1)}, u32[]{:S(2)}) copy-start(bf16[2,128,1024]{2,1,0:T(8,128)(2,1)} %copy-done.24) | copy-start | bytes 1572868
  256.9 4.8 %copy-start.23 = (f32[256,1024]{1,0:T(8,128)S(1)}, f32[256,1024]{1,0:T(8,128)}, u32[]{:S(2)}) copy-start(f32[256,1024]{1,0:T(8,128)} %copy-done.22) | copy-start | bytes 3145732
  256.9 4.8 %copy-start.68 = (f32[128]{0:T(128)S(1)}, f32[128]{0:T(128)}, u32[]{:S(2)}) copy-start(f32[128]{0:T(128)} %dynamic-slice.32) | copy-start | bytes 1540
  257.7 9.7 %collective-permute-start.3 = (f32[128,1024]{1,0:T(8,128)}, f32[128,1024]{1,0:T(8,128)}, u32[]{:S(2)}, u32[]{:S(2)}) collective-permute-start(f32[128,1024]{1,0:T(8,128)} %constant_dynamic-slice_fusion), channel_id=1, source_target_pairs={{0,1},{1,0},{2,3},{3,2},{4,5},{5,4},{6,7},{7,6},{8,9},{9,8},{10,11... | collective-permute-start | bytes 1572872 | tf_op jit(solution)/shard_map/ppermute | solution.py:754
  260.2 3.7 %copy-start.49 = (bf16[2,256,512]{2,1,0:T(8,128)(2,1)S(1)}, bf16[2,256,512]{2,1,0:T(8,128)(2,1)}, u32[]{:S(2)}) copy-start(bf16[2,256,512]{2,1,0:T(8,128)(2,1)} %get-tuple-element.124) | copy-start | bytes 1572868
  263.8 3.6 %copy-start.36 = (f32[256,1024]{1,0:T(8,128)S(1)}, f32[256,1024]{1,0:T(8,128)}, u32[]{:S(2)}) copy-start(f32[256,1024]{1,0:T(8,128)} %copy-done.35) | copy-start | bytes 3145732
  263.8 3.6 %copy-start.40 = (f32[256,1024]{1,0:T(8,128)S(1)}, f32[256,1024]{1,0:T(8,128)}, u32[]{:S(2)}) copy-start(f32[256,1024]{1,0:T(8,128)} %convert.30) | copy-start | bytes 3145732
  263.9 3.6 %copy-start.53 = (f32[1024,1]{0,1:T(1,128)S(1)}, f32[1024,1]{0,1:T(1,128)}, u32[]{:S(2)}) copy-start(f32[1024,1]{0,1:T(1,128)} %copy-done.52) | copy-start | bytes 12292
  263.9 3.6 %copy-start.65 = (f32[128]{0:T(128)S(1)}, f32[128]{0:T(128)}, u32[]{:S(2)}) copy-start(f32[128]{0:T(128)} %get-tuple-element.195) | copy-start | bytes 1540
  269.7 63.2 %copy-start.66 = (f32[128]{0:T(128)S(1)}, f32[128]{0:T(128)}, u32[]{:S(2)}) copy-start(f32[128]{0:T(128)} %get-tuple-element.194) | copy-start | bytes 1540
  320.8 12.0 %copy-start.41 = (f32[256,1024]{1,0:T(8,128)S(1)}, f32[256,1024]{1,0:T(8,128)}, u32[]{:S(2)}) copy-start(f32[256,1024]{1,0:T(8,128)} %convert.30) | copy-start | bytes 3145732
  (50 other events, 82.0 us)

commit v3 on v2

v3 whole, which is shorter than its diff:
```python
import functools
import math

import jax
import jax.numpy as jnp
from jax import lax
from jax.experimental import pallas as pl
from jax.experimental.pallas import tpu as pltpu
from jax.sharding import PartitionSpec as P

HEADS = 16
KV_HEADS = 8
HEAD_DIM = 128
D = 1024
FF = 3072
BLOCK = 256
CORES = 2

TILE = 128

eps_norm = 1e-06
rope_base = 1000000.0
score_scale = 1.0 / math.sqrt(HEAD_DIM)
log2e = math.log2(math.e)


def place():
    dp = lax.axis_index("dp")
    seq = lax.axis_index("seq")
    return dp // 4, dp % 4, seq // 4, (seq // 2) % 2, seq % 2


def device(yh, z, x, yl, c):
    return {"dp": yh * 4 + z, "seq": x * 4 + yl * 2 + c}


def sibling():
    yh, z, x, yl, c = place()
    return device(yh, z, x, yl, 1 - c)


def neighbour(axis, step):
    yh, z, x, yl, c = place()
    if axis == "x":
        return device(yh, z, (x + step + 4) % 4, yl, c)
    if axis == "z":
        return device(yh, (z + step + 4) % 4, x, yl, c)
    y = (yh * 2 + yl + step + 4) % 4
    return device(y // 2, z, x, y % 2, c)


ORDERS = (("x", "y", "z"), ("y", "z", "x"), ("z", "x", "y"))


def chip_set(whole_axes, axis, step):
    yh, z, x, yl, _ = place()
    iz, ix, iyh, iyl = z, x, yh, yl
    if axis == "x":
        ix = (x + step + 4) % 4
    elif axis == "z":
        iz = (z + step + 4) % 4
    else:
        y = (yh * 2 + yl + step + 4) % 4
        iyh, iyl = y // 2, y % 2
    every = slice(None)
    if "x" in whole_axes:
        ix = every
    if "z" in whole_axes:
        iz = every
    if "y" in whole_axes:
        iyh, iyl = every, every
    return (iyh, iz, ix, iyl)


def set_dims(whole_axes):
    dims = ()
    if "y" in whole_axes:
        dims += (2,)
    if "z" in whole_axes:
        dims += (4,)
    if "x" in whole_axes:
        dims += (4,)
    if "y" in whole_axes:
        dims += (2,)
    return dims


NEAR_PIECES = (
    (((0, 0, 3),), ((0, 3, 3),)),
    (((1, 0, 3),), ((2, 0, 3),)),
    (((0, 6, 2), (1, 3, 1)), ((2, 3, 1), (3, 0, 1))),
)
FAR_PIECES = (
    (((4, 0, 8),), ((5, 0, 7),)),
    (((5, 7, 5), (6, 0, 2)), ((6, 2, 8),)),
    (((6, 10, 2), (7, 0, 5)), ((7, 5, 7),)),
)
NEAR = 4
LIMIT = 60 << 20


class Piece:
    def __init__(self, colour, half, array, first, tiles):
        self.name = (array, first)
        self.order = ORDERS[colour]
        self.way = 1 if half == 0 else -1
        self.array = array
        self.width = tiles * TILE
        self.cols = pl.ds(first * TILE, self.width)


def flat_pieces(pieces):
    return [
        Piece(colour, half, *piece)
        for colour in range(3)
        for half in range(2)
        for piece in pieces[colour][half]
    ]


def greet(others):
    barrier = pltpu.get_barrier_semaphore()
    for other in others:
        pl.semaphore_signal(barrier, inc=1, device_id=other)
    pl.semaphore_wait(barrier, len(others))


def torus_neighbours():
    return [neighbour(axis, step) for axis in ("x", "y", "z") for step in (1, -1)]


def sequence_chip(number):
    yh, z, x, yl, c = place()
    return device(yh, z, number // 2, number % 2, c)


def sequence_others():
    yh, z, x, yl, c = place()
    me = x * 2 + yl
    return [sequence_chip((me + step) % 8) for step in range(1, 8)]


HBM = pl.BlockSpec(memory_space=pltpu.HBM)
VMEM = pl.BlockSpec(memory_space=pltpu.VMEM)


def load_all(pairs, sems):
    copies = [pltpu.make_async_copy(a, b, sems.at[n]) for n, (a, b) in enumerate(pairs)]
    for copy in copies:
        copy.start()
    return copies


def nt(left, right):
    return lax.dot_general(left, right, (((1,), (1,)), ((), ())), preferred_element_type=jnp.float32)


def rms_scale(values):
    return lax.rsqrt(jnp.mean(values * values, axis=-1, keepdims=True) + eps_norm)


def norm_back(grad_out, values, scale_factor, gain):
    weighted = grad_out * gain
    inner = jnp.mean(weighted * values, axis=-1, keepdims=True)
    grad_in = (
        scale_factor * weighted - values * (scale_factor * scale_factor * scale_factor) * inner
    )
    return (grad_in, grad_out * values * scale_factor)


def rope_pair(tab):
    table = tab[...].reshape(BLOCK, HEAD_DIM)
    turned = pltpu.roll(table, HEAD_DIM // 2, 1)
    low = lax.broadcasted_iota(jnp.int32, (BLOCK, HEAD_DIM), 1) < HEAD_DIM // 2
    return jnp.where(low, table, turned), jnp.where(low, -turned, table)


class Gather:
    def __init__(self, outs, send, recv):
        self.outs, self.send, self.recv = outs, send, recv
        self.copies = {}

    def start(self, n, piece, phase, which):
        axis, whole = piece.order[phase], piece.order[:phase]
        step, offset = ((piece.way, 0), (-piece.way, 0), (piece.way, -piece.way))[which]
        ref = self.outs[piece.array].at[
            (*chip_set(whole, axis, offset), slice(None), slice(None), piece.cols)
        ]
        copy = pltpu.make_async_remote_copy(
            ref, ref, self.send.at[n, which], self.recv.at[n, which],
            device_id=neighbour(axis, step),
        )
        copy.start()
        self.copies[n, which] = copy

    def begin(self, active):
        for which in (0, 1):
            for n, piece, phase in active:
                self.start(n, piece, phase, which)

    def forward(self, active):
        for n, piece, phase in active:
            self.copies[n, 0].wait_recv()
            self.start(n, piece, phase, 2)

    def arrive(self, active):
        for n, _, _ in active:
            self.copies[n, 1].wait_recv()
            self.copies[n, 2].wait_recv()

    def drain(self):
        for copy in self.copies.values():
            copy.wait_send()


def gather_kernel(n_w, n_p, *refs):
    gain_rows, shards, pairs_in = refs[0], list(refs[1:n_w]), refs[n_w : n_w + n_p]
    outs = refs[n_w + n_p : 2 * n_w + n_p]
    pairs = refs[2 * n_w + n_p : 2 * (n_w + n_p)]
    gain_tile, send, recv, pair_send, pair_recv, local = refs[2 * (n_w + n_p) :]
    yh, z, x, yl, c = place()
    sib = sibling()
    rows = jnp.concatenate([gain_rows[...].astype(jnp.float32), jnp.zeros((TILE - 8, TILE), jnp.float32)])
    tile = rows.T[:8].astype(jnp.bfloat16)
    gain_tile[0] = tile
    gain_tile[1] = tile
    shards.insert(NEAR - 1, gain_tile)
    greet(torus_neighbours() + [sib])
    units, others = [], []
    for k in range(n_w):
        mine = outs[k].at[yh, z, x, yl, c]
        own = pltpu.make_async_copy(shards[k].at[c], mine, local.at[k])
        own.start()
        away = pltpu.make_async_remote_copy(
            shards[k].at[1 - c], mine, pair_send.at[k], pair_recv.at[k], device_id=sib
        )
        away.start()
        units.append((own, away))
    for k in range(n_p):
        own = pltpu.make_async_copy(pairs_in[k], pairs[k].at[c], local.at[n_w + k])
        own.start()
        away = pltpu.make_async_remote_copy(
            pairs_in[k], pairs[k].at[c], pair_send.at[n_w + k], pair_recv.at[n_w + k], device_id=sib
        )
        away.start()
        others.append((own, away))
    near, far = flat_pieces(NEAR_PIECES), flat_pieces(FAR_PIECES)
    gather = Gather(outs, send, recv)
    for own, away in units[:NEAR]:
        own.wait()
        away.wait_recv()
    base = 3 * len(near)
    for stage in range(3):
        active = [(stage * len(near) + n, piece, stage) for n, piece in enumerate(near)]
        if stage == 1:
            for own, away in units[NEAR:]:
                own.wait()
                away.wait_recv()
        if stage >= 1:
            active += [
                (base + (stage - 1) * len(far) + n, piece, stage - 1) for n, piece in enumerate(far)
            ]
        gather.begin(active)
        gather.forward(active)
        gather.arrive(active)
    gather.drain()
    for own, away in units:
        away.wait_send()
    for own, away in others:
        own.wait()
        away.wait()


def gather_weights(gain_rows, shards, pairs):
    n_w, n_p = len(shards) + 1, len(pairs)
    count = 3 * len(flat_pieces(NEAR_PIECES)) + 2 * len(flat_pieces(FAR_PIECES))
    widths = [w.shape[-1] for w in shards]
    widths.insert(NEAR - 1, TILE)
    return pl.pallas_call(
        functools.partial(gather_kernel, n_w, n_p),
        out_shape=[jax.ShapeDtypeStruct((2, 4, 4, 2, 2, 8, w), jnp.bfloat16) for w in widths]
        + [jax.ShapeDtypeStruct((2, *p.shape), p.dtype) for p in pairs],
        in_specs=[VMEM] * (n_w + n_p),
        out_specs=[HBM] * (n_w + n_p),
        scratch_shapes=[
            pltpu.VMEM((2, 8, TILE), jnp.bfloat16),
            pltpu.SemaphoreType.DMA((count, 3)),
            pltpu.SemaphoreType.DMA((count, 3)),
            pltpu.SemaphoreType.DMA((n_w + n_p,)),
            pltpu.SemaphoreType.DMA((n_w + n_p,)),
            pltpu.SemaphoreType.DMA((n_w + n_p,)),
        ],
        compiler_params=pltpu.CompilerParams(
            collective_id=0, has_side_effects=True, vmem_limit_bytes=LIMIT
        ),
        name="gather_weights",
    )(gain_rows, *shards, *pairs)


def kept_index(kept, axis, step):
    iyh, iz, ix, iyl = chip_set(tuple(a for a in kept if a != axis), axis, step)
    index = ()
    if "y" in kept:
        index += (iyh,)
    if "z" in kept:
        index += (iz,)
    if "x" in kept:
        index += (ix,)
    if "y" in kept:
        index += (iyl,)
    return index


def add_sets(dims, target, terms):
    def one(flat_index, _):
        index, rest = [], flat_index
        for size in reversed(dims):
            index.insert(0, rest % size)
            rest = rest // size
        at = tuple(index)
        total = terms[0][at].astype(jnp.float32)
        for term in terms[1:]:
            total = total + term[at].astype(jnp.float32)
        target[at] = total.astype(jnp.bfloat16)
        return 0

    if dims:
        lax.fori_loop(0, math.prod(dims), one, 0)
    else:
        total = terms[0][...].astype(jnp.float32)
        for term in terms[1:]:
            total = total + term[...].astype(jnp.float32)
        target[...] = total.astype(jnp.bfloat16)


class Scatter:
    def __init__(self, landing, send, recv):
        self.landing, self.send, self.recv = landing, send, recv
        self.copies = {}

    def start(self, n, axis, step, source, which):
        copy = pltpu.make_async_remote_copy(
            source, self.landing[3 * n + which], self.send.at[n, which], self.recv.at[n, which],
            device_id=neighbour(axis, step),
        )
        copy.start()
        self.copies[n, which] = copy

    def drain(self):
        for copy in self.copies.values():
            copy.wait_send()


def scatter_dims(piece, phase):
    return set_dims(piece.order[: 2 - phase])


def landing_shapes(steps):
    return [
        pltpu.VMEM((*scatter_dims(piece, phase), 16, piece.width), jnp.bfloat16)
        for piece, phase in steps
        for _ in range(3)
    ]


def mid_shapes(steps):
    return [
        pltpu.VMEM((*scatter_dims(piece, phase), 16, piece.width), jnp.bfloat16)
        for piece, phase in steps
    ]


def grad_spot(grads, piece, offset):
    return grads[piece.array].at[
        (*chip_set(piece.order[:2], piece.order[2], offset), slice(None), piece.cols)
    ]


def last_kernel(*refs):
    near, far = flat_pieces(NEAR_PIECES), flat_pieces(FAR_PIECES)
    n_near, n_far, n_w = len(near), len(far), len(LAST_WIDTHS)
    steps = last_steps()
    n_steps = len(steps)
    gq_in, kparts_in, vparts_in, qpre_in, kpre_in, normed_in, tab_in, rows_in, x_in = refs[:9]
    wq_in, wk_in, wv_in, gmid_in, post_in = refs[9:14]
    planes_in, refs = refs[14 : 14 + n_far], refs[14 + n_far :]
    outs, refs = refs[:n_w], refs[n_w:]
    in_gain_out, post_gain_out, q_gain_out, k_gain_out, input_grad = refs[:5]
    refs = refs[5:]
    gq, kparts, vparts, qpre, kpre, normed, tab, rows, x_ref = refs[:9]
    wq, wk, wv, gmid, post = refs[9:14]
    planes, refs = refs[14 : 14 + n_far], refs[14 + n_far :]
    dq, dk, dv, normed_t, pair_out, pair_in, gain_got = refs[:7]
    refs = refs[7:]
    grads, refs = refs[:NEAR], refs[NEAR:]
    fin, refs = refs[: n_w + 1], refs[n_w + 1 :]
    landing, refs = refs[: 3 * n_steps], refs[3 * n_steps :]
    mids, refs = refs[:n_steps], refs[n_steps:]
    results, refs = refs[:n_steps], refs[n_steps:]
    send, recv, pair_send, pair_recv, local, load = refs
    yh, z, x, yl, c = place()
    sib = sibling()
    loads = load_all(
        [
            (gq_in, gq), (kparts_in, kparts), (vparts_in, vparts), (qpre_in, qpre), (kpre_in, kpre),
            (normed_in, normed), (tab_in, tab), (rows_in, rows), (x_in, x_ref), (wq_in, wq),
            (wk_in, wk), (wv_in, wv), (gmid_in, gmid), (post_in, post),
        ]
        + list(zip(planes_in, planes)),
        load,
    )
    greet(torus_neighbours() + [sib])
    for n in range(9):
        loads[n].wait()
    cosine, sine = rope_pair(tab)
    gain_q, gain_k = rows[2:3, :HEAD_DIM], rows[3:4, :HEAD_DIM]

    def head_back(grad, values, gain):
        grad = grad * cosine - pltpu.roll(grad, HEAD_DIM // 2, 1) * sine
        grad_in, terms = norm_back(grad, values, rms_scale(values), gain)
        return grad_in.astype(jnp.bfloat16), jnp.sum(terms, axis=0, keepdims=True)

    q_part = jnp.zeros((1, HEAD_DIM), jnp.float32)
    k_part = jnp.zeros((1, HEAD_DIM), jnp.float32)
    for h in range(8):
        at = slice(h * HEAD_DIM, (h + 1) * HEAD_DIM)
        dq[:, at], part = head_back(gq[:, at].astype(jnp.float32), qpre[:, at], gain_q)
        q_part = q_part + part
    for h in range(4):
        at = slice(h * HEAD_DIM, (h + 1) * HEAD_DIM)
        grad = kparts[0, :, at].astype(jnp.float32) + kparts[1, :, at].astype(jnp.float32)
        dk[:, at], part = head_back(grad, kpre[:, at], gain_k)
        k_part = k_part + part
    dv[...] = (vparts[0].astype(jnp.float32) + vparts[1].astype(jnp.float32)).astype(jnp.bfloat16)
    normed_t[...] = normed[...].T

    def weight_grads(n, _):
        lhs = normed_t[pl.ds(pl.multiple_of(n * 256, 256), 256), :]
        for grad, factor in ((grads[0], dq), (grads[1], dk), (grads[2], dv)):
            width = factor.shape[1]
            block = jnp.dot(lhs, factor[...], preferred_element_type=jnp.float32)
            grad[n // 2, pl.ds(n % 2 * 2, 2)] = block.astype(jnp.bfloat16).reshape(2, 4, 2, 16, width)
        return 0

    lax.fori_loop(0, 4, weight_grads, 0)
    scatter = Scatter(landing, send, recv)
    number = {(piece.name, phase): n for n, (piece, phase) in enumerate(steps)}

    def source(piece, phase, offset):
        if phase == 0:
            return grad_spot(grads, piece, offset)
        axis, kept = piece.order[2 - phase], piece.order[: 3 - phase]
        if phase == 1 and (piece.name, 0) not in number:
            held = planes[[p.name for p in far].index(piece.name)]
        else:
            held = results[number[piece.name, phase - 1]]
        return held.at[(*kept_index(kept, axis, offset), slice(None), slice(None))]

    def begin(active):
        for which in (0, 1):
            for piece, phase in active:
                axis = piece.order[2 - phase]
                offset, step = ((2, piece.way), (-piece.way, -piece.way))[which]
                scatter.start(number[piece.name, phase], axis, step, source(piece, phase, offset), which)

    def middle(active):
        for piece, phase in active:
            n = number[piece.name, phase]
            scatter.copies[n, 0].wait_recv()
            add_sets(
                scatter_dims(piece, phase), mids[n], [source(piece, phase, piece.way), landing[3 * n]]
            )
            scatter.start(n, piece.order[2 - phase], piece.way, mids[n], 2)

    def end(active):
        for piece, phase in active:
            n = number[piece.name, phase]
            scatter.copies[n, 1].wait_recv()
            scatter.copies[n, 2].wait_recv()
            base, dims = source(piece, phase, 0), scatter_dims(piece, phase)
            if phase < 2:
                add_sets(dims, results[n], [base, landing[3 * n + 1], landing[3 * n + 2]])
            else:
                total = (
                    base[...].astype(jnp.float32)
                    + landing[3 * n + 1][...].astype(jnp.float32)
                    + landing[3 * n + 2][...].astype(jnp.float32)
                )
                fin[piece.array][0, :, piece.cols] = total[:8]
                fin[piece.array][1, :, piece.cols] = total[8:]

    weights_first = [(piece, 0) for piece in near if piece.array != NEAR - 1]
    gains_first = [(piece, 0) for piece in near if piece.array == NEAR - 1]
    begin(weights_first)
    for n in range(9, 14 + n_far):
        loads[n].wait()
    begin([(piece, 1) for piece in far])

    def grad_normed(rows_at):
        return (
            nt(dq[rows_at, :], wq[...]) + nt(dk[rows_at, :], wk[...]) + nt(dv[rows_at, :], wv[...])
        )

    away = pl.ds(pl.multiple_of((1 - c) * 128, 128), 128)
    own = pl.ds(pl.multiple_of(c * 128, 128), 128)
    pair_out[...] = grad_normed(away).astype(jnp.bfloat16)
    swap = pltpu.make_async_remote_copy(
        pair_out, pair_in, pair_send.at[n_w + 1], pair_recv.at[n_w + 1], device_id=sib
    )
    swap.start()
    grad = grad_normed(own)
    values = x_ref[c].astype(jnp.float32)
    swap.wait_recv()
    grad = grad + pair_in[...].astype(jnp.float32)
    grad_in, terms = norm_back(grad, values, rms_scale(values), rows[0:1, :])
    input_grad[...] = (gmid[...] + grad_in).astype(jnp.bfloat16)
    in_part = jnp.sum(terms, axis=0, keepdims=True)
    spread = (
        lax.broadcasted_iota(jnp.int32, (HEAD_DIM, D), 1)
        == 8 * lax.broadcasted_iota(jnp.int32, (HEAD_DIM, D), 0)
    ).astype(jnp.bfloat16)
    qk = jnp.concatenate([q_part, k_part, jnp.zeros((6, HEAD_DIM), jnp.float32)]).astype(jnp.bfloat16)
    qk = jnp.dot(qk, spread, preferred_element_type=jnp.float32)
    gain_rows = jnp.concatenate(
        [in_part, post[0:1, :], qk[0:2], jnp.zeros((TILE - 4, D), jnp.float32)]
    )
    grads[NEAR - 1][...] = gain_rows.T.astype(jnp.bfloat16).reshape(2, 4, 4, 2, 16, TILE)
    begin(gains_first)
    stages = [
        [(piece, stage) for piece in near] + ([(piece, stage + 1) for piece in far] if stage < 2 else [])
        for stage in range(3)
    ]
    for stage, active in enumerate(stages):
        if stage > 0:
            begin(active)
        middle(active)
        end(active)
    copies = []
    for k in range(n_w + 1):
        if k == NEAR - 1:
            target = gain_got
        else:
            out = outs[k if k < NEAR else k - 1]
            width = out.shape[1] // 2
            target = out.at[:, pl.ds(pl.multiple_of(c * width, TILE), width)]
        swap_k = pltpu.make_async_remote_copy(
            fin[k].at[1 - c], target, pair_send.at[k], pair_recv.at[k], device_id=sib
        )
        swap_k.start()
        copies.append(swap_k)
        if k != NEAR - 1:
            keep = pltpu.make_async_copy(fin[k].at[c], target, local.at[k])
            keep.start()
            copies.append(keep)
    scatter.drain()
    swap.wait_send()
    for copy in copies:
        copy.wait()
    gain_sum = fin[NEAR - 1][c] + gain_got[...]
    gain_rows = jnp.concatenate([gain_sum, jnp.zeros((TILE - 8, TILE), jnp.float32)]).T
    in_gain_out[...] = gain_rows[0:1, :8]
    post_gain_out[...] = gain_rows[1:2, :8]
    q_gain_out[...] = gain_rows[2:3, :1]
    k_gain_out[...] = gain_rows[3:4, :1]


LAST_WIDTHS = (1024, 512, 512, 1024, 1536, 1536, 1536)


def last_steps():
    near, far = flat_pieces(NEAR_PIECES), flat_pieces(FAR_PIECES)
    return [(p, ph) for ph in range(3) for p in near] + [(p, ph) for ph in (1, 2) for p in far]


def finish(arrays, planes):
    steps = last_steps()
    n_w = len(LAST_WIDTHS)
    fin_widths = list(LAST_WIDTHS)
    fin_widths.insert(NEAR - 1, TILE)
    loaded = [*arrays, *planes]
    return pl.pallas_call(
        last_kernel,
        out_shape=[jax.ShapeDtypeStruct((8, 2 * w), jnp.float32) for w in LAST_WIDTHS]
        + [jax.ShapeDtypeStruct((1, n), jnp.float32) for n in (8, 8, 1, 1)]
        + [jax.ShapeDtypeStruct((128, D), jnp.bfloat16)],
        in_specs=[HBM] * len(loaded),
        out_specs=[HBM] * n_w + [VMEM] * 5,
        scratch_shapes=[pltpu.VMEM(a.shape, a.dtype) for a in loaded]
        + [
            pltpu.VMEM((BLOCK, 1024), jnp.bfloat16),
            pltpu.VMEM((BLOCK, 512), jnp.bfloat16),
            pltpu.VMEM((BLOCK, 512), jnp.bfloat16),
            pltpu.VMEM((D, BLOCK), jnp.bfloat16),
            pltpu.VMEM((128, D), jnp.bfloat16),
            pltpu.VMEM((128, D), jnp.bfloat16),
            pltpu.VMEM((8, TILE), jnp.float32),
        ]
        + [pltpu.VMEM((2, 4, 4, 2, 16, w), jnp.bfloat16) for w in fin_widths[:NEAR]]
        + [pltpu.VMEM((2, 8, w), jnp.float32) for w in fin_widths]
        + landing_shapes(steps)
        + mid_shapes(steps)
        + mid_shapes(steps)
        + [
            pltpu.SemaphoreType.DMA((len(steps), 3)),
            pltpu.SemaphoreType.DMA((len(steps), 3)),
            pltpu.SemaphoreType.DMA((n_w + 2,)),
            pltpu.SemaphoreType.DMA((n_w + 2,)),
            pltpu.SemaphoreType.DMA((n_w + 1,)),
            pltpu.SemaphoreType.DMA((len(loaded),)),
        ],
        compiler_params=pltpu.CompilerParams(
            collective_id=1, has_side_effects=True, vmem_limit_bytes=LIMIT
        ),
        name="finish",
    )(*loaded)


def columns(head):
    return pl.ds(pl.multiple_of(head * HEAD_DIM, HEAD_DIM), HEAD_DIM)


def exchange_start(moves, me, send, recv, local, first):
    copies = []
    for step in range(1, 8):
        there = (me + step) % 8
        for n, (source, target) in enumerate(moves):
            copy = pltpu.make_async_remote_copy(
                source(there), target(me), send.at[first + n, step], recv.at[first + n, step],
                device_id=sequence_chip(there),
            )
            copy.start()
            copies.append(copy)
    for n, (source, target) in enumerate(moves):
        copy = pltpu.make_async_copy(source(me), target(me), local.at[first + n])
        copy.start()
        copies.append(copy)
    return copies


def forward_kernel(*refs):
    x_in, tab_in, gains_in, wq_in, wk_in, wv_in = refs[:6]
    weights, refs = refs[10:14], refs[14:]
    q_out, k_out, v_out, o32_out, lse_ref, attended, normed_out, qpre_out, kpre_out, rows_ref = refs[:10]
    x_ref, tab, gains, wq, wk, wv, normed, qpre, kpre, q_low, k_low, v_low = refs[10:22]
    q_ref, k_ref, v_ref, o32_ref, o_low, scores, vt = refs[22:29]
    send, recv, head_send, head_recv, local, load, store = refs[29:]
    yh, z, x, yl, c = place()
    me = x * 2 + yl
    loads = load_all(
        [(x_in, x_ref), (gains_in, gains), (tab_in, tab), (wq_in, wq), (wk_in, wk), (wv_in, wv)], load
    )
    far = flat_pieces(FAR_PIECES)
    greet(torus_neighbours() + sequence_others())
    gather = Gather([None] * NEAR + list(weights), send, recv)
    active = [(n, piece, 2) for n, piece in enumerate(far)]
    gather.begin(active)
    for copy in loads:
        copy.wait()

    gain_rows = gains[...].astype(jnp.float32).T[:8]
    pick = (
        lax.broadcasted_iota(jnp.int32, (D, HEAD_DIM), 0)
        == 8 * lax.broadcasted_iota(jnp.int32, (D, HEAD_DIM), 1)
    ).astype(jnp.bfloat16)
    head_gains = jnp.dot(gain_rows.astype(jnp.bfloat16), pick, preferred_element_type=jnp.float32)
    rows_ref[...] = gain_rows
    rows_ref[2:4, :HEAD_DIM] = head_gains[2:4]
    gain_q, gain_k = head_gains[2:3], head_gains[3:4]
    values = x_ref[...].reshape(BLOCK, D).astype(jnp.float32)
    normed[...] = (values * rms_scale(values) * gain_rows[0:1]).astype(jnp.bfloat16)
    cosine, sine = rope_pair(tab)

    def head(pre, gain):
        unit = pre * rms_scale(pre) * gain
        return (unit * cosine + pltpu.roll(unit, HEAD_DIM // 2, 1) * sine).astype(jnp.bfloat16)

    for weight, pre_ref, low_ref, gain in ((wq, qpre, q_low, gain_q), (wk, kpre, k_low, gain_k)):
        for n in range(weight.shape[1] // 256):
            at = slice(n * 256, n * 256 + 256)
            pre = jnp.dot(normed[...], weight[:, at], preferred_element_type=jnp.float32)
            pre_ref[:, at] = pre
            low_ref[:, n * 256 : n * 256 + 128] = head(pre[:, :128], gain)
            low_ref[:, n * 256 + 128 : n * 256 + 256] = head(pre[:, 128:], gain)
    v_low[...] = jnp.dot(normed[...], wv[...], preferred_element_type=jnp.float32).astype(jnp.bfloat16)
    arriving = exchange_start(
        [
            (lambda j: q_low.at[:, columns(j)], lambda i: q_ref.at[i]),
            (lambda j: k_low.at[:, columns(j // 2)], lambda i: k_ref.at[i]),
            (lambda j: v_low.at[:, columns(j // 2)], lambda i: v_ref.at[i]),
        ],
        me, head_send, head_recv, local, 0,
    )
    stores = [
        pltpu.make_async_copy(a, b, store.at[n])
        for n, (a, b) in enumerate(
            ((normed, normed_out), (qpre, qpre_out), (kpre, kpre_out), (q_ref, q_out), (k_ref, k_out),
             (v_ref, v_out), (o32_ref, o32_out))
        )
    ]
    for copy in stores[:3]:
        copy.start()
    for copy in arriving:
        copy.wait()
    for copy in stores[3:6]:
        copy.start()
    for j in range(8):
        vt[j] = v_ref[j].T

    def one_block(i, _):
        q = q_ref[i]

        def score(j, top):
            s = nt(k_ref[j], q) * (score_scale * log2e)
            scores[j] = s
            return jnp.maximum(top, jnp.max(s, axis=0, keepdims=True))

        top = lax.fori_loop(0, i + 1, score, jnp.full((1, BLOCK), -1e30, jnp.float32))

        def weigh(j, carry):
            total, mixed = carry
            p = jnp.exp2(scores[j] - top)
            total = total + jnp.sum(p, axis=0, keepdims=True)
            mixed = mixed + jnp.dot(vt[j], p.astype(jnp.bfloat16), preferred_element_type=jnp.float32)
            return total, mixed

        total, mixed = lax.fori_loop(
            0, i + 1, weigh,
            (jnp.zeros((1, BLOCK), jnp.float32), jnp.zeros((HEAD_DIM, BLOCK), jnp.float32)),
        )
        out = (mixed / total).T
        o32_ref[i] = out
        o_low[i] = out.astype(jnp.bfloat16)
        lse_ref[i] = top + jnp.log2(total)
        return 0

    lax.fori_loop(0, 6, one_block, 0)
    gather.forward(active)
    lax.fori_loop(6, 8, one_block, 0)
    leaving = exchange_start(
        [(lambda j: o_low.at[j], lambda i: attended.at[:, columns(i)])],
        me, head_send, head_recv, local, 3,
    )
    stores[6].start()
    gather.arrive(active)
    gather.drain()
    for copy in stores:
        copy.wait()
    for copy in leaving:
        copy.wait()


def attend(near, weights):
    blocks = (8, BLOCK, HEAD_DIM)
    n_far = len(flat_pieces(FAR_PIECES))
    n_near = len(near)
    low, wide = jnp.bfloat16, jnp.float32
    return pl.pallas_call(
        forward_kernel,
        out_shape=[jax.ShapeDtypeStruct(w.shape, w.dtype) for w in weights]
        + [jax.ShapeDtypeStruct(blocks, low)] * 3
        + [
            jax.ShapeDtypeStruct(blocks, wide),
            jax.ShapeDtypeStruct((8, 1, BLOCK), wide),
            jax.ShapeDtypeStruct((BLOCK, 1024), low),
            jax.ShapeDtypeStruct((BLOCK, D), low),
            jax.ShapeDtypeStruct((BLOCK, 1024), wide),
            jax.ShapeDtypeStruct((BLOCK, 512), wide),
            jax.ShapeDtypeStruct((8, D), wide),
        ],
        in_specs=[HBM] * (n_near + 4),
        out_specs=[HBM] * 8 + [VMEM] + [HBM] * 4 + [VMEM],
        input_output_aliases={n_near + n: n for n in range(4)},
        scratch_shapes=[
            pltpu.VMEM((2, 128, D), low),
            pltpu.VMEM((2, 128, HEAD_DIM), wide),
            pltpu.VMEM((D, TILE), low),
            pltpu.VMEM((D, 1024), low),
            pltpu.VMEM((D, 512), low),
            pltpu.VMEM((D, 512), low),
            pltpu.VMEM((BLOCK, D), low),
            pltpu.VMEM((BLOCK, 1024), wide),
            pltpu.VMEM((BLOCK, 512), wide),
            pltpu.VMEM((BLOCK, 1024), low),
            pltpu.VMEM((BLOCK, 512), low),
            pltpu.VMEM((BLOCK, 512), low),
        ]
        + [pltpu.VMEM(blocks, low)] * 3
        + [
            pltpu.VMEM(blocks, wide),
            pltpu.VMEM(blocks, low),
            pltpu.VMEM((8, BLOCK, BLOCK), wide),
            pltpu.VMEM((8, HEAD_DIM, BLOCK), low),
            pltpu.SemaphoreType.DMA((n_far, 3)),
            pltpu.SemaphoreType.DMA((n_far, 3)),
            pltpu.SemaphoreType.DMA((4, 8)),
            pltpu.SemaphoreType.DMA((4, 8)),
            pltpu.SemaphoreType.DMA((4,)),
            pltpu.SemaphoreType.DMA((6,)),
            pltpu.SemaphoreType.DMA((7,)),
        ],
        compiler_params=pltpu.CompilerParams(
            collective_id=2, has_side_effects=True, vmem_limit_bytes=LIMIT
        ),
        name="attend",
    )(*near, *weights)


def backward_kernel(*refs):
    far = flat_pieces(FAR_PIECES)
    n_far = len(far)
    q_in, k_in, v_in, o32_in, lse_in, do_in = refs[:6]
    grads = [None] * NEAR + list(refs[6:10])
    dq_out, dk_out, dv_out = refs[10:13]
    planes_out, refs = refs[13 : 13 + n_far], refs[13 + n_far :]
    q_ref, k_ref, v_ref, o32_ref, lse_ref = refs[:5]
    do_ref, dq_low, dk_low, dv_low, kt, dk_acc, dv_acc = refs[5:12]
    planes, refs = refs[12 : 12 + n_far], refs[12 + n_far :]
    landing, refs = refs[: 3 * n_far], refs[3 * n_far :]
    mids, bases, refs = refs[:n_far], refs[n_far : 2 * n_far], refs[2 * n_far :]
    send, recv, load, head_send, head_recv, local, saved_load, store = refs
    yh, z, x, yl, c = place()
    me = x * 2 + yl
    saved = load_all(
        [(q_in, q_ref), (k_in, k_ref), (v_in, v_ref), (o32_in, o32_ref), (lse_in, lse_ref)], saved_load
    )
    loads = {}
    for n, piece in enumerate(far):
        for m, (offset, target) in enumerate(((piece.way, mids[n]), (0, bases[n]))):
            loads[n, m] = pltpu.make_async_copy(grad_spot(grads, piece, offset), target, load.at[n, m])
            loads[n, m].start()
    greet(torus_neighbours() + sequence_others())
    arriving = exchange_start(
        [(lambda j: do_in.at[:, columns(j)], lambda i: do_ref.at[i])],
        me, head_send, head_recv, local, 0,
    )
    scatter = Scatter(landing, send, recv)
    for which in (0, 1):
        for n, piece in enumerate(far):
            offset, step = ((2, piece.way), (-piece.way, -piece.way))[which]
            scatter.start(n, piece.order[2], step, grad_spot(grads, piece, offset), which)
    for copy in saved:
        copy.wait()
    for j in range(8):
        kt[j] = k_ref[j].T
    dk_acc[...] = jnp.zeros_like(dk_acc)
    dv_acc[...] = jnp.zeros_like(dv_acc)
    for copy in arriving:
        copy.wait()

    def one_block(i, _):
        q, do, lse = q_ref[i], do_ref[i], lse_ref[i]
        delta = jnp.sum((do.astype(jnp.float32) * o32_ref[i]).T, axis=0, keepdims=True)

        def one_pair(j, dqt):
            p = jnp.exp2(nt(k_ref[j], q) * (score_scale * log2e) - lse)
            dp = nt(v_ref[j], do)
            ds = (p * (dp - delta)).astype(jnp.bfloat16)
            dv_acc[j] += jnp.dot(p.astype(jnp.bfloat16), do, preferred_element_type=jnp.float32)
            dk_acc[j] += jnp.dot(ds, q, preferred_element_type=jnp.float32)
            return dqt + jnp.dot(kt[j], ds, preferred_element_type=jnp.float32)

        dqt = lax.fori_loop(0, i + 1, one_pair, jnp.zeros((HEAD_DIM, BLOCK), jnp.float32))
        dq_low[i] = (dqt * score_scale).T.astype(jnp.bfloat16)
        return 0

    lax.fori_loop(0, 6, one_block, 0)
    for n, piece in enumerate(far):
        scatter.copies[n, 0].wait_recv()
        loads[n, 0].wait()
        add_sets(scatter_dims(piece, 0), mids[n], [mids[n], landing[3 * n]])
        scatter.start(n, piece.order[2], piece.way, mids[n], 2)
    lax.fori_loop(6, 8, one_block, 0)
    dk_low[...] = (dk_acc[...] * score_scale).astype(jnp.bfloat16)
    dv_low[...] = dv_acc[...].astype(jnp.bfloat16)
    leaving = exchange_start(
        [
            (lambda j: dq_low.at[j], lambda i: dq_out.at[:, columns(i)]),
            (lambda j: dk_low.at[j], lambda i: dk_out.at[i % 2, :, columns(i // 2)]),
            (lambda j: dv_low.at[j], lambda i: dv_out.at[i % 2, :, columns(i // 2)]),
        ],
        me, head_send, head_recv, local, 1,
    )
    for n, piece in enumerate(far):
        scatter.copies[n, 1].wait_recv()
        scatter.copies[n, 2].wait_recv()
        loads[n, 1].wait()
        add_sets(scatter_dims(piece, 0), planes[n], [bases[n], landing[3 * n + 1], landing[3 * n + 2]])
        keep = pltpu.make_async_copy(planes[n], planes_out[n], store.at[n])
        keep.start()
        leaving.append(keep)
    scatter.drain()
    for copy in leaving:
        copy.wait()


def attend_back(saved, grad_att, grads):
    far = flat_pieces(FAR_PIECES)
    n_far = len(far)
    steps = [(p, 0) for p in far]
    blocks = (8, BLOCK, HEAD_DIM)
    return pl.pallas_call(
        backward_kernel,
        out_shape=[
            jax.ShapeDtypeStruct((BLOCK, 1024), jnp.bfloat16),
            jax.ShapeDtypeStruct((2, BLOCK, 512), jnp.bfloat16),
            jax.ShapeDtypeStruct((2, BLOCK, 512), jnp.bfloat16),
        ]
        + [
            jax.ShapeDtypeStruct((*scatter_dims(p, 0), 16, p.width), jnp.bfloat16) for p in far
        ],
        in_specs=[HBM] * 10,
        out_specs=[HBM] * (3 + n_far),
        scratch_shapes=[pltpu.VMEM(a.shape, a.dtype) for a in saved]
        + [pltpu.VMEM(blocks, jnp.bfloat16)] * 4
        + [
            pltpu.VMEM((8, HEAD_DIM, BLOCK), jnp.bfloat16),
            pltpu.VMEM(blocks, jnp.float32),
            pltpu.VMEM(blocks, jnp.float32),
        ]
        + mid_shapes(steps)
        + landing_shapes(steps)
        + mid_shapes(steps)
        + mid_shapes(steps)
        + [
            pltpu.SemaphoreType.DMA((n_far, 3)),
            pltpu.SemaphoreType.DMA((n_far, 3)),
            pltpu.SemaphoreType.DMA((n_far, 2)),
            pltpu.SemaphoreType.DMA((4, 8)),
            pltpu.SemaphoreType.DMA((4, 8)),
            pltpu.SemaphoreType.DMA((4,)),
            pltpu.SemaphoreType.DMA((5,)),
            pltpu.SemaphoreType.DMA((n_far,)),
        ],
        compiler_params=pltpu.CompilerParams(
            collective_id=3, has_side_effects=True, vmem_limit_bytes=LIMIT
        ),
        name="attend_back",
    )(*saved, grad_att, *grads)


def middle_kernel(*refs):
    att_in, x_in, g_in, rows_in, wo_in, wg_in, wu_in, wd_in = refs[:8]
    output, grad_att_out, gmid_out, post_out = refs[8:12]
    dwo_out, dwg_out, dwu_out, dwd_out = refs[12:16]
    att, x_ref, g_ref, rows, wo, wg, wu, wd = refs[16:24]
    (branch, middle, hidden, hidden_t, g_t, grad_act, act, gate_grad, up_grad, grad_hidden, branch_t,
     down_own, grad_att, dwo, dwg, dwu, dwd) = refs[24:41]
    out1, in1, out2, in2, out3, in3 = refs[41:47]
    pair_send, pair_recv, load, store = refs[47:]
    yh, z, x, yl, c = place()
    sib = sibling()
    loads = load_all(
        [(att_in, att), (wo_in, wo), (g_in, g_ref), (wd_in, wd), (x_in, x_ref), (rows_in, rows),
         (wg_in, wg), (wu_in, wu)], load
    )
    greet([sib])
    swaps = []

    def swap(source, target):
        n = len(swaps)
        copy = pltpu.make_async_remote_copy(
            source, target, pair_send.at[n], pair_recv.at[n], device_id=sib
        )
        copy.start()
        swaps.append(copy)
        return copy

    def part(n, width=256):
        return pl.ds(n * width, width)

    loads[0].wait()
    loads[1].wait()
    first = []
    for n in range(4):
        block = nt(att[...], wo[part(n), :])
        branch[:, part(n)] = block
        out1[n] = block.astype(jnp.bfloat16)
        first.append(swap(out1.at[n], in1.at[n]))
    loads[2].wait()
    loads[3].wait()
    g_low = g_ref[...].reshape(BLOCK, D)
    for n in range(6):
        grad_act[:, part(n)] = jnp.dot(g_low, wd[:, part(n)], preferred_element_type=jnp.float32)
    g_t[...] = g_low.T
    loads[4].wait()
    loads[5].wait()
    for n in range(4):
        first[n].wait_recv()
        middle[:, part(n)] = (
            x_ref[...].reshape(BLOCK, D)[:, n * 256 : n * 256 + 256].astype(jnp.float32)
            + (branch[:, part(n)] + in1[n].astype(jnp.float32))
        )
    gain = rows[1:2, :]
    scale = rms_scale(middle[...])
    hidden[...] = (middle[...] * scale * gain).astype(jnp.bfloat16)
    loads[6].wait()
    loads[7].wait()
    for n in range(6):
        gate = jnp.dot(hidden[...], wg[:, part(n)], preferred_element_type=jnp.float32)
        up = jnp.dot(hidden[...], wu[:, part(n)], preferred_element_type=jnp.float32)
        sigma = jax.nn.sigmoid(gate)
        swish = gate * sigma
        grad = grad_act[:, part(n)]
        act[:, part(n)] = (swish * up).astype(jnp.bfloat16)
        gate_grad[:, part(n)] = (grad * up * (sigma * (1.0 + gate * (1.0 - sigma)))).astype(jnp.bfloat16)
        up_grad[:, part(n)] = (grad * swish).astype(jnp.bfloat16)
    second = []
    for n in range(4):
        block = nt(gate_grad[...], wg[part(n), :]) + nt(up_grad[...], wu[part(n), :])
        grad_hidden[:, part(n)] = block
        out2[n] = block.astype(jnp.bfloat16)
        second.append(swap(out2.at[n], in2.at[n]))
    away = pl.ds(pl.multiple_of((1 - c) * 128, 128), 128)
    own = pl.ds(pl.multiple_of(c * 128, 128), 128)
    out3[...] = nt(act[away, :], wd[...]).astype(jnp.bfloat16)
    third = swap(out3, in3)
    down_own[...] = nt(act[own, :], wd[...])
    hidden_t[...] = hidden[...].T
    stores = []

    def keep(source, target):
        copy = pltpu.make_async_copy(source, target, store.at[len(stores)])
        copy.start()
        stores.append(copy)

    for lhs, rhs, grads, target in (
        (hidden_t, gate_grad, dwg, dwg_out), (hidden_t, up_grad, dwu, dwu_out), (g_t, act, dwd, dwd_out)
    ):
        for n in range(4):
            grads[part(n), :] = jnp.dot(
                lhs[part(n), :], rhs[...], preferred_element_type=jnp.float32
            ).astype(jnp.bfloat16)
        keep(grads, target)
    for n in range(4):
        second[n].wait_recv()
        grad_hidden[:, part(n)] = grad_hidden[:, part(n)] + in2[n].astype(jnp.float32)
    grad_in, terms = norm_back(grad_hidden[...], middle[...], scale, gain)
    grad_hidden[...] = terms
    post_out[...] = jnp.broadcast_to(jnp.sum(grad_hidden[own, :], axis=0, keepdims=True), (8, D))
    grad_hidden[...] = g_low.astype(jnp.float32) + grad_in
    gmid_out[...] = grad_hidden[own, :]
    branch_grad = grad_hidden[...].astype(jnp.bfloat16)
    branch_t[...] = branch_grad.T
    for n in range(4):
        grad_att[:, part(n)] = jnp.dot(
            branch_grad, wo[:, part(n)], preferred_element_type=jnp.float32
        ).astype(jnp.bfloat16)
    keep(grad_att, grad_att_out)
    for n in range(4):
        dwo[part(n), :] = jnp.dot(
            branch_t[part(n), :], att[...], preferred_element_type=jnp.float32
        ).astype(jnp.bfloat16)
    keep(dwo, dwo_out)
    third.wait_recv()
    output[...] = (
        middle[own, :] + (down_own[...] + in3[...].astype(jnp.float32))
    ).astype(jnp.bfloat16)
    for copy in swaps:
        copy.wait_send()
    for copy in stores:
        copy.wait()


def feed_forward(arrays):
    low, wide = jnp.bfloat16, jnp.float32
    shapes = [(D, 1024), (D, 1536), (D, 1536), (D, 1536)]
    return pl.pallas_call(
        middle_kernel,
        out_shape=[
            jax.ShapeDtypeStruct((128, D), low),
            jax.ShapeDtypeStruct((BLOCK, 1024), low),
            jax.ShapeDtypeStruct((128, D), wide),
            jax.ShapeDtypeStruct((8, D), wide),
        ]
        + [jax.ShapeDtypeStruct(s, low) for s in shapes],
        in_specs=[HBM] * 8,
        out_specs=[VMEM, HBM, VMEM, VMEM] + [HBM] * 4,
        scratch_shapes=[pltpu.VMEM(a.shape, a.dtype) for a in arrays]
        + [
            pltpu.VMEM((BLOCK, D), wide),
            pltpu.VMEM((BLOCK, D), wide),
            pltpu.VMEM((BLOCK, D), low),
            pltpu.VMEM((D, BLOCK), low),
            pltpu.VMEM((D, BLOCK), low),
            pltpu.VMEM((BLOCK, 1536), wide),
            pltpu.VMEM((BLOCK, 1536), low),
            pltpu.VMEM((BLOCK, 1536), low),
            pltpu.VMEM((BLOCK, 1536), low),
            pltpu.VMEM((BLOCK, D), wide),
            pltpu.VMEM((D, BLOCK), low),
            pltpu.VMEM((128, D), wide),
            pltpu.VMEM((BLOCK, 1024), low),
        ]
        + [pltpu.VMEM(s, low) for s in shapes]
        + [pltpu.VMEM((4, BLOCK, 256), low)] * 4
        + [pltpu.VMEM((128, D), low)] * 2
        + [
            pltpu.SemaphoreType.DMA((9,)),
            pltpu.SemaphoreType.DMA((9,)),
            pltpu.SemaphoreType.DMA((8,)),
            pltpu.SemaphoreType.DMA((5,)),
        ],
        compiler_params=pltpu.CompilerParams(
            collective_id=4, has_side_effects=True, vmem_limit_bytes=LIMIT
        ),
        name="feed_forward",
    )(*arrays)


def results_kernel(n, *refs):
    for source, target in zip(refs[:n], refs[n:]):
        target[...] = source[...]


def results(arrays):
    n = len(arrays)
    return pl.pallas_call(
        functools.partial(results_kernel, n),
        out_shape=[jax.ShapeDtypeStruct(a.shape, a.dtype) for a in arrays],
        in_specs=[VMEM] * n,
        out_specs=[VMEM] * n,
        name="results",
    )(*arrays)


def split_columns(shard):
    rows, width = shard.shape
    return jnp.transpose(shard.reshape(rows, CORES, width // CORES), (1, 0, 2))


def body(
    tokens,
    positions,
    in_gain,
    q_gain,
    k_gain,
    w_query,
    w_key,
    w_value,
    w_out,
    post_gain,
    w_gate,
    w_up,
    w_down,
    cotangent,
):
    half = HEAD_DIM // 2
    frequency = rope_base ** (-2.0 * jnp.arange(half, dtype=jnp.float32) / HEAD_DIM)
    angles = positions[0].astype(jnp.float32)[:, None] * frequency[None, :]
    table = jnp.concatenate([jnp.cos(angles), jnp.sin(angles)], axis=-1)
    gain_rows = jnp.stack(
        [jnp.pad(g, (0, TILE - g.shape[0])) for g in (in_gain, post_gain, q_gain, k_gain)]
    )
    gain_rows = jnp.pad(gain_rows, ((0, 4), (0, 0)))
    shards = [
        split_columns(w) for w in (w_query, w_key, w_value, w_out.T, w_gate, w_up, w_down.T)
    ]
    gathered = gather_weights(gain_rows, shards, [tokens[0], cotangent[0], table])

    def whole(weight):
        return weight.reshape(D, weight.shape[-1])

    wq, wk, wv, gains = [whole(w) for w in gathered[:4]]
    x_pair, g_pair, tables = gathered[8:]
    *far, q_all, k_all, v_all, mixed, log_total, attended, normed, q_pre, k_pre, rows = attend(
        [x_pair, tables, gains, wq, wk, wv], gathered[4:8]
    )
    wo, wg, wu, wd = [whole(w) for w in far]
    output, grad_att, grad_middle, post_part, *far_grads = feed_forward(
        [attended, x_pair, g_pair, rows, wo, wg, wu, wd]
    )
    grad_query, key_parts, value_parts, *planes = attend_back(
        (q_all, k_all, v_all, mixed, log_total),
        grad_att,
        [g.reshape(2, 4, 4, 2, 16, g.shape[-1]) for g in far_grads],
    )
    last = finish(
        [grad_query, key_parts, value_parts, q_pre, k_pre, normed, tables, rows, x_pair, wq, wk, wv,
         grad_middle, post_part],
        planes,
    )
    *sums, in_gain_grad, post_gain_grad, q_gain_grad, k_gain_grad, input_grad, output = results(
        [*last, output]
    )
    return (
        output[None],
        input_grad[None],
        in_gain_grad[0],
        q_gain_grad[0],
        k_gain_grad[0],
        sums[0],
        sums[1],
        sums[2],
        sums[3].T,
        post_gain_grad[0],
        sums[4],
        sums[5],
        sums[6].T,
    )


def solution(mesh):
    placed = (
        P("dp", "seq", None),
        P("dp", "seq"),
        P(("dp", "seq")),
        P(("dp", "seq")),
        P(("dp", "seq")),
        P(("dp", "seq"), None),
        P(("dp", "seq"), None),
        P(("dp", "seq"), None),
        P(None, ("dp", "seq")),
        P(("dp", "seq")),
        P(("dp", "seq"), None),
        P(("dp", "seq"), None),
        P(None, ("dp", "seq")),
        P("dp", "seq", None),
    )
    return jax.shard_map(
        body,
        mesh=mesh,
        in_specs=placed,
        out_specs=(
            P("dp", "seq", None),
            P("dp", "seq", None),
            P(("dp", "seq")),
            P(("dp", "seq")),
            P(("dp", "seq")),
            P(("dp", "seq"), None),
            P(("dp", "seq"), None),
            P(("dp", "seq"), None),
            P(None, ("dp", "seq")),
            P(("dp", "seq")),
            P(("dp", "seq"), None),
            P(("dp", "seq"), None),
            P(None, ("dp", "seq")),
        ),
        check_vma=False,
    )
```

time: 336 us -> 263 us (0.78)
  local copies, waits for them, and re-layouts: 45.3 us -> 0.69 us
  Pallas kernels: 216 us -> 257 us
  matrix products: 31.9 us -> 0 us
  other arithmetic: 31.5 us -> 2.28 us
  starting transfers between devices: 6.16 us -> 0 us
    pallas_call x1 -> x3, Pallas kernels: 51.1 us -> 86.2 us  [the longest x1 57.4 us: finish(): pl.pallas_call(last_kernel, out_shape=[jax.ShapeDtypeStruct((8, 2 * w), j...]
    dot_general x21 -> x0, matrix products: 31.9 us -> none  [the longest x14 21.7 us: contract(): lax.dot_general(left_op, right_op, (((left_dim,), (right_dim,)), ((), ())...]
    unnamed x143 -> x0, local copies, waits for them, and re-layouts: 20.4 us -> none
    reduce_sum x7 -> x0, other arithmetic: 9.42 us -> none  [the longest x2 3.05 us: rms_scale(): jnp.mean(values * values, axis=-1, keepdims=True) + eps_norm]
    pallas_call x1, Pallas kernels: 57 us -> 63.9 us  [attend(): pl.pallas_call(forward_kernel, out_shape=[jax.ShapeDtypeStruct(w.shape, w...]
    ppermute x4 -> x0, starting transfers between devices: 6.16 us -> none  [other_core(): return lax.ppermute(values, 'seq', [(s, s ^ 1) for s in range(16)])]
    squeeze x7 -> x0, local copies, waits for them, and re-layouts: 5.52 us -> none  [body(): wide = [jnp.concatenate([s[0], s[1]], axis=1) for s in sums[:3] + sums[4:]]]
    another operation x7 -> x1, other arithmetic: 4.6 us -> 0.59 us  [body(): jnp.stack([jnp.pad(g, (0, TILE - g.shape[0])) for g in (in_gain, post_gai...]
  transfers between devices with their start and end apart: 4 -> 0, of which waited for: 0 -> 0; matrix products, arithmetic and copies ran while one was open for 12% -> 0% of each run, Pallas kernels for 19% -> 0%
where the time goes in v3:
time: 263 us; the launch traced here: 262 us
  Pallas kernels  257 us (98%)
    pallas_call x1, Pallas kernels, attend(): pl.pallas_call(forward_kernel, out_shape=[jax.ShapeDtypeStruct(w.shape, w...  63.9 us
    pallas_call x1, Pallas kernels, attend_back(): pl.pallas_call(backward_kernel, out_shape=[jax.ShapeDtypeStruct((BLOCK, 1...  60.6 us
    pallas_call x1, Pallas kernels, finish(): pl.pallas_call(last_kernel, out_shape=[jax.ShapeDtypeStruct((8, 2 * w), j...  57.4 us
    pallas_call x1, Pallas kernels, gather_weights(): pl.pallas_call(functools.partial(gather_kernel, n_w, n_p), out_shape=[jax...  46.7 us
    pallas_call x1, Pallas kernels, feed_forward(): pl.pallas_call(middle_kernel, out_shape=[jax.ShapeDtypeStruct((128, D), l...  25.4 us

profile of v3, /device:TPU:1, one launch (start us, length us, event | category | flops | bytes accessed | tf_op | source)
XLA Modules:
  0.0 262.5 jit_solution(14110456385314881865)
XLA Ops:
  2.0 0.7 convert_bitcast_fusion
  2.6 0.7 pad_bitcast_fusion.2
  3.3 0.6 fusion.6.refs_0_
  3.9 0.3 multiply_cosine_fusion
  4.2 0.7 pad_maximum_fusion.refs_10_
  4.9 46.7 %gather_weights.1 = (bf16[2,4,4,2,2,8,1024]{6,5,4,3,2,1,0:T(8,128)(2,1)}, bf16[2,4,4,2,2,8,512]{6,5,4,3,2,1,0:T(8,128)(2,1)}, bf16[2,4,4,2,2,8,512]{6,5,4,3,2,1,...) custom-call(bf16[8,128]{1,0:T(8,128)(2,1)} %fusion.6.refs_0_, ...), custom_call_target="tpu_custom_call" | custom-call | tf_op jit(solution)/shard_map/gather_weights/pallas_call | solution.py:279
  51.6 63.9 %attend.1 = (bf16[2,4,4,2,2,8,1024]{6,5,4,3,2,1,0:T(8,128)(2,1)}, bf16[2,4,4,2,2,8,1536]{6,5,4,3,2,1,0:T(8,128)(2,1)}, bf16[2,4,4,2,2,8,1536]{6,5,4,3,2,1,0:T(8,...) custom-call(bf16[2,128,1024]{2,1,0:T(8,128)(2,1)} %get-tuple-element, ...), custom_call_target="tpu_custom_call", output_to_operand_aliasing={{0}: (6, {}), {1}: (7, {}), {2}: (8, {}), {3}: (9, {})} | custom-call | tf_op jit(solution)/shard_map/attend/pallas_call | solution.py:757
  115.5 25.4 %feed_forward.1 = (bf16[128,1024]{1,0:T(8,128)(2,1)}, bf16[256,1024]{1,0:T(8,128)(2,1)}, f32[128,1024]{1,0:T(8,128)}, f32[8,1024]{1,0:T(8,128)}, bf16[1024,1024]...) custom-call(bf16[256,1024]{1,0:T(8,128)(2,1)} %get-tuple-element.97.refs_0_, ...), custom_call_target="tpu_custom_call" | custom-call | tf_op jit(solution)/shard_map/feed_forward/pallas_call | solution.py:1067
  141.0 60.6 %attend_back.1 = (bf16[256,1024]{1,0:T(8,128)(2,1)}, bf16[2,256,512]{2,1,0:T(8,128)(2,1)}, bf16[2,256,512]{2,1,0:T(8,128)(2,1)}, bf16[2,4,2,16,1024]{4,3,2,1,0:T...) custom-call(bf16[8,256,128]{2,1,0:T(8,128)(2,1)} %get-tuple-element., ...), custom_call_target="tpu_custom_call" | custom-call | tf_op jit(solution)/shard_map/attend_back/pallas_call | solution.py:901
  201.6 57.4 %finish.1 = (f32[8,2048]{1,0:T(8,128)}, f32[8,1024]{1,0:T(8,128)}, f32[8,1024]{1,0:T(8,128)}, f32[8,2048]{1,0:T(8,128)}, f32[8,3072]{1,0:T(8,128)}, /*index=5*/f...) custom-call(bf16[256,1024]{1,0:T(8,128)(2,1)} %get-tuple-element.109, ...), custom_call_target="tpu_custom_call" | custom-call | tf_op jit(solution)/shard_map/finish/pallas_call | solution.py:581
  259.0 3.4 %results.1 = (f32[8,2048]{1,0:T(8,128)}, f32[8,1024]{1,0:T(8,128)}, f32[8,1024]{1,0:T(8,128)}, f32[8,2048]{1,0:T(8,128)}, f32[8,3072]{1,0:T(8,128)}, /*index=5*/...) custom-call(f32[8,2048]{1,0:T(8,128)} %get-tuple-element.125.refs_0_, ...), custom_call_target="tpu_custom_call" | custom-call | tf_op jit(solution)/shard_map/results/pallas_call | solution.py:1117
  (2 shorter events, 0.0 us)

commit v4 on v3

v4 whole, which is shorter than its diff:
```python
import functools
import math

import jax
import jax.numpy as jnp
from jax import lax
from jax.experimental import pallas as pl
from jax.experimental.pallas import tpu as pltpu
from jax.sharding import PartitionSpec as P

HEADS = 16
KV_HEADS = 8
HEAD_DIM = 128
D = 1024
FF = 3072
BLOCK = 256
CORES = 2

TILE = 128

eps_norm = 1e-06
rope_base = 1000000.0
score_scale = 1.0 / math.sqrt(HEAD_DIM)
log2e = math.log2(math.e)


def place():
    dp = lax.axis_index("dp")
    seq = lax.axis_index("seq")
    return dp // 4, dp % 4, seq // 4, (seq // 2) % 2, seq % 2


def device(yh, z, x, yl, c):
    return {"dp": yh * 4 + z, "seq": x * 4 + yl * 2 + c}


def sibling():
    yh, z, x, yl, c = place()
    return device(yh, z, x, yl, 1 - c)


def neighbour(axis, step):
    yh, z, x, yl, c = place()
    if axis == "x":
        return device(yh, z, (x + step + 4) % 4, yl, c)
    if axis == "z":
        return device(yh, (z + step + 4) % 4, x, yl, c)
    y = (yh * 2 + yl + step + 4) % 4
    return device(y // 2, z, x, y % 2, c)


ORDERS = (("x", "y", "z"), ("y", "z", "x"), ("z", "x", "y"))


def chip_set(whole_axes, axis, step):
    yh, z, x, yl, _ = place()
    iz, ix, iyh, iyl = z, x, yh, yl
    if axis == "x":
        ix = (x + step + 4) % 4
    elif axis == "z":
        iz = (z + step + 4) % 4
    else:
        y = (yh * 2 + yl + step + 4) % 4
        iyh, iyl = y // 2, y % 2
    every = slice(None)
    if "x" in whole_axes:
        ix = every
    if "z" in whole_axes:
        iz = every
    if "y" in whole_axes:
        iyh, iyl = every, every
    return (iyh, iz, ix, iyl)


def set_dims(whole_axes):
    dims = ()
    if "y" in whole_axes:
        dims += (2,)
    if "z" in whole_axes:
        dims += (4,)
    if "x" in whole_axes:
        dims += (4,)
    if "y" in whole_axes:
        dims += (2,)
    return dims


NEAR_PIECES = (
    (((0, 0, 3),), ((0, 3, 3),)),
    (((1, 0, 3),), ((2, 0, 3),)),
    (((0, 6, 2), (1, 3, 1)), ((2, 3, 1), (3, 0, 1))),
)
FAR_PIECES = (
    (((5, 0, 10),), ((6, 0, 10),)),
    (((4, 0, 6),), ((7, 0, 6),)),
    (((7, 6, 6),), ((4, 6, 2), (5, 10, 2), (6, 10, 2))),
)
NEAR = 4
LIMIT = 60 << 20


class Piece:
    def __init__(self, colour, half, array, first, tiles):
        self.name = (array, first)
        self.order = ORDERS[colour]
        self.way = 1 if half == 0 else -1
        self.array = array
        self.width = tiles * TILE
        self.cols = pl.ds(first * TILE, self.width)


def flat_pieces(pieces):
    return [
        Piece(colour, half, *piece)
        for colour in range(3)
        for half in range(2)
        for piece in pieces[colour][half]
    ]


def greet(others):
    barrier = pltpu.get_barrier_semaphore()
    for other in others:
        pl.semaphore_signal(barrier, inc=1, device_id=other)
    pl.semaphore_wait(barrier, len(others))


def torus_neighbours():
    return [neighbour(axis, step) for axis in ("x", "y", "z") for step in (1, -1)]


def sequence_chip(number):
    yh, z, x, yl, c = place()
    return device(yh, z, number // 2, number % 2, c)


def sequence_others():
    yh, z, x, yl, c = place()
    me = x * 2 + yl
    return [sequence_chip((me + step) % 8) for step in range(1, 8)]


HBM = pl.BlockSpec(memory_space=pltpu.HBM)
VMEM = pl.BlockSpec(memory_space=pltpu.VMEM)


def load_all(pairs, sems):
    copies = [pltpu.make_async_copy(a, b, sems.at[n]) for n, (a, b) in enumerate(pairs)]
    for copy in copies:
        copy.start()
    return copies


def nt(left, right):
    return lax.dot_general(left, right, (((1,), (1,)), ((), ())), preferred_element_type=jnp.float32)


def rms_scale(values):
    return lax.rsqrt(jnp.mean(values * values, axis=-1, keepdims=True) + eps_norm)


def norm_back(grad_out, values, scale_factor, gain):
    weighted = grad_out * gain
    inner = jnp.mean(weighted * values, axis=-1, keepdims=True)
    grad_in = (
        scale_factor * weighted - values * (scale_factor * scale_factor * scale_factor) * inner
    )
    return (grad_in, grad_out * values * scale_factor)


def rope_pair(tab):
    table = tab[...].reshape(BLOCK, HEAD_DIM)
    turned = pltpu.roll(table, HEAD_DIM // 2, 1)
    low = lax.broadcasted_iota(jnp.int32, (BLOCK, HEAD_DIM), 1) < HEAD_DIM // 2
    return jnp.where(low, table, turned), jnp.where(low, -turned, table)


class Gather:
    def __init__(self, outs, send, recv):
        self.outs, self.send, self.recv = outs, send, recv
        self.copies = {}

    def start(self, n, piece, phase, which):
        axis, whole = piece.order[phase], piece.order[:phase]
        step, offset = ((piece.way, 0), (-piece.way, 0), (piece.way, -piece.way))[which]
        ref = self.outs[piece.array].at[
            (*chip_set(whole, axis, offset), slice(None), slice(None), piece.cols)
        ]
        copy = pltpu.make_async_remote_copy(
            ref, ref, self.send.at[n, which], self.recv.at[n, which],
            device_id=neighbour(axis, step),
        )
        copy.start()
        self.copies[n, which] = copy

    def begin(self, active):
        for which in (0, 1):
            for n, piece, phase in active:
                self.start(n, piece, phase, which)

    def forward(self, active):
        for n, piece, phase in active:
            self.copies[n, 0].wait_recv()
            self.start(n, piece, phase, 2)

    def arrive(self, active):
        for n, _, _ in active:
            self.copies[n, 1].wait_recv()
            self.copies[n, 2].wait_recv()

    def advance(self, active, following):
        for (n, _, _), (m, piece, phase) in zip(active, following):
            self.copies[n, 1].wait_recv()
            self.copies[n, 2].wait_recv()
            self.start(m, piece, phase, 0)
            self.start(m, piece, phase, 1)

    def drain(self):
        for copy in self.copies.values():
            copy.wait_send()


def kept_index(kept, axis, step):
    iyh, iz, ix, iyl = chip_set(tuple(a for a in kept if a != axis), axis, step)
    index = ()
    if "y" in kept:
        index += (iyh,)
    if "z" in kept:
        index += (iz,)
    if "x" in kept:
        index += (ix,)
    if "y" in kept:
        index += (iyl,)
    return index


def add_sets(dims, target, terms):
    def one(flat_index, _):
        index, rest = [], flat_index
        for size in reversed(dims):
            index.insert(0, rest % size)
            rest = rest // size
        at = tuple(index)
        total = terms[0][at].astype(jnp.float32)
        for term in terms[1:]:
            total = total + term[at].astype(jnp.float32)
        target[at] = total.astype(jnp.bfloat16)
        return 0

    if dims:
        lax.fori_loop(0, math.prod(dims), one, 0)
    else:
        total = terms[0][...].astype(jnp.float32)
        for term in terms[1:]:
            total = total + term[...].astype(jnp.float32)
        target[...] = total.astype(jnp.bfloat16)


class Scatter:
    def __init__(self, steps, grads, landing, mids, results, fin, send, recv):
        self.grads, self.landing, self.mids, self.results = grads, landing, mids, results
        self.fin, self.send, self.recv = fin, send, recv
        self.number = {(piece.name, phase): n for n, (piece, phase) in enumerate(steps)}
        self.copies = {}
        self.loads = {}

    def source(self, piece, phase, offset):
        if phase == 0:
            return grad_spot(self.grads, piece, offset)
        axis, kept = piece.order[2 - phase], piece.order[: 3 - phase]
        held = self.results[self.number[piece.name, phase - 1]]
        return held.at[(*kept_index(kept, axis, offset), slice(None), slice(None))]

    def load(self, piece, sems):
        n = self.number[piece.name, 0]
        for m, (offset, target) in enumerate(((piece.way, self.mids[n]), (0, self.results[n]))):
            self.loads[n, m] = pltpu.make_async_copy(
                grad_spot(self.grads, piece, offset), target, sems.at[m]
            )
            self.loads[n, m].start()

    def start(self, piece, phase, which):
        n = self.number[piece.name, phase]
        way = piece.way
        offset, step = ((2, way), (-way, -way), (way, way))[which]
        source = self.mids[n] if which == 2 else self.source(piece, phase, offset)
        copy = pltpu.make_async_remote_copy(
            source, self.landing[3 * n + which], self.send.at[n, which], self.recv.at[n, which],
            device_id=neighbour(piece.order[2 - phase], step),
        )
        copy.start()
        self.copies[n, which] = copy

    def begin(self, pieces, phase):
        for which in (0, 1):
            for piece in pieces:
                self.start(piece, phase, which)

    def middle(self, pieces, phase):
        for piece in pieces:
            n = self.number[piece.name, phase]
            self.copies[n, 0].wait_recv()
            own = self.source(piece, phase, piece.way)
            if (n, 0) in self.loads:
                self.loads[n, 0].wait()
                own = self.mids[n]
            add_sets(scatter_dims(piece, phase), self.mids[n], [own, self.landing[3 * n]])
            self.start(piece, phase, 2)

    def end(self, pieces, phase):
        for piece in pieces:
            n = self.number[piece.name, phase]
            self.copies[n, 1].wait_recv()
            self.copies[n, 2].wait_recv()
            base = self.source(piece, phase, 0)
            if (n, 1) in self.loads:
                self.loads[n, 1].wait()
                base = self.results[n]
            terms = [base, self.landing[3 * n + 1], self.landing[3 * n + 2]]
            if phase < 2:
                add_sets(scatter_dims(piece, phase), self.results[n], terms)
                self.start(piece, phase + 1, 0)
                self.start(piece, phase + 1, 1)
            else:
                total = terms[0][...].astype(jnp.float32)
                for term in terms[1:]:
                    total = total + term[...].astype(jnp.float32)
                self.fin[piece.array][0, :, piece.cols] = total[:8]
                self.fin[piece.array][1, :, piece.cols] = total[8:]

    def drain(self):
        for copy in self.copies.values():
            copy.wait_send()


def scatter_dims(piece, phase):
    return set_dims(piece.order[: 2 - phase])


def landing_shapes(steps):
    return [
        pltpu.VMEM((*scatter_dims(piece, phase), 16, piece.width), jnp.bfloat16)
        for piece, phase in steps
        for _ in range(3)
    ]


def mid_shapes(steps):
    return [
        pltpu.VMEM((*scatter_dims(piece, phase), 16, piece.width), jnp.bfloat16)
        for piece, phase in steps
    ]


def grad_spot(grads, piece, offset):
    return grads[piece.array].at[
        (*chip_set(piece.order[:2], piece.order[2], offset), slice(None), piece.cols)
    ]


def columns(head):
    return pl.ds(pl.multiple_of(head * HEAD_DIM, HEAD_DIM), HEAD_DIM)


def exchange_start(moves, me, send, recv, local, first):
    copies = []
    for step in range(1, 8):
        there = (me + step) % 8
        for n, (source, target) in enumerate(moves):
            copy = pltpu.make_async_remote_copy(
                source(there), target(me), send.at[first + n, step], recv.at[first + n, step],
                device_id=sequence_chip(there),
            )
            copy.start()
            copies.append(copy)
    for n, (source, target) in enumerate(moves):
        copy = pltpu.make_async_copy(source(me), target(me), local.at[first + n])
        copy.start()
        copies.append(copy)
    return copies


def forward_kernel(*refs):
    gain_in, shards, (x_in, g_in, tab_in), refs = refs[0], list(refs[1:8]), refs[8:11], refs[11:]
    weights, (x_out, g_out, tab_out), refs = refs[:8], refs[8:11], refs[11:]
    q_out, k_out, v_out, o32_out, lse_ref, attended, normed_out, qpre_out, kpre_out, rows_ref = refs[:10]
    x_ref, tab, gains, wq, wk, wv, normed, qpre, kpre, q_low, k_low, v_low = refs[10:22]
    q_ref, k_ref, v_ref, o32_ref, o_low, scores, vt, gain_tile = refs[22:30]
    send, recv, head_send, head_recv, local, load, store, pair_send, pair_recv, pair_local = refs[30:]
    yh, z, x, yl, c = place()
    me = x * 2 + yl
    sib = sibling()
    tile_rows = jnp.concatenate([gain_in[...].astype(jnp.float32), jnp.zeros((TILE - 8, TILE), jnp.float32)])
    tile = tile_rows.T[:8].astype(jnp.bfloat16)
    gain_tile[0] = tile
    gain_tile[1] = tile
    shards.insert(NEAR - 1, gain_tile)
    greet(torus_neighbours() + sequence_others() + [sib])
    units = []
    for k in range(8):
        mine = weights[k].at[yh, z, x, yl, c]
        own = pltpu.make_async_copy(shards[k].at[c], mine, pair_local.at[k])
        away = pltpu.make_async_remote_copy(
            shards[k].at[1 - c], mine, pair_send.at[k], pair_recv.at[k], device_id=sib
        )
        units.append((own, away))
    for k, (source, target) in enumerate(((x_in, x_ref), (tab_in, tab), (g_in, g_out))):
        own = pltpu.make_async_copy(source, target.at[c], pair_local.at[8 + k])
        away = pltpu.make_async_remote_copy(
            source, target.at[c], pair_send.at[8 + k], pair_recv.at[8 + k], device_id=sib
        )
        units.append((own, away))
    for own, away in units:
        own.start()
        away.start()

    def met(some):
        for own, away in some:
            own.wait()
            away.wait_recv()

    near, far = flat_pieces(NEAR_PIECES), flat_pieces(FAR_PIECES)
    gather = Gather(weights, send, recv)

    def steps(pieces, first, phase):
        return [(first + phase * len(pieces) + n, piece, phase) for n, piece in enumerate(pieces)]

    near0, near1, near2 = (steps(near, 0, phase) for phase in range(3))
    far0, far1, far2 = (steps(far, 3 * len(near), phase) for phase in range(3))
    met(units[:NEAR])
    gather.begin(near0)
    met(units[NEAR:8])
    gather.begin(far0)
    gather.forward(near0)
    gather.advance(near0, near1)
    gather.forward(far0)
    gather.forward(near1)
    gather.advance(near1, near2)
    gather.advance(far0, far1)
    gather.forward(near2)
    gather.forward(far1)
    gather.arrive(near2)
    pieces_in = [(weights[3], gains), (weights[0], wq), (weights[1], wk), (weights[2], wv)]
    loads = load_all(pieces_in, load)
    gather.advance(far1[:2], far2[:2])
    gather.advance(far1[2:3], far2[2:3])
    gather.advance(far1[4:5], far2[4:5])
    met(units[8:])
    for copy in loads:
        copy.wait()

    gain_rows = gains[...].reshape(D, TILE).astype(jnp.float32).T[:8]
    pick = (
        lax.broadcasted_iota(jnp.int32, (D, HEAD_DIM), 0)
        == 8 * lax.broadcasted_iota(jnp.int32, (D, HEAD_DIM), 1)
    ).astype(jnp.bfloat16)
    head_gains = jnp.dot(gain_rows.astype(jnp.bfloat16), pick, preferred_element_type=jnp.float32)
    rows_ref[...] = gain_rows
    rows_ref[2:4, :HEAD_DIM] = head_gains[2:4]
    gain_q, gain_k = head_gains[2:3], head_gains[3:4]
    values = x_ref[...].reshape(BLOCK, D).astype(jnp.float32)
    normed[...] = (values * rms_scale(values) * gain_rows[0:1]).astype(jnp.bfloat16)
    cosine, sine = rope_pair(tab)

    def matrix(ref, at):
        value = ref[:, :, :, :, :, :, at]
        return value.reshape(D, value.shape[-1])

    def head(pre, gain):
        unit = pre * rms_scale(pre) * gain
        return (unit * cosine + pltpu.roll(unit, HEAD_DIM // 2, 1) * sine).astype(jnp.bfloat16)

    for weight, pre_ref, low_ref, gain in ((wq, qpre, q_low, gain_q), (wk, kpre, k_low, gain_k)):
        for n in range(weight.shape[-1] // 256):
            at = slice(n * 256, n * 256 + 256)
            pre = jnp.dot(normed[...], matrix(weight, at), preferred_element_type=jnp.float32)
            pre_ref[:, at] = pre
            low_ref[:, n * 256 : n * 256 + 128] = head(pre[:, :128], gain)
            low_ref[:, n * 256 + 128 : n * 256 + 256] = head(pre[:, 128:], gain)
    v_low[...] = jnp.dot(normed[...], matrix(wv, slice(None)), preferred_element_type=jnp.float32).astype(jnp.bfloat16)
    arriving = exchange_start(
        [
            (lambda j: q_low.at[:, columns(j)], lambda i: q_ref.at[i]),
            (lambda j: k_low.at[:, columns(j // 2)], lambda i: k_ref.at[i]),
            (lambda j: v_low.at[:, columns(j // 2)], lambda i: v_ref.at[i]),
        ],
        me, head_send, head_recv, local, 0,
    )
    stores = [
        pltpu.make_async_copy(a, b, store.at[n])
        for n, (a, b) in enumerate(
            ((normed, normed_out), (qpre, qpre_out), (kpre, kpre_out), (q_ref, q_out), (k_ref, k_out),
             (v_ref, v_out), (o32_ref, o32_out), (x_ref, x_out), (tab, tab_out))
        )
    ]
    for copy in stores[:3] + stores[7:]:
        copy.start()
    for copy in arriving:
        copy.wait()
    gather.advance(far1[3:4], far2[3:4])
    gather.advance(far1[5:6], far2[5:6])
    gather.advance(far1[6:7], far2[6:7])
    gather.advance(far1[7:8], far2[7:8])
    gather.forward(far2[:2])
    for copy in stores[3:6]:
        copy.start()
    for j in range(8):
        vt[j] = v_ref[j].T

    def one_block(i, _):
        q = q_ref[i]

        def score(j, top):
            s = nt(k_ref[j], q) * (score_scale * log2e)
            scores[j] = s
            return jnp.maximum(top, jnp.max(s, axis=0, keepdims=True))

        top = lax.fori_loop(0, i + 1, score, jnp.full((1, BLOCK), -1e30, jnp.float32))

        def weigh(j, carry):
            total, mixed = carry
            p = jnp.exp2(scores[j] - top)
            total = total + jnp.sum(p, axis=0, keepdims=True)
            mixed = mixed + jnp.dot(vt[j], p.astype(jnp.bfloat16), preferred_element_type=jnp.float32)
            return total, mixed

        total, mixed = lax.fori_loop(
            0, i + 1, weigh,
            (jnp.zeros((1, BLOCK), jnp.float32), jnp.zeros((HEAD_DIM, BLOCK), jnp.float32)),
        )
        out = (mixed / total).T
        o32_ref[i] = out
        o_low[i] = out.astype(jnp.bfloat16)
        lse_ref[i] = top + jnp.log2(total)
        return 0

    lax.fori_loop(0, 6, one_block, 0)
    gather.forward(far2[2:])
    lax.fori_loop(6, 8, one_block, 0)
    leaving = exchange_start(
        [(lambda j: o_low.at[j], lambda i: attended.at[:, columns(i)])],
        me, head_send, head_recv, local, 3,
    )
    stores[6].start()
    gather.arrive(far2)
    gather.drain()
    for copy in stores:
        copy.wait()
    for copy in leaving:
        copy.wait()
    for _, away in units:
        away.wait_send()


def attend(gain_rows, shards, pairs):
    blocks = (8, BLOCK, HEAD_DIM)
    count = 3 * (len(flat_pieces(NEAR_PIECES)) + len(flat_pieces(FAR_PIECES)))
    low, wide = jnp.bfloat16, jnp.float32
    widths = [w.shape[-1] for w in shards]
    widths.insert(NEAR - 1, TILE)
    whole = [(2, 4, 4, 2, 2, 8, w) for w in widths]
    return pl.pallas_call(
        forward_kernel,
        out_shape=[jax.ShapeDtypeStruct(w, low) for w in whole]
        + [jax.ShapeDtypeStruct((2, *p.shape), p.dtype) for p in pairs]
        + [jax.ShapeDtypeStruct(blocks, low)] * 3
        + [
            jax.ShapeDtypeStruct(blocks, wide),
            jax.ShapeDtypeStruct((8, 1, BLOCK), wide),
            jax.ShapeDtypeStruct((BLOCK, 1024), low),
            jax.ShapeDtypeStruct((BLOCK, D), low),
            jax.ShapeDtypeStruct((BLOCK, 1024), wide),
            jax.ShapeDtypeStruct((BLOCK, 512), wide),
            jax.ShapeDtypeStruct((8, D), wide),
        ],
        in_specs=[VMEM] * 11,
        out_specs=[HBM] * 15 + [VMEM] + [HBM] * 4 + [VMEM],
        scratch_shapes=[
            pltpu.VMEM((2, 128, D), low),
            pltpu.VMEM((2, 128, HEAD_DIM), wide),
            pltpu.VMEM(whole[3], low),
            pltpu.VMEM(whole[0], low),
            pltpu.VMEM(whole[1], low),
            pltpu.VMEM(whole[2], low),
            pltpu.VMEM((BLOCK, D), low),
            pltpu.VMEM((BLOCK, 1024), wide),
            pltpu.VMEM((BLOCK, 512), wide),
            pltpu.VMEM((BLOCK, 1024), low),
            pltpu.VMEM((BLOCK, 512), low),
            pltpu.VMEM((BLOCK, 512), low),
        ]
        + [pltpu.VMEM(blocks, low)] * 3
        + [
            pltpu.VMEM(blocks, wide),
            pltpu.VMEM(blocks, low),
            pltpu.VMEM((8, BLOCK, BLOCK), wide),
            pltpu.VMEM((8, HEAD_DIM, BLOCK), low),
            pltpu.VMEM((2, 8, TILE), low),
            pltpu.SemaphoreType.DMA((count, 3)),
            pltpu.SemaphoreType.DMA((count, 3)),
            pltpu.SemaphoreType.DMA((4, 8)),
            pltpu.SemaphoreType.DMA((4, 8)),
            pltpu.SemaphoreType.DMA((4,)),
            pltpu.SemaphoreType.DMA((4,)),
            pltpu.SemaphoreType.DMA((9,)),
            pltpu.SemaphoreType.DMA((11,)),
            pltpu.SemaphoreType.DMA((11,)),
            pltpu.SemaphoreType.DMA((11,)),
        ],
        compiler_params=pltpu.CompilerParams(
            collective_id=2, has_side_effects=True, vmem_limit_bytes=LIMIT
        ),
        name="attend",
    )(gain_rows, *shards, *pairs)


LAST_WIDTHS = (1024, 512, 512, 1024, 1536, 1536, 1536)


def scatter_steps():
    pieces = flat_pieces(NEAR_PIECES) + flat_pieces(FAR_PIECES)
    return [(piece, phase) for piece in pieces for phase in range(3)]


def backward_kernel(*refs):
    near, far = flat_pieces(NEAR_PIECES), flat_pieces(FAR_PIECES)
    n_w, steps = len(LAST_WIDTHS), scatter_steps()
    n_steps = len(steps)
    ins, far_grads, do_in, refs = refs[:16], refs[16:20], refs[20], refs[21:]
    outs, refs = refs[:n_w], refs[n_w:]
    in_gain_out, post_gain_out, q_gain_out, k_gain_out, input_grad = refs[:5]
    held, refs = refs[5:21], refs[21:]
    q_ref, k_ref, v_ref, o32_ref, lse_ref, qpre, kpre, normed, tab, rows, x_ref = held[:11]
    wq, wk, wv, gmid, post = held[11:]
    do_ref, dq_low, dk_low, dv_low, kt, dk_acc, dv_acc = refs[:7]
    gq, kparts, vparts, dq, dk, dv, normed_t, pair_out, pair_in, gain_got = refs[7:17]
    refs = refs[17:]
    grads, refs = refs[:NEAR], refs[NEAR:]
    fin, refs = refs[: n_w + 1], refs[n_w + 1 :]
    landing, refs = refs[: 3 * n_steps], refs[3 * n_steps :]
    mids, refs = refs[:n_steps], refs[n_steps:]
    results, refs = refs[:n_steps], refs[n_steps:]
    send, recv, pair_send, pair_recv, local, load, far_load, head_send, head_recv, head_local = refs
    yh, z, x, yl, c = place()
    me = x * 2 + yl
    sib = sibling()
    scatter = Scatter(steps, list(grads) + list(far_grads), landing, mids, results, fin, send, recv)
    loads = load_all(list(zip(ins, held)), load)
    for n, piece in enumerate(far):
        scatter.load(piece, far_load.at[n])
    greet(torus_neighbours() + sequence_others() + [sib])
    arriving = exchange_start(
        [(lambda j: do_in.at[:, columns(j)], lambda i: do_ref.at[i])],
        me, head_send, head_recv, head_local, 0,
    )
    scatter.begin(far[:2], 0)
    scatter.begin(far[2:], 0)
    for copy in loads[:5]:
        copy.wait()
    for j in range(8):
        kt[j] = k_ref[j].T
    dk_acc[...] = jnp.zeros_like(dk_acc)
    dv_acc[...] = jnp.zeros_like(dv_acc)
    for copy in arriving:
        copy.wait()

    def one_block(i, _):
        q, do, lse = q_ref[i], do_ref[i], lse_ref[i]
        delta = jnp.sum((do.astype(jnp.float32) * o32_ref[i]).T, axis=0, keepdims=True)

        def one_pair(j, dqt):
            p = jnp.exp2(nt(k_ref[j], q) * (score_scale * log2e) - lse)
            dp = nt(v_ref[j], do)
            ds = (p * (dp - delta)).astype(jnp.bfloat16)
            dv_acc[j] += jnp.dot(p.astype(jnp.bfloat16), do, preferred_element_type=jnp.float32)
            dk_acc[j] += jnp.dot(ds, q, preferred_element_type=jnp.float32)
            return dqt + jnp.dot(kt[j], ds, preferred_element_type=jnp.float32)

        dqt = lax.fori_loop(0, i + 1, one_pair, jnp.zeros((HEAD_DIM, BLOCK), jnp.float32))
        dq_low[i] = (dqt * score_scale).T.astype(jnp.bfloat16)
        return 0

    lax.fori_loop(0, 6, one_block, 0)
    scatter.middle(far[:2], 0)
    scatter.middle(far[2:], 0)
    lax.fori_loop(6, 8, one_block, 0)
    dk_low[...] = (dk_acc[...] * score_scale).astype(jnp.bfloat16)
    dv_low[...] = dv_acc[...].astype(jnp.bfloat16)
    arriving = exchange_start(
        [
            (lambda j: dq_low.at[j], lambda i: gq.at[:, columns(i)]),
            (lambda j: dk_low.at[j], lambda i: kparts.at[i % 2, :, columns(i // 2)]),
            (lambda j: dv_low.at[j], lambda i: vparts.at[i % 2, :, columns(i // 2)]),
        ],
        me, head_send, head_recv, head_local, 1,
    )
    scatter.end(far[:2], 0)
    scatter.end(far[2:], 0)
    for copy in loads[5:]:
        copy.wait()
    normed_t[...] = normed[...].T
    for copy in arriving:
        copy.wait()
    cosine, sine = rope_pair(tab)
    gain_q, gain_k = rows[2:3, :HEAD_DIM], rows[3:4, :HEAD_DIM]

    def head_back(grad, values, gain):
        grad = grad * cosine - pltpu.roll(grad, HEAD_DIM // 2, 1) * sine
        grad_in, terms = norm_back(grad, values, rms_scale(values), gain)
        return grad_in.astype(jnp.bfloat16), jnp.sum(terms, axis=0, keepdims=True)

    q_part = jnp.zeros((1, HEAD_DIM), jnp.float32)
    k_part = jnp.zeros((1, HEAD_DIM), jnp.float32)
    for h in range(8):
        at = slice(h * HEAD_DIM, (h + 1) * HEAD_DIM)
        dq[:, at], part = head_back(gq[:, at].astype(jnp.float32), qpre[:, at], gain_q)
        q_part = q_part + part
    for h in range(4):
        at = slice(h * HEAD_DIM, (h + 1) * HEAD_DIM)
        grad = kparts[0, :, at].astype(jnp.float32) + kparts[1, :, at].astype(jnp.float32)
        dk[:, at], part = head_back(grad, kpre[:, at], gain_k)
        k_part = k_part + part
    dv[...] = (vparts[0].astype(jnp.float32) + vparts[1].astype(jnp.float32)).astype(jnp.bfloat16)

    def weight_grads(n, _):
        lhs = normed_t[pl.ds(pl.multiple_of(n * 256, 256), 256), :]
        for grad, factor in ((grads[0], dq), (grads[1], dk), (grads[2], dv)):
            width = factor.shape[1]
            block = jnp.dot(lhs, factor[...], preferred_element_type=jnp.float32)
            grad[n // 2, pl.ds(n % 2 * 2, 2)] = block.astype(jnp.bfloat16).reshape(2, 4, 2, 16, width)
        return 0

    lax.fori_loop(0, 4, weight_grads, 0)
    weights = [piece for piece in near if piece.array != NEAR - 1]
    gains = [piece for piece in near if piece.array == NEAR - 1]
    scatter.begin(weights, 0)

    def grad_normed(rows_at):
        return (
            nt(dq[rows_at, :], wq[...]) + nt(dk[rows_at, :], wk[...]) + nt(dv[rows_at, :], wv[...])
        )

    away = pl.ds(pl.multiple_of((1 - c) * 128, 128), 128)
    own = pl.ds(pl.multiple_of(c * 128, 128), 128)
    pair_out[...] = grad_normed(away).astype(jnp.bfloat16)
    swap = pltpu.make_async_remote_copy(
        pair_out, pair_in, pair_send.at[n_w + 1], pair_recv.at[n_w + 1], device_id=sib
    )
    swap.start()
    grad = grad_normed(own)
    values = x_ref[c].astype(jnp.float32)
    swap.wait_recv()
    grad = grad + pair_in[...].astype(jnp.float32)
    grad_in, terms = norm_back(grad, values, rms_scale(values), rows[0:1, :])
    input_grad[...] = (gmid[...] + grad_in).astype(jnp.bfloat16)
    in_part = jnp.sum(terms, axis=0, keepdims=True)
    spread = (
        lax.broadcasted_iota(jnp.int32, (HEAD_DIM, D), 1)
        == 8 * lax.broadcasted_iota(jnp.int32, (HEAD_DIM, D), 0)
    ).astype(jnp.bfloat16)
    qk = jnp.concatenate([q_part, k_part, jnp.zeros((6, HEAD_DIM), jnp.float32)]).astype(jnp.bfloat16)
    qk = jnp.dot(qk, spread, preferred_element_type=jnp.float32)
    gain_rows = jnp.concatenate(
        [in_part, post[0:1, :], qk[0:2], jnp.zeros((TILE - 4, D), jnp.float32)]
    )
    grads[NEAR - 1][...] = gain_rows.T.astype(jnp.bfloat16).reshape(2, 4, 4, 2, 16, TILE)
    scatter.begin(gains, 0)

    copies = []

    def deliver(k):
        if k == NEAR - 1:
            target = gain_got
        else:
            out = outs[k if k < NEAR else k - 1]
            width = out.shape[1] // 2
            target = out.at[:, pl.ds(pl.multiple_of(c * width, TILE), width)]
            keep = pltpu.make_async_copy(fin[k].at[c], target, local.at[k])
            keep.start()
            copies.append(keep)
        away_k = pltpu.make_async_remote_copy(
            fin[k].at[1 - c], target, pair_send.at[k], pair_recv.at[k], device_id=sib
        )
        away_k.start()
        copies.append(away_k)

    near = weights + gains
    scatter.middle(near, 0)
    scatter.middle(far, 1)
    scatter.end(near, 0)
    scatter.end(far, 1)
    scatter.middle(near, 1)
    scatter.middle(far, 2)
    scatter.end(near, 1)
    scatter.middle(near, 2)
    scatter.end(far, 2)
    for k in range(NEAR, 8):
        deliver(k)
    scatter.end(near, 2)
    for k in range(NEAR):
        deliver(k)
    scatter.drain()
    swap.wait_send()
    for copy in copies:
        copy.wait()
    gain_sum = fin[NEAR - 1][c] + gain_got[...]
    gain_rows = jnp.concatenate([gain_sum, jnp.zeros((TILE - 8, TILE), jnp.float32)]).T
    in_gain_out[...] = gain_rows[0:1, :8]
    post_gain_out[...] = gain_rows[1:2, :8]
    q_gain_out[...] = gain_rows[2:3, :1]
    k_gain_out[...] = gain_rows[3:4, :1]


def attend_back(arrays, far_grads, grad_att):
    steps = scatter_steps()
    blocks = (8, BLOCK, HEAD_DIM)
    low, wide = jnp.bfloat16, jnp.float32
    n_w = len(LAST_WIDTHS)
    fin_widths = list(LAST_WIDTHS)
    fin_widths.insert(NEAR - 1, TILE)
    far = flat_pieces(FAR_PIECES)
    return pl.pallas_call(
        backward_kernel,
        out_shape=[jax.ShapeDtypeStruct((8, 2 * w), wide) for w in LAST_WIDTHS]
        + [jax.ShapeDtypeStruct((1, n), wide) for n in (8, 8, 1, 1)]
        + [jax.ShapeDtypeStruct((128, D), low)],
        in_specs=[HBM] * (len(arrays) + 5),
        out_specs=[HBM] * n_w + [VMEM] * 5,
        scratch_shapes=[pltpu.VMEM(a.shape, a.dtype) for a in arrays]
        + [pltpu.VMEM(blocks, low)] * 4
        + [
            pltpu.VMEM((8, HEAD_DIM, BLOCK), low),
            pltpu.VMEM(blocks, wide),
            pltpu.VMEM(blocks, wide),
            pltpu.VMEM((BLOCK, 1024), low),
            pltpu.VMEM((2, BLOCK, 512), low),
            pltpu.VMEM((2, BLOCK, 512), low),
            pltpu.VMEM((BLOCK, 1024), low),
            pltpu.VMEM((BLOCK, 512), low),
            pltpu.VMEM((BLOCK, 512), low),
            pltpu.VMEM((D, BLOCK), low),
            pltpu.VMEM((128, D), low),
            pltpu.VMEM((128, D), low),
            pltpu.VMEM((8, TILE), wide),
        ]
        + [pltpu.VMEM((2, 4, 4, 2, 16, w), low) for w in fin_widths[:NEAR]]
        + [pltpu.VMEM((2, 8, w), wide) for w in fin_widths]
        + landing_shapes(steps)
        + mid_shapes(steps)
        + mid_shapes(steps)
        + [
            pltpu.SemaphoreType.DMA((len(steps), 3)),
            pltpu.SemaphoreType.DMA((len(steps), 3)),
            pltpu.SemaphoreType.DMA((n_w + 2,)),
            pltpu.SemaphoreType.DMA((n_w + 2,)),
            pltpu.SemaphoreType.DMA((n_w + 1,)),
            pltpu.SemaphoreType.DMA((len(arrays),)),
            pltpu.SemaphoreType.DMA((len(far), 2)),
            pltpu.SemaphoreType.DMA((4, 8)),
            pltpu.SemaphoreType.DMA((4, 8)),
            pltpu.SemaphoreType.DMA((4,)),
        ],
        compiler_params=pltpu.CompilerParams(
            collective_id=3, has_side_effects=True, vmem_limit_bytes=LIMIT
        ),
        name="attend_back",
    )(*arrays, *far_grads, grad_att)


def middle_kernel(*refs):
    att_in, x_in, g_in, rows_in, wo_in, wg_in, wu_in, wd_in = refs[:8]
    output, grad_att_out, gmid_out, post_out = refs[8:12]
    dwo_out, dwg_out, dwu_out, dwd_out = refs[12:16]
    att, x_ref, g_ref, rows, wo, wg, wu, wd = refs[16:24]
    (branch, middle, hidden, hidden_t, g_t, grad_act, act, gate_grad, up_grad, grad_hidden, branch_t,
     down_own, grad_att, dwo, dwg, dwu, dwd) = refs[24:41]
    out1, in1, out2, in2, out3, in3 = refs[41:47]
    pair_send, pair_recv, load, store = refs[47:]
    yh, z, x, yl, c = place()
    sib = sibling()
    loads = load_all(
        [(att_in, att), (wo_in, wo), (g_in, g_ref), (wd_in, wd), (x_in, x_ref), (rows_in, rows),
         (wg_in, wg), (wu_in, wu)], load
    )
    greet([sib])
    swaps = []

    def swap(source, target):
        n = len(swaps)
        copy = pltpu.make_async_remote_copy(
            source, target, pair_send.at[n], pair_recv.at[n], device_id=sib
        )
        copy.start()
        swaps.append(copy)
        return copy

    def part(n, width=256):
        return pl.ds(n * width, width)

    loads[0].wait()
    loads[1].wait()
    first = []
    for n in range(4):
        block = nt(att[...], wo[part(n), :])
        branch[:, part(n)] = block
        out1[n] = block.astype(jnp.bfloat16)
        first.append(swap(out1.at[n], in1.at[n]))
    loads[2].wait()
    loads[3].wait()
    g_low = g_ref[...].reshape(BLOCK, D)
    for n in range(6):
        grad_act[:, part(n)] = jnp.dot(g_low, wd[:, part(n)], preferred_element_type=jnp.float32)
    g_t[...] = g_low.T
    loads[4].wait()
    loads[5].wait()
    for n in range(4):
        first[n].wait_recv()
        middle[:, part(n)] = (
            x_ref[...].reshape(BLOCK, D)[:, n * 256 : n * 256 + 256].astype(jnp.float32)
            + (branch[:, part(n)] + in1[n].astype(jnp.float32))
        )
    gain = rows[1:2, :]
    scale = rms_scale(middle[...])
    hidden[...] = (middle[...] * scale * gain).astype(jnp.bfloat16)
    loads[6].wait()
    loads[7].wait()
    for n in range(6):
        gate = jnp.dot(hidden[...], wg[:, part(n)], preferred_element_type=jnp.float32)
        up = jnp.dot(hidden[...], wu[:, part(n)], preferred_element_type=jnp.float32)
        sigma = jax.nn.sigmoid(gate)
        swish = gate * sigma
        grad = grad_act[:, part(n)]
        act[:, part(n)] = (swish * up).astype(jnp.bfloat16)
        gate_grad[:, part(n)] = (grad * up * (sigma * (1.0 + gate * (1.0 - sigma)))).astype(jnp.bfloat16)
        up_grad[:, part(n)] = (grad * swish).astype(jnp.bfloat16)
    second = []
    for n in range(4):
        block = nt(gate_grad[...], wg[part(n), :]) + nt(up_grad[...], wu[part(n), :])
        grad_hidden[:, part(n)] = block
        out2[n] = block.astype(jnp.bfloat16)
        second.append(swap(out2.at[n], in2.at[n]))
    away = pl.ds(pl.multiple_of((1 - c) * 128, 128), 128)
    own = pl.ds(pl.multiple_of(c * 128, 128), 128)
    out3[...] = nt(act[away, :], wd[...]).astype(jnp.bfloat16)
    third = swap(out3, in3)
    down_own[...] = nt(act[own, :], wd[...])
    hidden_t[...] = hidden[...].T
    stores = []

    def keep(source, target):
        copy = pltpu.make_async_copy(source, target, store.at[len(stores)])
        copy.start()
        stores.append(copy)

    for lhs, rhs, grads, target in (
        (hidden_t, gate_grad, dwg, dwg_out), (hidden_t, up_grad, dwu, dwu_out), (g_t, act, dwd, dwd_out)
    ):
        for n in range(4):
            grads[part(n), :] = jnp.dot(
                lhs[part(n), :], rhs[...], preferred_element_type=jnp.float32
            ).astype(jnp.bfloat16)
        keep(grads, target)
    for n in range(4):
        second[n].wait_recv()
        grad_hidden[:, part(n)] = grad_hidden[:, part(n)] + in2[n].astype(jnp.float32)
    grad_in, terms = norm_back(grad_hidden[...], middle[...], scale, gain)
    grad_hidden[...] = terms
    post_out[...] = jnp.broadcast_to(jnp.sum(grad_hidden[own, :], axis=0, keepdims=True), (8, D))
    grad_hidden[...] = g_low.astype(jnp.float32) + grad_in
    gmid_out[...] = grad_hidden[own, :]
    branch_grad = grad_hidden[...].astype(jnp.bfloat16)
    branch_t[...] = branch_grad.T
    for n in range(4):
        grad_att[:, part(n)] = jnp.dot(
            branch_grad, wo[:, part(n)], preferred_element_type=jnp.float32
        ).astype(jnp.bfloat16)
    keep(grad_att, grad_att_out)
    for n in range(4):
        dwo[part(n), :] = jnp.dot(
            branch_t[part(n), :], att[...], preferred_element_type=jnp.float32
        ).astype(jnp.bfloat16)
    keep(dwo, dwo_out)
    third.wait_recv()
    output[...] = (
        middle[own, :] + (down_own[...] + in3[...].astype(jnp.float32))
    ).astype(jnp.bfloat16)
    for copy in swaps:
        copy.wait_send()
    for copy in stores:
        copy.wait()


def feed_forward(arrays):
    low, wide = jnp.bfloat16, jnp.float32
    shapes = [(D, 1024), (D, 1536), (D, 1536), (D, 1536)]
    return pl.pallas_call(
        middle_kernel,
        out_shape=[
            jax.ShapeDtypeStruct((128, D), low),
            jax.ShapeDtypeStruct((BLOCK, 1024), low),
            jax.ShapeDtypeStruct((128, D), wide),
            jax.ShapeDtypeStruct((8, D), wide),
        ]
        + [jax.ShapeDtypeStruct(s, low) for s in shapes],
        in_specs=[HBM] * 8,
        out_specs=[VMEM, HBM, VMEM, VMEM] + [HBM] * 4,
        scratch_shapes=[pltpu.VMEM(a.shape, a.dtype) for a in arrays]
        + [
            pltpu.VMEM((BLOCK, D), wide),
            pltpu.VMEM((BLOCK, D), wide),
            pltpu.VMEM((BLOCK, D), low),
            pltpu.VMEM((D, BLOCK), low),
            pltpu.VMEM((D, BLOCK), low),
            pltpu.VMEM((BLOCK, 1536), wide),
            pltpu.VMEM((BLOCK, 1536), low),
            pltpu.VMEM((BLOCK, 1536), low),
            pltpu.VMEM((BLOCK, 1536), low),
            pltpu.VMEM((BLOCK, D), wide),
            pltpu.VMEM((D, BLOCK), low),
            pltpu.VMEM((128, D), wide),
            pltpu.VMEM((BLOCK, 1024), low),
        ]
        + [pltpu.VMEM(s, low) for s in shapes]
        + [pltpu.VMEM((4, BLOCK, 256), low)] * 4
        + [pltpu.VMEM((128, D), low)] * 2
        + [
            pltpu.SemaphoreType.DMA((9,)),
            pltpu.SemaphoreType.DMA((9,)),
            pltpu.SemaphoreType.DMA((8,)),
            pltpu.SemaphoreType.DMA((5,)),
        ],
        compiler_params=pltpu.CompilerParams(
            collective_id=4, has_side_effects=True, vmem_limit_bytes=LIMIT
        ),
        name="feed_forward",
    )(*arrays)


def results_kernel(n, *refs):
    for source, target in zip(refs[:n], refs[n:]):
        target[...] = source[...]


def results(arrays):
    n = len(arrays)
    return pl.pallas_call(
        functools.partial(results_kernel, n),
        out_shape=[jax.ShapeDtypeStruct(a.shape, a.dtype) for a in arrays],
        in_specs=[VMEM] * n,
        out_specs=[VMEM] * n,
        name="results",
    )(*arrays)


def split_columns(shard):
    rows, width = shard.shape
    return jnp.transpose(shard.reshape(rows, CORES, width // CORES), (1, 0, 2))


def body(
    tokens,
    positions,
    in_gain,
    q_gain,
    k_gain,
    w_query,
    w_key,
    w_value,
    w_out,
    post_gain,
    w_gate,
    w_up,
    w_down,
    cotangent,
):
    half = HEAD_DIM // 2
    frequency = rope_base ** (-2.0 * jnp.arange(half, dtype=jnp.float32) / HEAD_DIM)
    angles = positions[0].astype(jnp.float32)[:, None] * frequency[None, :]
    table = jnp.concatenate([jnp.cos(angles), jnp.sin(angles)], axis=-1)
    gain_rows = jnp.stack(
        [jnp.pad(g, (0, TILE - g.shape[0])) for g in (in_gain, post_gain, q_gain, k_gain)]
    )
    gain_rows = jnp.pad(gain_rows, ((0, 4), (0, 0)))
    shards = [
        split_columns(w) for w in (w_query, w_key, w_value, w_out.T, w_gate, w_up, w_down.T)
    ]
    *gathered, x_pair, g_pair, tables, q_all, k_all, v_all, mixed, log_total, attended, normed, q_pre, k_pre, rows = attend(
        gain_rows, shards, [tokens[0], cotangent[0], table]
    )
    wq, wk, wv, _, wo, wg, wu, wd = [w.reshape(D, w.shape[-1]) for w in gathered]
    output, grad_att, grad_middle, post_part, *far_grads = feed_forward(
        [attended, x_pair, g_pair, rows, wo, wg, wu, wd]
    )
    last = attend_back(
        [q_all, k_all, v_all, mixed, log_total, q_pre, k_pre, normed, tables, rows, x_pair, wq, wk, wv,
         grad_middle, post_part],
        [g.reshape(2, 4, 4, 2, 16, g.shape[-1]) for g in far_grads],
        grad_att,
    )
    *sums, in_gain_grad, post_gain_grad, q_gain_grad, k_gain_grad, input_grad, output = results(
        [*last, output]
    )
    return (
        output[None],
        input_grad[None],
        in_gain_grad[0],
        q_gain_grad[0],
        k_gain_grad[0],
        sums[0],
        sums[1],
        sums[2],
        sums[3].T,
        post_gain_grad[0],
        sums[4],
        sums[5],
        sums[6].T,
    )


def solution(mesh):
    placed = (
        P("dp", "seq", None),
        P("dp", "seq"),
        P(("dp", "seq")),
        P(("dp", "seq")),
        P(("dp", "seq")),
        P(("dp", "seq"), None),
        P(("dp", "seq"), None),
        P(("dp", "seq"), None),
        P(None, ("dp", "seq")),
        P(("dp", "seq")),
        P(("dp", "seq"), None),
        P(("dp", "seq"), None),
        P(None, ("dp", "seq")),
        P("dp", "seq", None),
    )
    return jax.shard_map(
        body,
        mesh=mesh,
        in_specs=placed,
        out_specs=(
            P("dp", "seq", None),
            P("dp", "seq", None),
            P(("dp", "seq")),
            P(("dp", "seq")),
            P(("dp", "seq")),
            P(("dp", "seq"), None),
            P(("dp", "seq"), None),
            P(("dp", "seq"), None),
            P(None, ("dp", "seq")),
            P(("dp", "seq")),
            P(("dp", "seq"), None),
            P(("dp", "seq"), None),
            P(None, ("dp", "seq")),
        ),
        check_vma=False,
    )
```

time: 263 us -> 231 us (0.88)
  Pallas kernels: 257 us -> 226 us
    pallas_call x4 -> x2, Pallas kernels: 229 us -> 197 us  [the longest x1 99.8 us: attend_back(): pl.pallas_call(backward_kernel, out_shape=[jax.ShapeDtypeStruct((8, 2 * w...]
where the time goes in v4:
time: 231 us
  Pallas kernels  226 us (98%)
    pallas_call x1, Pallas kernels, attend_back(): pl.pallas_call(backward_kernel, out_shape=[jax.ShapeDtypeStruct((8, 2 * w...  99.8 us
    pallas_call x1, Pallas kernels, attend(): pl.pallas_call(forward_kernel, out_shape=[jax.ShapeDtypeStruct(w, low) fo...  97.2 us
    pallas_call x1, Pallas kernels, feed_forward(): pl.pallas_call(middle_kernel, out_shape=[jax.ShapeDtypeStruct((128, D), l...  25.5 us

profile of v4, /device:TPU:1, one launch (start us, length us, event | category | flops | bytes accessed | tf_op | source)
XLA Modules:
  0.0 231.1 jit_solution(9361372217520074543)
XLA Ops:
  2.0 0.7 convert_bitcast_fusion
  2.6 0.7 pad_bitcast_fusion.2
  3.3 0.6 fusion.6.refs_0_
  3.9 0.3 multiply_cosine_fusion
  4.2 0.7 pad_maximum_fusion.refs_10_
  4.9 97.2 %attend.1 = (bf16[2,4,4,2,2,8,1024]{6,5,4,3,2,1,0:T(8,128)(2,1)}, bf16[2,4,4,2,2,8,512]{6,5,4,3,2,1,0:T(8,128)(2,1)}, bf16[2,4,4,2,2,8,512]{6,5,4,3,2,1,0:T(8,12...) custom-call(bf16[8,128]{1,0:T(8,128)(2,1)} %fusion.6.refs_0_, ...), custom_call_target="tpu_custom_call" | custom-call | tf_op jit(solution)/shard_map/attend/pallas_call | solution.py:562
  102.1 25.5 %feed_forward.1 = (bf16[128,1024]{1,0:T(8,128)(2,1)}, bf16[256,1024]{1,0:T(8,128)(2,1)}, f32[128,1024]{1,0:T(8,128)}, f32[8,1024]{1,0:T(8,128)}, bf16[1024,1024]...) custom-call(bf16[256,1024]{1,0:T(8,128)(2,1)} %get-tuple-element.80.refs_0_, ...), custom_call_target="tpu_custom_call" | custom-call | tf_op jit(solution)/shard_map/feed_forward/pallas_call | solution.py:996
  127.7 99.8 %attend_back.1 = (f32[8,2048]{1,0:T(8,128)}, f32[8,1024]{1,0:T(8,128)}, f32[8,1024]{1,0:T(8,128)}, f32[8,2048]{1,0:T(8,128)}, f32[8,3072]{1,0:T(8,128)}, /*index...) custom-call(bf16[8,256,128]{2,1,0:T(8,128)(2,1)} %get-tuple-element., ...), custom_call_target="tpu_custom_call" | custom-call | tf_op jit(solution)/shard_map/attend_back/pallas_call | solution.py:822
  227.5 3.6 %results.1 = (f32[8,2048]{1,0:T(8,128)}, f32[8,1024]{1,0:T(8,128)}, f32[8,1024]{1,0:T(8,128)}, f32[8,2048]{1,0:T(8,128)}, f32[8,3072]{1,0:T(8,128)}, /*index=5*/...) custom-call(f32[8,2048]{1,0:T(8,128)} %get-tuple-element.93.refs_0_,, ...), custom_call_target="tpu_custom_call" | custom-call | tf_op jit(solution)/shard_map/results/pallas_call | solution.py:1046
  (2 shorter events, 0.0 us)

commit v5 on v4

v5 whole, which is shorter than its diff:
```python
import functools
import math

import jax
import jax.numpy as jnp
from jax import lax
from jax.experimental import pallas as pl
from jax.experimental.pallas import tpu as pltpu
from jax.sharding import PartitionSpec as P

HEADS = 16
KV_HEADS = 8
HEAD_DIM = 128
D = 1024
FF = 3072
BLOCK = 256
CORES = 2

TILE = 128

eps_norm = 1e-06
rope_base = 1000000.0
score_scale = 1.0 / math.sqrt(HEAD_DIM)
log2e = math.log2(math.e)


def place():
    dp = lax.axis_index("dp")
    seq = lax.axis_index("seq")
    return dp // 4, dp % 4, seq // 4, (seq // 2) % 2, seq % 2


def device(yh, z, x, yl, c):
    return {"dp": yh * 4 + z, "seq": x * 4 + yl * 2 + c}


def sibling():
    yh, z, x, yl, c = place()
    return device(yh, z, x, yl, 1 - c)


def neighbour(axis, step):
    yh, z, x, yl, c = place()
    if axis == "x":
        return device(yh, z, (x + step + 4) % 4, yl, c)
    if axis == "z":
        return device(yh, (z + step + 4) % 4, x, yl, c)
    y = (yh * 2 + yl + step + 4) % 4
    return device(y // 2, z, x, y % 2, c)


ORDERS = (("x", "y", "z"), ("y", "z", "x"), ("z", "x", "y"))


def chip_set(whole_axes, axis, step):
    yh, z, x, yl, _ = place()
    iz, ix, iyh, iyl = z, x, yh, yl
    if axis == "x":
        ix = (x + step + 4) % 4
    elif axis == "z":
        iz = (z + step + 4) % 4
    else:
        y = (yh * 2 + yl + step + 4) % 4
        iyh, iyl = y // 2, y % 2
    every = slice(None)
    if "x" in whole_axes:
        ix = every
    if "z" in whole_axes:
        iz = every
    if "y" in whole_axes:
        iyh, iyl = every, every
    return (iyh, iz, ix, iyl)


def set_dims(whole_axes):
    dims = ()
    if "y" in whole_axes:
        dims += (2,)
    if "z" in whole_axes:
        dims += (4,)
    if "x" in whole_axes:
        dims += (4,)
    if "y" in whole_axes:
        dims += (2,)
    return dims


NEAR, FAR = 0, 1
WIDE = (2176, 5632)
LIMIT = 60 << 20


class Part:
    def __init__(self, array, number, order, first, tiles):
        self.array, self.number, self.order = array, number, order
        self.start, self.width = first * TILE, tiles * TILE
        self.cols = pl.ds(self.start, self.width)
        cut = (tiles + 1) // 2 * TILE
        self.halves = ((0, 1, 0, cut), (1, -1, cut, self.width - cut))


def parts_of(array, tiles):
    parts, first = [], 0
    for number, count in enumerate(tiles):
        parts.append(Part(array, number, ORDERS[number], first, count))
        first += count
    return parts


def near_parts():
    return parts_of(NEAR, (6, 6, 5))


def far_parts():
    return parts_of(FAR, (20, 12, 12))


def greet(others):
    barrier = pltpu.get_barrier_semaphore()
    for other in others:
        pl.semaphore_signal(barrier, inc=1, device_id=other)
    pl.semaphore_wait(barrier, len(others))


def ring_device(axis, step, other):
    yh, z, x, yl, c = place()
    core = (c + other) % 2
    if axis == "x":
        return device(yh, z, (x + step + 4) % 4, yl, core)
    if axis == "z":
        return device(yh, (z + step + 4) % 4, x, yl, core)
    y = (yh * 2 + yl + step + 4) % 4
    return device(y // 2, z, x, y % 2, core)


def ring_devices():
    return [ring_device(axis, step, other) for axis in "xyz" for step in (1, 2, 3) for other in (0, 1)]


def sequence_chip(number):
    yh, z, x, yl, c = place()
    return device(yh, z, number // 2, number % 2, c)


def sequence_others():
    yh, z, x, yl, c = place()
    me = x * 2 + yl
    return [sequence_chip((me + step) % 8) for step in range(1, 8)]


HBM = pl.BlockSpec(memory_space=pltpu.HBM)
VMEM = pl.BlockSpec(memory_space=pltpu.VMEM)


def load_all(pairs, sems):
    copies = [pltpu.make_async_copy(a, b, sems.at[n]) for n, (a, b) in enumerate(pairs)]
    for copy in copies:
        copy.start()
    return copies


def nt(left, right):
    return lax.dot_general(left, right, (((1,), (1,)), ((), ())), preferred_element_type=jnp.float32)


def rms_scale(values):
    return lax.rsqrt(jnp.mean(values * values, axis=-1, keepdims=True) + eps_norm)


def norm_back(grad_out, values, scale_factor, gain):
    weighted = grad_out * gain
    inner = jnp.mean(weighted * values, axis=-1, keepdims=True)
    grad_in = (
        scale_factor * weighted - values * (scale_factor * scale_factor * scale_factor) * inner
    )
    return (grad_in, grad_out * values * scale_factor)


def rope_pair(tab):
    table = tab[...].reshape(BLOCK, HEAD_DIM)
    turned = pltpu.roll(table, HEAD_DIM // 2, 1)
    low = lax.broadcasted_iota(jnp.int32, (BLOCK, HEAD_DIM), 1) < HEAD_DIM // 2
    return jnp.where(low, table, turned), jnp.where(low, -turned, table)


class Gather:
    def __init__(self, units, outs, base, send, recv, local):
        self.units, self.outs, self.base = units, outs, base
        self.send, self.recv, self.local = send, recv, local
        self.copies = {}

    def remote(self, key, slot, source, target, device_id):
        copy = pltpu.make_async_remote_copy(
            source, target, self.send.at[slot], self.recv.at[slot], device_id=device_id
        )
        copy.start()
        self.copies[key] = copy

    def slot(self, part, n):
        return self.base[part.array] + part.number * GATHER_SLOTS + n

    def spread(self, parts):
        yh, z, x, yl, c = place()
        for part in parts:
            target = self.outs[part.array].at[yh, z, x, yl, c, :, part.cols]
            for step in range(4):
                for other in range(2):
                    source = self.units[part.array].at[(c + other) % 2, :, part.cols]
                    key = (part.array, part.number, 0, step, other)
                    if step == 0 and other == 0:
                        copy = pltpu.make_async_copy(
                            source, target, self.local.at[part.array * 3 + part.number]
                        )
                        copy.start()
                        self.copies[key] = copy
                    else:
                        slot = self.slot(part, step * 2 + other - 1)
                        self.remote(key, slot, source, target, ring_device(part.order[0], step, other))

    def settle(self, part):
        for step in range(4):
            for other in range(2):
                copy = self.copies[part.array, part.number, 0, step, other]
                if step == 0 and other == 0:
                    copy.wait()
                else:
                    copy.wait_recv()

    def block(self, part, phase, offset, first, width):
        index = chip_set(part.order[:phase], part.order[phase], offset)
        cols = pl.ds(part.start + first, width)
        return self.outs[part.array].at[(*index, slice(None), slice(None), cols)]

    def direct(self, part):
        ref = self.block(part, 1, 0, 0, part.width)
        for step in (1, 2, 3):
            key = (part.array, part.number, 1, step)
            self.remote(key, self.slot(part, 6 + step), ref, ref, ring_device(part.order[1], step, 0))

    def landed(self, part):
        for step in (1, 2, 3):
            self.copies[part.array, part.number, 1, step].wait_recv()

    def ring(self, part, phase, which):
        for half, way, first, width in part.halves:
            step, offset = ((way, 0), (-way, 0), (way, -way))[which]
            key = (part.array, part.number, phase, which, half)
            if which == 2:
                self.copies[part.array, part.number, phase, 0, half].wait_recv()
            ref = self.block(part, phase, offset, first, width)
            slot = self.slot(part, 7 + 6 * (phase - 1) + 2 * which + half)
            self.remote(key, slot, ref, ref, ring_device(part.order[phase], step, 0))

    def begin(self, parts, phase):
        for part in parts:
            self.ring(part, phase, 0)
            self.ring(part, phase, 1)

    def forward(self, parts, phase):
        for part in parts:
            self.ring(part, phase, 2)

    def arrive(self, parts, phase):
        for part in parts:
            for which in (1, 2):
                for half in (0, 1):
                    self.copies[part.array, part.number, phase, which, half].wait_recv()

    def drain(self):
        for key, copy in self.copies.items():
            if key[2:] != (0, 0, 0):
                copy.wait_send()


GATHER_SLOTS = 19


def kept_index(kept, axis, step):
    iyh, iz, ix, iyl = chip_set(tuple(a for a in kept if a != axis), axis, step)
    index = ()
    if "y" in kept:
        index += (iyh,)
    if "z" in kept:
        index += (iz,)
    if "x" in kept:
        index += (ix,)
    if "y" in kept:
        index += (iyl,)
    return index


def add_sets(dims, terms, store):
    def one(flat_index, _):
        index, rest = [], flat_index
        for size in reversed(dims):
            index.insert(0, rest % size)
            rest = rest // size
        at = tuple(index)
        total = terms[0][at].astype(jnp.float32)
        for term in terms[1:]:
            total = total + term[at].astype(jnp.float32)
        store(at, total)
        return 0

    lax.fori_loop(0, math.prod(dims), one, 0)


def scatter_shapes():
    low, shapes = jnp.bfloat16, []
    for part in near_parts() + far_parts():
        plane, line = set_dims(part.order[:2]), set_dims(part.order[:1])
        for _, _, _, width in part.halves:
            shapes += [pltpu.VMEM((*plane, 16, width), low)] * 4
            if part.array == FAR:
                shapes += [pltpu.VMEM((*line, 16, width), low)] * 4
        if part.array == NEAR:
            shapes += [pltpu.VMEM((*line, 16, part.width), low)] * 3
        shapes += [pltpu.VMEM((8, 8, part.width), low)]
        shapes += [pltpu.VMEM((*plane, 16, part.width), low)]
        shapes += [pltpu.VMEM((*line, 2, 8, part.width), low)]
    return shapes


class Scatter:
    def __init__(self, grads, fin, refs, send, recv):
        self.grads, self.fin, self.send, self.recv = grads, fin, send, recv
        self.copies, self.loads = {}, {}
        self.land, self.mids, self.plane, self.line = {}, {}, {}, {}
        refs = list(refs)
        for part in near_parts() + far_parts():
            name = (part.array, part.number)
            for half in (0, 1):
                for phase in (0, 1) if part.array == FAR else (0,):
                    self.land[name, phase, half] = [refs.pop(0) for _ in range(3)]
                    self.mids[name, phase, half] = refs.pop(0)
            if part.array == NEAR:
                self.land[name, 1] = [refs.pop(0) for _ in range(3)]
            self.land[name, 2] = refs.pop(0)
            self.plane[name] = refs.pop(0)
            self.line[name] = refs.pop(0)

    def remote(self, key, part, n, source, target, device_id):
        slot = (part.array * 3 + part.number) * GATHER_SLOTS + n
        copy = pltpu.make_async_remote_copy(
            source, target, self.send.at[slot], self.recv.at[slot], device_id=device_id
        )
        copy.start()
        self.copies[key] = copy

    def source(self, part, phase, offset, first, width):
        if phase == 0:
            index = chip_set(part.order[:2], part.order[2], offset)
            cols = pl.ds(part.start + first, width)
            return self.grads[part.array].at[(*index, slice(None), cols)]
        index = kept_index(part.order[:2], part.order[1], offset)
        return self.plane[part.array, part.number].at[(*index, slice(None), pl.ds(first, width))]

    def load(self, part, sems):
        name = (part.array, part.number)
        every = (slice(None),) * (len(set_dims(part.order[:2])) + 1)
        for half, way, first, width in part.halves:
            target = self.plane[name].at[(*every, pl.ds(first, width))]
            for m, (offset, place_to) in enumerate(((way, self.mids[name, 0, half]), (0, target))):
                copy = pltpu.make_async_copy(
                    self.source(part, 0, offset, first, width), place_to, sems.at[2 * half + m]
                )
                copy.start()
                self.loads[name, half, m] = copy

    def ring(self, part, phase, which):
        name = (part.array, part.number)
        for half, way, first, width in part.halves:
            offset, step = ((2, way), (-way, -way))[which]
            self.remote(
                (name, phase, which, half), part, 6 * phase + 2 * which + half,
                self.source(part, phase, offset, first, width), self.land[name, phase, half][which],
                ring_device(part.order[2 - phase], step, 0),
            )

    def begin(self, parts, phase):
        for part in parts:
            self.ring(part, phase, 0)
        for part in parts:
            self.ring(part, phase, 1)

    def middle(self, parts, phase):
        for part in parts:
            name = (part.array, part.number)
            for half, way, first, width in part.halves:
                self.copies[name, phase, 0, half].wait_recv()
                mid = self.mids[name, phase, half]
                own = self.source(part, phase, way, first, width)
                if (name, half, 0) in self.loads and phase == 0:
                    self.loads[name, half, 0].wait()
                    own = mid

                def store(at, total, mid=mid):
                    mid[at] = total.astype(jnp.bfloat16)

                add_sets(set_dims(part.order[: 2 - phase]), [own, self.land[name, phase, half][0]], store)
                self.remote(
                    (name, phase, 2, half), part, 6 * phase + 4 + half, mid,
                    self.land[name, phase, half][2], ring_device(part.order[2 - phase], way, 0),
                )

    def end(self, parts, phase):
        for part in parts:
            name = (part.array, part.number)
            for half, way, first, width in part.halves:
                self.copies[name, phase, 1, half].wait_recv()
                self.copies[name, phase, 2, half].wait_recv()
                base = self.source(part, phase, 0, first, width)
                cols = pl.ds(first, width)
                if phase == 0:
                    plane = self.plane[name]
                    if (name, half, 1) in self.loads:
                        self.loads[name, half, 1].wait()
                        base = plane.at[(*(slice(None),) * (len(plane.shape) - 1), cols)]

                    def store(at, total, plane=plane, cols=cols):
                        plane[(*at, slice(None), cols)] = total.astype(jnp.bfloat16)

                else:
                    line = self.line[name]

                    def store(at, total, line=line, cols=cols):
                        line[(*at, 0, slice(None), cols)] = total[:8].astype(jnp.bfloat16)
                        line[(*at, 1, slice(None), cols)] = total[8:].astype(jnp.bfloat16)

                add_sets(
                    set_dims(part.order[: 2 - phase]), [base, *self.land[name, phase, half][1:]], store
                )

    def direct(self, parts):
        for part in parts:
            name = (part.array, part.number)
            for step in (1, 2, 3):
                self.remote(
                    (name, 1, step), part, 5 + step, self.source(part, 1, step, 0, part.width),
                    self.land[name, 1][step - 1], ring_device(part.order[1], step, 0),
                )

    def landed(self, parts):
        for part in parts:
            name = (part.array, part.number)
            for step in (1, 2, 3):
                self.copies[name, 1, step].wait_recv()
            line = self.line[name]

            def store(at, total, line=line):
                line[(*at, 0)] = total[:8].astype(jnp.bfloat16)
                line[(*at, 1)] = total[8:].astype(jnp.bfloat16)

            add_sets(
                set_dims(part.order[:1]),
                [self.source(part, 1, 0, 0, part.width), *self.land[name, 1]], store,
            )

    def deliver(self, parts):
        c = place()[4]
        for part in parts:
            name, axis = (part.array, part.number), part.order[0]
            for step in range(4):
                for other in range(2):
                    if step or other:
                        source = self.line[name].at[
                            (*kept_index(part.order[:1], axis, step), (c + other) % 2)
                        ]
                        self.remote(
                            (name, 2, step, other), part, 11 + step * 2 + other, source,
                            self.land[name, 2].at[step * 2 + other], ring_device(axis, step, other),
                        )

    def finish(self, parts):
        c = place()[4]
        for part in parts:
            name, axis = (part.array, part.number), part.order[0]
            for other in range(2):
                total = None
                for step in range(4):
                    if step or other:
                        self.copies[name, 2, step, other].wait_recv()
                        term = self.land[name, 2][step * 2 + other]
                    else:
                        term = self.line[name][(*kept_index(part.order[:1], axis, 0), c)]
                    term = term.astype(jnp.float32)
                    total = term if total is None else total + term
                self.fin[part.array][(c + other) % 2, :, part.cols] = total

    def drain(self):
        for copy in self.copies.values():
            copy.wait_send()


def columns(head):
    return pl.ds(pl.multiple_of(head * HEAD_DIM, HEAD_DIM), HEAD_DIM)


def exchange_start(moves, me, send, recv, local, first):
    copies = []
    for step in range(1, 8):
        there = (me + step) % 8
        for n, (source, target) in enumerate(moves):
            copy = pltpu.make_async_remote_copy(
                source(there), target(me), send.at[first + n, step], recv.at[first + n, step],
                device_id=sequence_chip(there),
            )
            copy.start()
            copies.append(copy)
    for n, (source, target) in enumerate(moves):
        copy = pltpu.make_async_copy(source(me), target(me), local.at[first + n])
        copy.start()
        copies.append(copy)
    return copies


FAR_SPANS = ((0, 1024), (1024, 1536), (2560, 1536), (4096, 1536))


def middle_shapes():
    low, wide = jnp.bfloat16, jnp.float32
    return [
        pltpu.VMEM((BLOCK, D), wide),
        pltpu.VMEM((BLOCK, D), wide),
        pltpu.VMEM((BLOCK, D), low),
        pltpu.VMEM((D, BLOCK), low),
        pltpu.VMEM((D, BLOCK), low),
        pltpu.VMEM((BLOCK, 1536), wide),
        pltpu.VMEM((BLOCK, 1536), low),
        pltpu.VMEM((BLOCK, 1536), low),
        pltpu.VMEM((BLOCK, 1536), low),
        pltpu.VMEM((BLOCK, D), wide),
        pltpu.VMEM((128, D), wide),
        pltpu.VMEM((BLOCK, 1024), low),
        pltpu.VMEM((D, WIDE[FAR]), low),
        pltpu.VMEM((4, BLOCK, 256), low),
        pltpu.VMEM((4, BLOCK, 256), low),
        pltpu.VMEM((4, BLOCK, 256), low),
        pltpu.VMEM((4, BLOCK, 256), low),
        pltpu.VMEM((128, D), low),
        pltpu.VMEM((128, D), low),
    ]


def middle_layer(att, x_ref, g_low, rows, w_far, refs, outs, pair_send, pair_recv, sems, c, sib):
    output, grad_att_out, gmid_out, post_out, dw_out = outs
    (branch, middle, hidden, g_t, hidden_t, grad_act, act, gate_grad, up_grad, grad_hidden,
     down_own, grad_att, dw, out1, in1, out2, in2, out3, in3) = refs
    branch_t = hidden_t
    swaps = []

    def swap(source, target):
        n = 3 + len(swaps)
        copy = pltpu.make_async_remote_copy(
            source, target, pair_send.at[n], pair_recv.at[n], device_id=sib
        )
        copy.start()
        swaps.append(copy)
        return copy

    def part(n, width=256):
        return pl.ds(n * width, width)

    def far_rows(n, which):
        first, width = FAR_SPANS[which]
        half = n % 2 * 2
        return w_far[n // 2, half : half + 2, :, :, :, :, first : first + width].reshape(256, width)

    def far_cols(which, n):
        first = FAR_SPANS[which][0] + n * 256
        return w_far[:, :, :, :, :, :, first : first + 256].reshape(D, 256)

    first = []
    for n in range(4):
        block = nt(att[...], far_rows(n, 0))
        branch[:, part(n)] = block
        out1[n] = block.astype(jnp.bfloat16)
        first.append(swap(out1.at[n], in1.at[n]))
    for n in range(6):
        grad_act[:, part(n)] = jnp.dot(g_low, far_cols(3, n), preferred_element_type=jnp.float32)
    for n in range(4):
        first[n].wait_recv()
        middle[:, part(n)] = (
            x_ref[...].reshape(BLOCK, D)[:, n * 256 : n * 256 + 256].astype(jnp.float32)
            + (branch[:, part(n)] + in1[n].astype(jnp.float32))
        )
    gain = rows[1:2, :]
    scale = rms_scale(middle[...])
    hidden[...] = (middle[...] * scale * gain).astype(jnp.bfloat16)
    for n in range(6):
        gate = jnp.dot(hidden[...], far_cols(1, n), preferred_element_type=jnp.float32)
        up = jnp.dot(hidden[...], far_cols(2, n), preferred_element_type=jnp.float32)
        sigma = jax.nn.sigmoid(gate)
        swish = gate * sigma
        grad = grad_act[:, part(n)]
        act[:, part(n)] = (swish * up).astype(jnp.bfloat16)
        gate_grad[:, part(n)] = (grad * up * (sigma * (1.0 + gate * (1.0 - sigma)))).astype(jnp.bfloat16)
        up_grad[:, part(n)] = (grad * swish).astype(jnp.bfloat16)
    second = []
    for n in range(4):
        block = nt(gate_grad[...], far_rows(n, 1)) + nt(up_grad[...], far_rows(n, 2))
        grad_hidden[:, part(n)] = block
        out2[n] = block.astype(jnp.bfloat16)
        second.append(swap(out2.at[n], in2.at[n]))
    away = pl.ds(pl.multiple_of((1 - c) * 128, 128), 128)
    own = pl.ds(pl.multiple_of(c * 128, 128), 128)
    for n in range(4):
        out3[:, part(n)] = nt(act[away, :], far_rows(n, 3)).astype(jnp.bfloat16)
    third = swap(out3, in3)
    for n in range(4):
        down_own[:, part(n)] = nt(act[own, :], far_rows(n, 3))
    hidden_t[...] = hidden[...].T
    stores = []

    def keep(source, target):
        copy = pltpu.make_async_copy(source, target, sems.at[6 + len(stores)])
        copy.start()
        stores.append(copy)

    for lhs, rhs, (first, width) in (
        (hidden_t, gate_grad, FAR_SPANS[1]), (hidden_t, up_grad, FAR_SPANS[2]), (g_t, act, FAR_SPANS[3])
    ):
        for n in range(4):
            dw[part(n), first : first + width] = jnp.dot(
                lhs[part(n), :], rhs[...], preferred_element_type=jnp.float32
            ).astype(jnp.bfloat16)
        keep(dw.at[:, pl.ds(first, width)], dw_out.at[:, pl.ds(first, width)])
    for n in range(4):
        second[n].wait_recv()
        grad_hidden[:, part(n)] = grad_hidden[:, part(n)] + in2[n].astype(jnp.float32)
    grad_in, terms = norm_back(grad_hidden[...], middle[...], scale, gain)
    grad_hidden[...] = terms
    post_out[...] = jnp.broadcast_to(jnp.sum(grad_hidden[own, :], axis=0, keepdims=True), (8, D))
    grad_hidden[...] = g_low.astype(jnp.float32) + grad_in
    gmid_out[...] = grad_hidden[own, :]
    branch_grad = grad_hidden[...].astype(jnp.bfloat16)
    branch_t[...] = branch_grad.T
    for n in range(4):
        grad_att[:, part(n)] = jnp.dot(
            branch_grad, far_cols(0, n), preferred_element_type=jnp.float32
        ).astype(jnp.bfloat16)
    keep(grad_att, grad_att_out)
    for n in range(4):
        dw[part(n), :1024] = jnp.dot(
            branch_t[part(n), :], att[...], preferred_element_type=jnp.float32
        ).astype(jnp.bfloat16)
    keep(dw.at[:, pl.ds(0, 1024)], dw_out.at[:, pl.ds(0, 1024)])
    third.wait_recv()
    output[...] = (
        middle[own, :] + (down_own[...] + in3[...].astype(jnp.float32))
    ).astype(jnp.bfloat16)
    for copy in swaps:
        copy.wait_send()
    for copy in stores:
        copy.wait()


def forward_kernel(*refs):
    gains_in, shards, (x_in, g_in, cos_in, sin_in), refs = refs[:4], refs[4:11], refs[11:15], refs[15:]
    near_out, x_out, tab_out, q_out, k_out, v_out, o32_out, lse_ref, normed_out = refs[:9]
    qpre_out, kpre_out, rows_ref, output, grad_att_out, gmid_out, post_out, dw_out = refs[9:17]
    x_ref, g_ref, tab, w_near, w_far, normed, qpre, kpre, q_low, k_low, v_low = refs[17:28]
    q_ref, k_ref, v_ref, o32_ref, o_low, att, vt, near_unit, far_unit, tab_own = refs[28:38]
    middle_refs, refs = refs[38:57], refs[57:]
    send, recv, head_send, head_recv, local, load, store, pair_send, pair_recv, pair_local, own = refs
    weights = (w_near, w_far)
    yh, z, x, yl, c = place()
    me = x * 2 + yl
    sib = sibling()
    lanes = lax.broadcasted_iota(jnp.int32, (TILE, TILE), 1)
    rows = lax.broadcasted_iota(jnp.int32, (TILE, TILE), 0)
    tile = jnp.zeros((TILE, TILE), jnp.float32)
    for n, gain in enumerate(gains_in):
        value = gain[...].astype(jnp.float32)
        if value.shape[1] == 1:
            tile = jnp.where((rows == n) & (lanes == 0), value, tile)
        else:
            value = jnp.concatenate([value, jnp.zeros((1, TILE - 8), jnp.float32)], axis=1)
            tile = jnp.where(rows == n, value, tile)
    tile = tile.T[:8].astype(jnp.bfloat16)
    for unit, group, first in ((near_unit, shards[:3], 0), (far_unit, shards[3:], 0)):
        for shard in group:
            width = shard.shape[1] // 2
            for half in range(2):
                unit[half, :, first : first + width] = shard[:, half * width : (half + 1) * width]
            first += width
    near_unit[0, :, 2048:] = tile
    near_unit[1, :, 2048:] = tile
    tab_own[...] = jnp.concatenate([cos_in[...], sin_in[...]], axis=1)
    greet(ring_devices() + sequence_others() + [sib])
    near, far = near_parts(), far_parts()
    gather = Gather((near_unit, far_unit), weights, (0, 3 * GATHER_SLOTS), send, recv, own)
    gather.spread(near)
    pairs = []
    for k, (source, target) in enumerate(((x_in, x_ref), (tab_own, tab), (g_in, g_ref))):
        keep = pltpu.make_async_copy(source, target.at[c], pair_local.at[k])
        away = pltpu.make_async_remote_copy(
            source, target.at[c], pair_send.at[k], pair_recv.at[k], device_id=sib
        )
        keep.start()
        away.start()
        pairs.append((keep, away))
    gather.spread(far)
    for part in near:
        gather.settle(part)
        gather.direct(part)
    for part in near:
        gather.landed(part)
        gather.begin([part], 2)
    for part in far:
        gather.settle(part)
        gather.begin([part], 1)
    gather.forward(near, 2)
    gather.forward(far, 1)
    gather.arrive(far[:1], 1)
    gather.begin(far[:1], 2)
    gather.arrive(near, 2)
    keep_near = pltpu.make_async_copy(w_near, near_out, load.at[0])
    keep_near.start()
    gather.arrive(far[1:], 1)
    gather.ring(far[1], 2, 0)
    gather.ring(far[2], 2, 0)
    for keep, away in pairs:
        keep.wait()
        away.wait_recv()

    def matrix(first, width):
        return w_near[:, :, :, :, :, :, first : first + width].reshape(D, width)

    gain_rows = matrix(2048, TILE).astype(jnp.float32).T[:8]
    pick = (
        lax.broadcasted_iota(jnp.int32, (D, HEAD_DIM), 0)
        == 8 * lax.broadcasted_iota(jnp.int32, (D, HEAD_DIM), 1)
    ).astype(jnp.bfloat16)
    head_gains = jnp.dot(gain_rows.astype(jnp.bfloat16), pick, preferred_element_type=jnp.float32)
    rows_ref[...] = gain_rows
    rows_ref[2:4, :HEAD_DIM] = head_gains[2:4]
    gain_q, gain_k = head_gains[2:3], head_gains[3:4]
    values = x_ref[...].reshape(BLOCK, D).astype(jnp.float32)
    normed[...] = (values * rms_scale(values) * gain_rows[0:1]).astype(jnp.bfloat16)
    cosine, sine = rope_pair(tab)

    def head(pre, gain):
        unit = pre * rms_scale(pre) * gain
        return (unit * cosine + pltpu.roll(unit, HEAD_DIM // 2, 1) * sine).astype(jnp.bfloat16)

    for first, pre_ref, low_ref, gain in ((0, qpre, q_low, gain_q), (1024, kpre, k_low, gain_k)):
        for n in range(pre_ref.shape[1] // 256):
            at = slice(n * 256, n * 256 + 256)
            pre = jnp.dot(normed[...], matrix(first + n * 256, 256), preferred_element_type=jnp.float32)
            pre_ref[:, at] = pre
            low_ref[:, n * 256 : n * 256 + 128] = head(pre[:, :128], gain)
            low_ref[:, n * 256 + 128 : n * 256 + 256] = head(pre[:, 128:], gain)
    v_low[...] = jnp.dot(normed[...], matrix(1536, 512), preferred_element_type=jnp.float32).astype(jnp.bfloat16)
    arriving = exchange_start(
        [
            (lambda j: q_low.at[:, columns(j)], lambda i: q_ref.at[i]),
            (lambda j: k_low.at[:, columns(j // 2)], lambda i: k_ref.at[i]),
            (lambda j: v_low.at[:, columns(j // 2)], lambda i: v_ref.at[i]),
        ],
        me, head_send, head_recv, local, 0,
    )
    stores = [
        pltpu.make_async_copy(a, b, store.at[n])
        for n, (a, b) in enumerate(
            ((normed, normed_out), (qpre, qpre_out), (kpre, kpre_out), (q_ref, q_out), (k_ref, k_out),
             (v_ref, v_out), (o32_ref, o32_out), (x_ref, x_out), (tab, tab_out))
        )
    ]
    for copy in stores[:3] + stores[7:]:
        copy.start()
    for copy in arriving:
        copy.wait()
    gather.forward(far[:1], 2)
    gather.ring(far[1], 2, 1)
    gather.ring(far[2], 2, 1)
    for copy in stores[3:6]:
        copy.start()
    for j in range(8):
        vt[j] = v_ref[j].T

    def one_block(i, _):
        q = q_ref[i]

        def weigh(j, carry):
            total, mixed = carry
            p = jnp.exp2(nt(k_ref[j], q) * (score_scale * log2e))
            total = total + jnp.sum(p, axis=0, keepdims=True)
            mixed = mixed + jnp.dot(vt[j], p.astype(jnp.bfloat16), preferred_element_type=jnp.float32)
            return total, mixed

        carry = (jnp.zeros((1, BLOCK), jnp.float32), jnp.zeros((HEAD_DIM, BLOCK), jnp.float32))
        carry = lax.fori_loop(
            0, (i + 1) // 2, lambda t, carry: weigh(2 * t + 1, weigh(2 * t, carry)), carry
        )
        total, mixed = lax.fori_loop(i // 2 * 2 + (i % 2) * 2, i + 1, weigh, carry)
        out = (mixed / total).T
        o32_ref[i] = out
        o_low[i] = out.astype(jnp.bfloat16)
        lse_ref[i] = jnp.log2(total)
        return 0

    lax.fori_loop(0, 6, one_block, 0)
    gather.forward(far[1:], 2)
    lax.fori_loop(6, 8, one_block, 0)
    leaving = exchange_start(
        [(lambda j: o_low.at[j], lambda i: att.at[:, columns(i)])],
        me, head_send, head_recv, local, 3,
    )
    stores[6].start()
    g_low = g_ref[...].reshape(BLOCK, D)
    g_t = middle_refs[3]
    g_t[...] = g_low.T
    gather.arrive(far, 2)
    for copy in leaving:
        copy.wait()
    middle_layer(
        att, x_ref, g_low, rows_ref, w_far, middle_refs, (output, grad_att_out, gmid_out, post_out, dw_out),
        pair_send, pair_recv, own, c, sib,
    )
    gather.drain()
    for copy in stores:
        copy.wait()
    keep_near.wait()
    for _, away in pairs:
        away.wait_send()


def attend(gains, shards, tokens):
    blocks = (8, BLOCK, HEAD_DIM)
    low, wide = jnp.bfloat16, jnp.float32
    whole = [(2, 4, 4, 2, 2, 8, w) for w in WIDE]
    return pl.pallas_call(
        forward_kernel,
        out_shape=[
            jax.ShapeDtypeStruct(whole[NEAR], low),
            jax.ShapeDtypeStruct((2, 128, D), low),
            jax.ShapeDtypeStruct((2, 128, HEAD_DIM), wide),
        ]
        + [jax.ShapeDtypeStruct(blocks, low)] * 3
        + [
            jax.ShapeDtypeStruct(blocks, wide),
            jax.ShapeDtypeStruct((8, 1, BLOCK), wide),
            jax.ShapeDtypeStruct((BLOCK, D), low),
            jax.ShapeDtypeStruct((BLOCK, 1024), wide),
            jax.ShapeDtypeStruct((BLOCK, 512), wide),
            jax.ShapeDtypeStruct((8, D), wide),
            jax.ShapeDtypeStruct((128, D), low),
            jax.ShapeDtypeStruct((BLOCK, 1024), low),
            jax.ShapeDtypeStruct((128, D), wide),
            jax.ShapeDtypeStruct((8, D), wide),
            jax.ShapeDtypeStruct((D, WIDE[FAR]), low),
        ],
        in_specs=[VMEM] * 15,
        out_specs=[HBM] * 7 + [VMEM] + [HBM] * 3 + [VMEM, VMEM, HBM, VMEM, VMEM, HBM],
        scratch_shapes=[
            pltpu.VMEM((2, 128, D), low),
            pltpu.VMEM((2, 128, D), low),
            pltpu.VMEM((2, 128, HEAD_DIM), wide),
            pltpu.VMEM(whole[NEAR], low),
            pltpu.VMEM(whole[FAR], low),
            pltpu.VMEM((BLOCK, D), low),
            pltpu.VMEM((BLOCK, 1024), wide),
            pltpu.VMEM((BLOCK, 512), wide),
            pltpu.VMEM((BLOCK, 1024), low),
            pltpu.VMEM((BLOCK, 512), low),
            pltpu.VMEM((BLOCK, 512), low),
        ]
        + [pltpu.VMEM(blocks, low)] * 3
        + [
            pltpu.VMEM(blocks, wide),
            pltpu.VMEM(blocks, low),
            pltpu.VMEM((BLOCK, 1024), low),
            pltpu.VMEM((8, HEAD_DIM, BLOCK), low),
            pltpu.VMEM((2, 8, WIDE[0]), low),
            pltpu.VMEM((2, 8, WIDE[1]), low),
            pltpu.VMEM((128, HEAD_DIM), wide),
        ]
        + middle_shapes()
        + [
            pltpu.SemaphoreType.DMA((6 * GATHER_SLOTS,)),
            pltpu.SemaphoreType.DMA((6 * GATHER_SLOTS,)),
            pltpu.SemaphoreType.DMA((4, 8)),
            pltpu.SemaphoreType.DMA((4, 8)),
            pltpu.SemaphoreType.DMA((4,)),
            pltpu.SemaphoreType.DMA((1,)),
            pltpu.SemaphoreType.DMA((9,)),
            pltpu.SemaphoreType.DMA((12,)),
            pltpu.SemaphoreType.DMA((12,)),
            pltpu.SemaphoreType.DMA((3,)),
            pltpu.SemaphoreType.DMA((11,)),
        ],
        compiler_params=pltpu.CompilerParams(
            collective_id=2, has_side_effects=True, vmem_limit_bytes=LIMIT
        ),
        name="attend",
    )(*gains, *shards, *tokens)


def backward_kernel(*refs):
    near, far = near_parts(), far_parts()
    n_scatter = len(scatter_shapes())
    ins, far_grad, do_in, refs = refs[:14], refs[14], refs[15], refs[16:]
    fin, input_grad, held, refs = refs[:2], refs[2], refs[3:17], refs[17:]
    q_ref, k_ref, v_ref, o32_ref, lse_ref, qpre, kpre, normed, tab, rows, x_ref = held[:11]
    w_near, gmid, post = held[11:]
    do_ref, dq_low, dk_low, dv_low, kt, dk_acc, dv_acc = refs[:7]
    gq, kparts, vparts, dqkv, normed_t, pair_out, pair_in, near_grad = refs[7:15]
    places, refs = refs[15 : 15 + n_scatter], refs[15 + n_scatter :]
    send, recv, pair_send, pair_recv, load, far_load, head_send, head_recv, head_local = refs
    yh, z, x, yl, c = place()
    me = x * 2 + yl
    sib = sibling()
    scatter = Scatter((near_grad, far_grad), fin, places, send, recv)
    loads = load_all(list(zip(ins, held)), load)
    for n, part in enumerate(far):
        scatter.load(part, far_load.at[n])
    greet(ring_devices() + sequence_others() + [sib])
    arriving = exchange_start(
        [(lambda j: do_in.at[:, columns(j)], lambda i: do_ref.at[i])],
        me, head_send, head_recv, head_local, 0,
    )
    scatter.begin(far[:1], 0)
    scatter.begin(far[1:], 0)
    for copy in loads[:5]:
        copy.wait()
    for j in range(8):
        kt[j] = k_ref[j].T
    dk_acc[...] = jnp.zeros_like(dk_acc)
    dv_acc[...] = jnp.zeros_like(dv_acc)
    for copy in arriving:
        copy.wait()

    def one_block(i, _):
        q, do, lse = q_ref[i], do_ref[i], lse_ref[i]
        delta = jnp.sum((do.astype(jnp.float32) * o32_ref[i]).T, axis=0, keepdims=True)

        def one_pair(j, dqt):
            p = jnp.exp2(nt(k_ref[j], q) * (score_scale * log2e) - lse)
            dp = nt(v_ref[j], do)
            ds = (p * (dp - delta)).astype(jnp.bfloat16)
            dv_acc[j] += jnp.dot(p.astype(jnp.bfloat16), do, preferred_element_type=jnp.float32)
            dk_acc[j] += jnp.dot(ds, q, preferred_element_type=jnp.float32)
            return dqt + jnp.dot(kt[j], ds, preferred_element_type=jnp.float32)

        dqt = lax.fori_loop(
            0, (i + 1) // 2, lambda t, carry: one_pair(2 * t + 1, one_pair(2 * t, carry)),
            jnp.zeros((HEAD_DIM, BLOCK), jnp.float32),
        )
        dqt = lax.fori_loop(i // 2 * 2 + (i % 2) * 2, i + 1, one_pair, dqt)
        dq_low[i] = (dqt * score_scale).T.astype(jnp.bfloat16)
        return 0

    lax.fori_loop(0, 6, one_block, 0)
    scatter.middle(far[:1], 0)
    scatter.middle(far[1:], 0)
    lax.fori_loop(6, 8, one_block, 0)
    dk_low[...] = (dk_acc[...] * score_scale).astype(jnp.bfloat16)
    dv_low[...] = dv_acc[...].astype(jnp.bfloat16)
    arriving = exchange_start(
        [
            (lambda j: dq_low.at[j], lambda i: gq.at[:, columns(i)]),
            (lambda j: dk_low.at[j], lambda i: kparts.at[i % 2, :, columns(i // 2)]),
            (lambda j: dv_low.at[j], lambda i: vparts.at[i % 2, :, columns(i // 2)]),
        ],
        me, head_send, head_recv, head_local, 1,
    )
    scatter.end(far[:1], 0)
    scatter.begin(far[:1], 1)
    scatter.end(far[1:], 0)
    scatter.begin(far[1:], 1)
    for copy in loads[5:]:
        copy.wait()
    normed_t[...] = normed[...].T
    for copy in arriving:
        copy.wait()
    cosine, sine = rope_pair(tab)
    gain_q, gain_k = rows[2:3, :HEAD_DIM], rows[3:4, :HEAD_DIM]

    def head_back(grad, values, gain):
        grad = grad * cosine - pltpu.roll(grad, HEAD_DIM // 2, 1) * sine
        grad_in, terms = norm_back(grad, values, rms_scale(values), gain)
        return grad_in.astype(jnp.bfloat16), jnp.sum(terms, axis=0, keepdims=True)

    q_part = jnp.zeros((1, HEAD_DIM), jnp.float32)
    k_part = jnp.zeros((1, HEAD_DIM), jnp.float32)
    for h in range(8):
        at = slice(h * HEAD_DIM, (h + 1) * HEAD_DIM)
        dqkv[:, at], part = head_back(gq[:, at].astype(jnp.float32), qpre[:, at], gain_q)
        q_part = q_part + part
    for h in range(4):
        at = slice(h * HEAD_DIM, (h + 1) * HEAD_DIM)
        grad = kparts[0, :, at].astype(jnp.float32) + kparts[1, :, at].astype(jnp.float32)
        low_at = slice(1024 + h * HEAD_DIM, 1024 + (h + 1) * HEAD_DIM)
        dqkv[:, low_at], part = head_back(grad, kpre[:, at], gain_k)
        k_part = k_part + part
    dqkv[:, 1536:] = (vparts[0].astype(jnp.float32) + vparts[1].astype(jnp.float32)).astype(jnp.bfloat16)

    def weight_grads(n, _):
        lhs = normed_t[pl.ds(pl.multiple_of(n * 256, 256), 256), :]
        for first in range(0, 2048, 512):
            block = jnp.dot(lhs, dqkv[:, first : first + 512], preferred_element_type=jnp.float32)
            near_grad[n // 2, pl.ds(n % 2 * 2, 2), :, :, :, first : first + 512] = block.astype(
                jnp.bfloat16
            ).reshape(2, 4, 2, 16, 512)
        return 0

    lax.fori_loop(0, 4, weight_grads, 0)
    scatter.begin(near[:2], 0)

    def grad_normed(rows_at):
        return nt(dqkv[rows_at, :], w_near[:, :2048])

    away = pl.ds(pl.multiple_of((1 - c) * 128, 128), 128)
    own = pl.ds(pl.multiple_of(c * 128, 128), 128)
    pair_out[...] = grad_normed(away).astype(jnp.bfloat16)
    swap = pltpu.make_async_remote_copy(
        pair_out, pair_in, pair_send.at[0], pair_recv.at[0], device_id=sib
    )
    swap.start()
    grad = grad_normed(own)
    values = x_ref[c].astype(jnp.float32)
    swap.wait_recv()
    grad = grad + pair_in[...].astype(jnp.float32)
    grad_in, terms = norm_back(grad, values, rms_scale(values), rows[0:1, :])
    input_grad[...] = (gmid[...] + grad_in).astype(jnp.bfloat16)
    in_part = jnp.sum(terms, axis=0, keepdims=True)
    spread = (
        lax.broadcasted_iota(jnp.int32, (HEAD_DIM, D), 1)
        == 8 * lax.broadcasted_iota(jnp.int32, (HEAD_DIM, D), 0)
    ).astype(jnp.bfloat16)
    qk = jnp.concatenate([q_part, k_part, jnp.zeros((6, HEAD_DIM), jnp.float32)]).astype(jnp.bfloat16)
    qk = jnp.dot(qk, spread, preferred_element_type=jnp.float32)
    gain_rows = jnp.concatenate(
        [in_part, post[0:1, :], qk[0:2], jnp.zeros((TILE - 4, D), jnp.float32)]
    )
    near_grad[:, :, :, :, :, 2048:] = gain_rows.T.astype(jnp.bfloat16).reshape(2, 4, 4, 2, 16, TILE)
    scatter.begin(near[2:], 0)
    scatter.middle(near, 0)
    scatter.middle(far, 1)
    for part in near:
        scatter.end([part], 0)
        scatter.direct([part])
    for part in far:
        scatter.end([part], 1)
        scatter.deliver([part])
    for part in near:
        scatter.landed([part])
        scatter.deliver([part])
    scatter.finish(far)
    scatter.finish(near)
    scatter.drain()
    swap.wait_send()


def attend_back(arrays, far_grad, grad_att):
    blocks = (8, BLOCK, HEAD_DIM)
    low, wide = jnp.bfloat16, jnp.float32
    return pl.pallas_call(
        backward_kernel,
        out_shape=[jax.ShapeDtypeStruct((2, 8, w), wide) for w in WIDE]
        + [jax.ShapeDtypeStruct((128, D), low)],
        in_specs=[HBM] * (len(arrays) + 2),
        out_specs=[VMEM] * 3,
        scratch_shapes=[pltpu.VMEM(a.shape, a.dtype) for a in arrays]
        + [pltpu.VMEM(blocks, low)] * 4
        + [
            pltpu.VMEM((8, HEAD_DIM, BLOCK), low),
            pltpu.VMEM(blocks, wide),
            pltpu.VMEM(blocks, wide),
            pltpu.VMEM((BLOCK, 1024), low),
            pltpu.VMEM((2, BLOCK, 512), low),
            pltpu.VMEM((2, BLOCK, 512), low),
            pltpu.VMEM((BLOCK, 2048), low),
            pltpu.VMEM((D, BLOCK), low),
            pltpu.VMEM((128, D), low),
            pltpu.VMEM((128, D), low),
            pltpu.VMEM((2, 4, 4, 2, 16, WIDE[0]), low),
        ]
        + scatter_shapes()
        + [
            pltpu.SemaphoreType.DMA((6 * GATHER_SLOTS,)),
            pltpu.SemaphoreType.DMA((6 * GATHER_SLOTS,)),
            pltpu.SemaphoreType.DMA((1,)),
            pltpu.SemaphoreType.DMA((1,)),
            pltpu.SemaphoreType.DMA((len(arrays),)),
            pltpu.SemaphoreType.DMA((3, 4)),
            pltpu.SemaphoreType.DMA((4, 8)),
            pltpu.SemaphoreType.DMA((4, 8)),
            pltpu.SemaphoreType.DMA((4,)),
        ],
        compiler_params=pltpu.CompilerParams(
            collective_id=3, has_side_effects=True, vmem_limit_bytes=LIMIT
        ),
        name="attend_back",
    )(*arrays, far_grad, grad_att)


def results_kernel(near, far, grad_in, out_in, *refs):
    (q, k, v, in_gain, post_gain, q_gain, k_gain, w_out, gate, up, down, grad, out) = refs
    for source, group in ((near, ((q, 0), (k, 1024), (v, 1536))), (far, zip((w_out, gate, up, down), [s for s, _ in FAR_SPANS]))):
        for target, first in group:
            width = target.shape[1] // 2
            for half in range(2):
                target[:, half * width : (half + 1) * width] = source[half, :, first : first + width]
    gains = near[0, :, 2048:] + near[1, :, 2048:]
    gains = jnp.concatenate([gains, jnp.zeros((TILE - 8, TILE), jnp.float32)]).T
    in_gain[...] = gains[0:1, :8]
    post_gain[...] = gains[1:2, :8]
    q_gain[...] = gains[2:3, :1]
    k_gain[...] = gains[3:4, :1]
    grad[...] = grad_in[...]
    out[...] = out_in[...]


def results(arrays):
    shapes = [(8, 2048), (8, 1024), (8, 1024), (1, 8), (1, 8), (1, 1), (1, 1)]
    shapes += [(8, 2 * width) for _, width in FAR_SPANS]
    return pl.pallas_call(
        results_kernel,
        out_shape=[jax.ShapeDtypeStruct(s, jnp.float32) for s in shapes]
        + [jax.ShapeDtypeStruct((128, D), jnp.bfloat16)] * 2,
        in_specs=[VMEM] * 4,
        out_specs=[VMEM] * 13,
        name="results",
    )(*arrays)


def body(
    tokens,
    positions,
    in_gain,
    q_gain,
    k_gain,
    w_query,
    w_key,
    w_value,
    w_out,
    post_gain,
    w_gate,
    w_up,
    w_down,
    cotangent,
):
    half = HEAD_DIM // 2
    frequency = rope_base ** (-2.0 * jnp.arange(half, dtype=jnp.float32) / HEAD_DIM)
    angles = positions[0].astype(jnp.float32)[:, None] * frequency[None, :]
    gains = [g[None] for g in (in_gain, post_gain, q_gain, k_gain)]
    shards = [w_query, w_key, w_value, w_out.T, w_gate, w_up, w_down.T]
    (near, x_pair, tables, q_all, k_all, v_all, mixed, log_total, normed, q_pre, k_pre, rows, output,
     grad_att, grad_middle, post_part, far_grad) = attend(
        gains, shards, [tokens[0], cotangent[0], jnp.cos(angles), jnp.sin(angles)]
    )
    near_sum, far_sum, input_grad = attend_back(
        [q_all, k_all, v_all, mixed, log_total, q_pre, k_pre, normed, tables, rows, x_pair,
         near.reshape(D, WIDE[NEAR]), grad_middle, post_part],
        far_grad.reshape(2, 4, 4, 2, 16, WIDE[FAR]),
        grad_att,
    )
    (query, key, value, in_gain_grad, post_gain_grad, q_gain_grad, k_gain_grad, out_grad, gate, up, down,
     input_grad, output) = results([near_sum, far_sum, input_grad, output])
    return (
        output[None],
        input_grad[None],
        in_gain_grad[0],
        q_gain_grad[0],
        k_gain_grad[0],
        query,
        key,
        value,
        out_grad.T,
        post_gain_grad[0],
        gate,
        up,
        down.T,
    )


def solution(mesh):
    placed = (
        P("dp", "seq", None),
        P("dp", "seq"),
        P(("dp", "seq")),
        P(("dp", "seq")),
        P(("dp", "seq")),
        P(("dp", "seq"), None),
        P(("dp", "seq"), None),
        P(("dp", "seq"), None),
        P(None, ("dp", "seq")),
        P(("dp", "seq")),
        P(("dp", "seq"), None),
        P(("dp", "seq"), None),
        P(None, ("dp", "seq")),
        P("dp", "seq", None),
    )
    return jax.shard_map(
        body,
        mesh=mesh,
        in_specs=placed,
        out_specs=(
            P("dp", "seq", None),
            P("dp", "seq", None),
            P(("dp", "seq")),
            P(("dp", "seq")),
            P(("dp", "seq")),
            P(("dp", "seq"), None),
            P(("dp", "seq"), None),
            P(("dp", "seq"), None),
            P(None, ("dp", "seq")),
            P(("dp", "seq")),
            P(("dp", "seq"), None),
            P(("dp", "seq"), None),
            P(None, ("dp", "seq")),
        ),
        check_vma=False,
    )
```

time: 231 us -> 224 us (0.970)
  Pallas kernels: 226 us -> 221 us
    pallas_call x4 -> x3, Pallas kernels: 226 us -> 221 us  [the longest x1 120 us: attend(): pl.pallas_call(forward_kernel, out_shape=[jax.ShapeDtypeStruct(whole[NEAR...]
where the time goes in v5:
time: 224 us
  Pallas kernels  221 us (99%)
    pallas_call x1, Pallas kernels, attend(): pl.pallas_call(forward_kernel, out_shape=[jax.ShapeDtypeStruct(whole[NEAR...  120 us
    pallas_call x1, Pallas kernels, attend_back(): pl.pallas_call(backward_kernel, out_shape=[jax.ShapeDtypeStruct((2, 8, w)...  98.2 us

profile of v5, /device:TPU:1, one launch (start us, length us, event | category | flops | bytes accessed | tf_op | source)
XLA Modules:
  0.0 224.3 jit_solution(10294130732893132495)
XLA Ops:
  2.0 0.7 convert_bitcast_fusion
  2.6 1.0 multiply_sine_fusion
  3.6 120.2 %attend.1 = (bf16[2,4,4,2,2,8,2176]{6,5,4,3,2,1,0:T(8,128)(2,1)}, bf16[2,128,1024]{2,1,0:T(8,128)(2,1)}, f32[2,128,128]{2,1,0:T(8,128)}, bf16[8,256,128]{2,1,0:T...) custom-call(bf16[1,8]{1,0:T(2,128)(2,1)} %bitcast.28, ...), custom_call_target="tpu_custom_call" | custom-call | tf_op jit(solution)/shard_map/attend/pallas_call | solution.py:833
  123.8 98.2 %attend_back.1 = (f32[2,8,2176]{2,1,0:T(8,128)}, f32[2,8,5632]{2,1,0:T(8,128)}, bf16[128,1024]{1,0:T(8,128)(2,1)}) custom-call(bf16[8,256,128]{2,1,0:T(8,128)(2,1)} %get-tuple-element.46.refs_0_, bf16[8,256,128]{2,1,0:T(8,128)(2,1)} %get-tuple-element.47.refs_1_, bf16[8,256,128]{2,1,0:T(8,128)(2,1)} %get-tuple-element.48.refs_2_, ...), custom_call_target="tpu_custom_call" | custom-call | tf_op jit(solution)/shard_map/attend_back/pallas_call | solution.py:1059
  222.0 2.1 results.1
  (1 shorter events, 0.0 us)

commit v6 on v5

--- a/solution.py
+++ b/solution.py
@@ -137,17 +137,6 @@
     return [ring_device(axis, step, other) for axis in "xyz" for step in (1, 2, 3) for other in (0, 1)]
 
 
-def sequence_chip(number):
-    yh, z, x, yl, c = place()
-    return device(yh, z, number // 2, number % 2, c)
-
-
-def sequence_others():
-    yh, z, x, yl, c = place()
-    me = x * 2 + yl
-    return [sequence_chip((me + step) % 8) for step in range(1, 8)]
-
-
 HBM = pl.BlockSpec(memory_space=pltpu.HBM)
 VMEM = pl.BlockSpec(memory_space=pltpu.VMEM)
 
@@ -492,25 +481,28 @@
             copy.wait_send()
 
 
-def columns(head):
-    return pl.ds(pl.multiple_of(head * HEAD_DIM, HEAD_DIM), HEAD_DIM)
-
-
-def exchange_start(moves, me, send, recv, local, first):
-    copies = []
-    for step in range(1, 8):
-        there = (me + step) % 8
-        for n, (source, target) in enumerate(moves):
-            copy = pltpu.make_async_remote_copy(
-                source(there), target(me), send.at[first + n, step], recv.at[first + n, step],
-                device_id=sequence_chip(there),
+def columns(head, heads=1):
+    width = heads * HEAD_DIM
+    return pl.ds(pl.multiple_of(head * width, width), width)
+
+
+def y_partner():
+    yh, z, x, yl, c = place()
+    return device(yh, z, x, 1 - yl, c)
+
+
+def along_x(n, source, target, send, recv, local):
+    x = place()[2]
+    copies = [pltpu.make_async_copy(source(x), target(x), local.at[n])]
+    for step in (1, 2, 3):
+        copies.append(
+            pltpu.make_async_remote_copy(
+                source((x + step) % 4), target(x), send.at[n, step], recv.at[n, step],
+                device_id=ring_device("x", step, 0),
             )
-            copy.start()
-            copies.append(copy)
-    for n, (source, target) in enumerate(moves):
-        copy = pltpu.make_async_copy(source(me), target(me), local.at[first + n])
+        )
+    for copy in copies[1:] + copies[:1]:
         copy.start()
-        copies.append(copy)
     return copies
 
 
@@ -665,7 +657,6 @@
     send, recv, head_send, head_recv, local, load, store, pair_send, pair_recv, pair_local, own = refs
     weights = (w_near, w_far)
     yh, z, x, yl, c = place()
-    me = x * 2 + yl
     sib = sibling()
     lanes = lax.broadcasted_iota(jnp.int32, (TILE, TILE), 1)
     rows = lax.broadcasted_iota(jnp.int32, (TILE, TILE), 0)
@@ -687,7 +678,7 @@
     near_unit[0, :, 2048:] = tile
     near_unit[1, :, 2048:] = tile
     tab_own[...] = jnp.concatenate([cos_in[...], sin_in[...]], axis=1)
-    greet(ring_devices() + sequence_others() + [sib])
+    greet(ring_devices() + [sib])
     near, far = near_parts(), far_parts()
     gather = Gather((near_unit, far_unit), weights, (0, 3 * GATHER_SLOTS), send, recv, own)
     gather.spread(near)
@@ -752,13 +743,27 @@
             low_ref[:, n * 256 : n * 256 + 128] = head(pre[:, :128], gain)
             low_ref[:, n * 256 + 128 : n * 256 + 256] = head(pre[:, 128:], gain)
     v_low[...] = jnp.dot(normed[...], matrix(1536, 512), preferred_element_type=jnp.float32).astype(jnp.bfloat16)
-    arriving = exchange_start(
-        [
-            (lambda j: q_low.at[:, columns(j)], lambda i: q_ref.at[i]),
-            (lambda j: k_low.at[:, columns(j // 2)], lambda i: k_ref.at[i]),
-            (lambda j: v_low.at[:, columns(j // 2)], lambda i: v_ref.at[i]),
-        ],
-        me, head_send, head_recv, local, 0,
+    pairs_kv = ((k_low, k_ref), (v_low, v_ref))
+    ring_kv = [
+        along_x(
+            n, lambda t, low=low: low.at[:, columns(t)], lambda t, ref=ref: ref.at[2 * t + yl],
+            head_send, head_recv, local,
+        )
+        for n, (low, ref) in enumerate(pairs_kv)
+    ]
+    relays = []
+
+    def relay(n, step, source, target):
+        copy = pltpu.make_async_remote_copy(
+            source, target, head_send.at[4 + n, step], head_recv.at[4 + n, step], device_id=y_partner()
+        )
+        copy.start()
+        relays.append(copy)
+
+    for n, (low, ref) in enumerate(pairs_kv):
+        relay(n, 0, low.at[:, columns(x)], ref.at[2 * x + yl])
+    ring_q = along_x(
+        2, lambda t: q_low.at[:, columns(t, 2)], lambda t: q_ref.at[t], head_send, head_recv, local
     )
     stores = [
         pltpu.make_async_copy(a, b, store.at[n])
@@ -769,8 +774,17 @@
     ]
     for copy in stores[:3] + stores[7:]:
         copy.start()
-    for copy in arriving:
-        copy.wait()
+    for step in (1, 3, 2):
+        there = 2 * ((x - step + 4) % 4) + yl
+        for n, (_, ref) in enumerate(pairs_kv):
+            ring_kv[n][step].wait_recv()
+            relay(n, step, ref.at[there], ref.at[there])
+    for copies in (*ring_kv, ring_q):
+        copies[0].wait()
+    for step in (1, 2, 3):
+        ring_q[step].wait_recv()
+    for copy in relays:
+        copy.wait_recv()
     gather.forward(far[:1], 2)
     gather.ring(far[1], 2, 1)
     gather.ring(far[2], 2, 1)
@@ -779,33 +793,34 @@
     for j in range(8):
         vt[j] = v_ref[j].T
 
-    def one_block(i, _):
-        q = q_ref[i]
+    def one_block(n, _):
+        queries = (q_ref[n, :, :HEAD_DIM], q_ref[n, :, HEAD_DIM:])
 
         def weigh(j, carry):
-            total, mixed = carry
-            p = jnp.exp2(nt(k_ref[j], q) * (score_scale * log2e))
-            total = total + jnp.sum(p, axis=0, keepdims=True)
-            mixed = mixed + jnp.dot(vt[j], p.astype(jnp.bfloat16), preferred_element_type=jnp.float32)
-            return total, mixed
-
-        carry = (jnp.zeros((1, BLOCK), jnp.float32), jnp.zeros((HEAD_DIM, BLOCK), jnp.float32))
-        carry = lax.fori_loop(
-            0, (i + 1) // 2, lambda t, carry: weigh(2 * t + 1, weigh(2 * t, carry)), carry
-        )
-        total, mixed = lax.fori_loop(i // 2 * 2 + (i % 2) * 2, i + 1, weigh, carry)
-        out = (mixed / total).T
-        o32_ref[i] = out
-        o_low[i] = out.astype(jnp.bfloat16)
-        lse_ref[i] = jnp.log2(total)
+            after = []
+            for q, (total, mixed) in zip(queries, carry):
+                p = jnp.exp2(nt(k_ref[j], q) * (score_scale * log2e))
+                total = total + jnp.sum(p, axis=0, keepdims=True)
+                mixed = mixed + jnp.dot(
+                    vt[j], p.astype(jnp.bfloat16), preferred_element_type=jnp.float32
+                )
+                after.append((total, mixed))
+            return tuple(after)
+
+        start = (jnp.zeros((1, BLOCK), jnp.float32), jnp.zeros((HEAD_DIM, BLOCK), jnp.float32))
+        carry = lax.fori_loop(0, 2 * n + yl + 1, weigh, (start, start))
+        for h, (total, mixed) in enumerate(carry):
+            out = (mixed / total).T
+            o32_ref[n, :, h * HEAD_DIM : (h + 1) * HEAD_DIM] = out
+            o_low[n, :, h * HEAD_DIM : (h + 1) * HEAD_DIM] = out.astype(jnp.bfloat16)
+            lse_ref[n, h] = jnp.log2(total)
         return 0
 
-    lax.fori_loop(0, 6, one_block, 0)
+    lax.fori_loop(0, 3, one_block, 0)
     gather.forward(far[1:], 2)
-    lax.fori_loop(6, 8, one_block, 0)
-    leaving = exchange_start(
-        [(lambda j: o_low.at[j], lambda i: att.at[:, columns(i)])],
-        me, head_send, head_recv, local, 3,
+    lax.fori_loop(3, 4, one_block, 0)
+    leaving = along_x(
+        3, lambda t: o_low.at[t], lambda t: att.at[:, columns(t, 2)], head_send, head_recv, local
     )
     stores[6].start()
     g_low = g_ref[...].reshape(BLOCK, D)
@@ -824,10 +839,15 @@
     keep_near.wait()
     for _, away in pairs:
         away.wait_send()
+    for copies in (*ring_kv, ring_q):
+        for copy in copies[1:]:
+            copy.wait_send()
+    for copy in relays:
+        copy.wait_send()
 
 
 def attend(gains, shards, tokens):
-    blocks = (8, BLOCK, HEAD_DIM)
+    blocks, pairs = (8, BLOCK, HEAD_DIM), (4, BLOCK, 2 * HEAD_DIM)
     low, wide = jnp.bfloat16, jnp.float32
     whole = [(2, 4, 4, 2, 2, 8, w) for w in WIDE]
     return pl.pallas_call(
@@ -837,10 +857,12 @@
             jax.ShapeDtypeStruct((2, 128, D), low),
             jax.ShapeDtypeStruct((2, 128, HEAD_DIM), wide),
         ]
-        + [jax.ShapeDtypeStruct(blocks, low)] * 3
         + [
-            jax.ShapeDtypeStruct(blocks, wide),
-            jax.ShapeDtypeStruct((8, 1, BLOCK), wide),
+            jax.ShapeDtypeStruct(pairs, low),
+            jax.ShapeDtypeStruct(blocks, low),
+            jax.ShapeDtypeStruct(blocks, low),
+            jax.ShapeDtypeStruct(pairs, wide),
+            jax.ShapeDtypeStruct((4, 2, 1, BLOCK), wide),
             jax.ShapeDtypeStruct((BLOCK, D), low),
             jax.ShapeDtypeStruct((BLOCK, 1024), wide),
             jax.ShapeDtypeStruct((BLOCK, 512), wide),
@@ -866,10 +888,12 @@
             pltpu.VMEM((BLOCK, 512), low),
             pltpu.VMEM((BLOCK, 512), low),
         ]
-        + [pltpu.VMEM(blocks, low)] * 3
         + [
-            pltpu.VMEM(blocks, wide),
+            pltpu.VMEM(pairs, low),
             pltpu.VMEM(blocks, low),
+            pltpu.VMEM(blocks, low),
+            pltpu.VMEM(pairs, wide),
+            pltpu.VMEM(pairs, low),
             pltpu.VMEM((BLOCK, 1024), low),
             pltpu.VMEM((8, HEAD_DIM, BLOCK), low),
             pltpu.VMEM((2, 8, WIDE[0]), low),
@@ -880,8 +904,8 @@
         + [
             pltpu.SemaphoreType.DMA((6 * GATHER_SLOTS,)),
             pltpu.SemaphoreType.DMA((6 * GATHER_SLOTS,)),
-            pltpu.SemaphoreType.DMA((4, 8)),
-            pltpu.SemaphoreType.DMA((4, 8)),
+            pltpu.SemaphoreType.DMA((6, 4)),
+            pltpu.SemaphoreType.DMA((6, 4)),
             pltpu.SemaphoreType.DMA((4,)),
             pltpu.SemaphoreType.DMA((1,)),
             pltpu.SemaphoreType.DMA((9,)),
@@ -904,21 +928,19 @@
     fin, input_grad, held, refs = refs[:2], refs[2], refs[3:17], refs[17:]
     q_ref, k_ref, v_ref, o32_ref, lse_ref, qpre, kpre, normed, tab, rows, x_ref = held[:11]
     w_near, gmid, post = held[11:]
-    do_ref, dq_low, dk_low, dv_low, kt, dk_acc, dv_acc = refs[:7]
-    gq, kparts, vparts, dqkv, normed_t, pair_out, pair_in, near_grad = refs[7:15]
-    places, refs = refs[15 : 15 + n_scatter], refs[15 + n_scatter :]
+    do_ref, dq_low, dk_low, dv_low, kt, dk_acc, dv_acc, k_in, v_in, k_sum, v_sum = refs[:11]
+    gq, k_part_in, v_part_in, dqkv, normed_t, pair_out, pair_in, near_grad = refs[11:19]
+    places, refs = refs[19 : 19 + n_scatter], refs[19 + n_scatter :]
     send, recv, pair_send, pair_recv, load, far_load, head_send, head_recv, head_local = refs
     yh, z, x, yl, c = place()
-    me = x * 2 + yl
     sib = sibling()
     scatter = Scatter((near_grad, far_grad), fin, places, send, recv)
     loads = load_all(list(zip(ins, held)), load)
     for n, part in enumerate(far):
         scatter.load(part, far_load.at[n])
-    greet(ring_devices() + sequence_others() + [sib])
-    arriving = exchange_start(
-        [(lambda j: do_in.at[:, columns(j)], lambda i: do_ref.at[i])],
-        me, head_send, head_recv, head_local, 0,
+    greet(ring_devices() + [sib])
+    arriving = along_x(
+        0, lambda t: do_in.at[:, columns(t, 2)], lambda t: do_ref.at[t], head_send, head_recv, head_local
     )
     scatter.begin(far[:1], 0)
     scatter.begin(far[1:], 0)
@@ -931,40 +953,70 @@
     for copy in arriving:
         copy.wait()
 
-    def one_block(i, _):
-        q, do, lse = q_ref[i], do_ref[i], lse_ref[i]
-        delta = jnp.sum((do.astype(jnp.float32) * o32_ref[i]).T, axis=0, keepdims=True)
-
-        def one_pair(j, dqt):
-            p = jnp.exp2(nt(k_ref[j], q) * (score_scale * log2e) - lse)
-            dp = nt(v_ref[j], do)
-            ds = (p * (dp - delta)).astype(jnp.bfloat16)
-            dv_acc[j] += jnp.dot(p.astype(jnp.bfloat16), do, preferred_element_type=jnp.float32)
-            dk_acc[j] += jnp.dot(ds, q, preferred_element_type=jnp.float32)
-            return dqt + jnp.dot(kt[j], ds, preferred_element_type=jnp.float32)
-
-        dqt = lax.fori_loop(
-            0, (i + 1) // 2, lambda t, carry: one_pair(2 * t + 1, one_pair(2 * t, carry)),
-            jnp.zeros((HEAD_DIM, BLOCK), jnp.float32),
-        )
-        dqt = lax.fori_loop(i // 2 * 2 + (i % 2) * 2, i + 1, one_pair, dqt)
-        dq_low[i] = (dqt * score_scale).T.astype(jnp.bfloat16)
+    def one_block(n, _):
+        heads = []
+        for h in range(2):
+            at = slice(h * HEAD_DIM, (h + 1) * HEAD_DIM)
+            q, do = q_ref[n, :, at], do_ref[n, :, at]
+            delta = jnp.sum((do.astype(jnp.float32) * o32_ref[n, :, at]).T, axis=0, keepdims=True)
+            heads.append((q, do, lse_ref[n, h], delta))
+
+        def one_pair(j, dqts):
+            after, dk_term, dv_term = [], 0.0, 0.0
+            for (q, do, lse, delta), dqt in zip(heads, dqts):
+                p = jnp.exp2(nt(k_ref[j], q) * (score_scale * log2e) - lse)
+                ds = (p * (nt(v_ref[j], do) - delta)).astype(jnp.bfloat16)
+                dv_term += jnp.dot(p.astype(jnp.bfloat16), do, preferred_element_type=jnp.float32)
+                dk_term += jnp.dot(ds, q, preferred_element_type=jnp.float32)
+                after.append(dqt + jnp.dot(kt[j], ds, preferred_element_type=jnp.float32))
+            dv_acc[j // 2, j % 2] += dv_term
+            dk_acc[j // 2, j % 2] += dk_term
+            return tuple(after)
+
+        start = jnp.zeros((HEAD_DIM, BLOCK), jnp.float32)
+        dqts = lax.fori_loop(0, 2 * n + yl + 1, one_pair, (start, start))
+        for h, dqt in enumerate(dqts):
+            dq_low[n, :, h * HEAD_DIM : (h + 1) * HEAD_DIM] = (dqt * score_scale).T.astype(jnp.bfloat16)
         return 0
 
-    lax.fori_loop(0, 6, one_block, 0)
+    lax.fori_loop(0, 3, one_block, 0)
     scatter.middle(far[:1], 0)
     scatter.middle(far[1:], 0)
-    lax.fori_loop(6, 8, one_block, 0)
-    dk_low[...] = (dk_acc[...] * score_scale).astype(jnp.bfloat16)
-    dv_low[...] = dv_acc[...].astype(jnp.bfloat16)
-    arriving = exchange_start(
-        [
-            (lambda j: dq_low.at[j], lambda i: gq.at[:, columns(i)]),
-            (lambda j: dk_low.at[j], lambda i: kparts.at[i % 2, :, columns(i // 2)]),
-            (lambda j: dv_low.at[j], lambda i: vparts.at[i % 2, :, columns(i // 2)]),
-        ],
-        me, head_send, head_recv, head_local, 1,
+    lax.fori_loop(3, 4, one_block, 0)
+    sums = ((dk_acc, dk_low, k_in, k_sum, k_part_in, score_scale), (dv_acc, dv_low, v_in, v_sum, v_part_in, 1.0))
+    across = {}
+    for n, (acc, low, landing, _, _, scale) in enumerate(sums):
+        low[...] = (acc[:, 1 - yl] * scale).astype(jnp.bfloat16)
+        for step in (1, 2, 3, 0):
+            there = (x + step) % 4
+            copy = pltpu.make_async_remote_copy(
+                low.at[there], landing.at[there], head_send.at[4 + n, step], head_recv.at[4 + n, step],
+                device_id=y_partner(),
+            )
+            copy.start()
+            across[n, step] = copy
+    ring_q = along_x(
+        1, lambda t: dq_low.at[t], lambda t: gq.at[:, columns(t, 2)], head_send, head_recv, head_local
     )
+    ring_kv = []
+    for step in (1, 2, 3, 0):
+        there = (x + step) % 4
+        for n, (acc, _, landing, total, part_in, scale) in enumerate(sums):
+            across[n, step].wait_recv()
+            total[there] = (
+                acc[there, yl] * scale + landing[there].astype(jnp.float32)
+            ).astype(jnp.bfloat16)
+            target = part_in.at[:, columns(x)]
+            if step == 0:
+                copy = pltpu.make_async_copy(total.at[there], target, head_local.at[2 + n])
+            else:
+                copy = pltpu.make_async_remote_copy(
+                    total.at[there], target, head_send.at[2 + n, step], head_recv.at[2 + n, step],
+                    device_id=ring_device("x", step, 0),
+                )
+            copy.start()
+            ring_kv.append(copy)
+    arriving_late = ring_q + ring_kv
     scatter.end(far[:1], 0)
     scatter.begin(far[:1], 1)
     scatter.end(far[1:], 0)
@@ -972,7 +1024,7 @@
     for copy in loads[5:]:
         copy.wait()
     normed_t[...] = normed[...].T
-    for copy in arriving:
+    for copy in arriving_late:
         copy.wait()
     cosine, sine = rope_pair(tab)
     gain_q, gain_k = rows[2:3, :HEAD_DIM], rows[3:4, :HEAD_DIM]
@@ -990,11 +1042,11 @@
         q_part = q_part + part
     for h in range(4):
         at = slice(h * HEAD_DIM, (h + 1) * HEAD_DIM)
-        grad = kparts[0, :, at].astype(jnp.float32) + kparts[1, :, at].astype(jnp.float32)
+        grad = k_part_in[:, at].astype(jnp.float32)
         low_at = slice(1024 + h * HEAD_DIM, 1024 + (h + 1) * HEAD_DIM)
         dqkv[:, low_at], part = head_back(grad, kpre[:, at], gain_k)
         k_part = k_part + part
-    dqkv[:, 1536:] = (vparts[0].astype(jnp.float32) + vparts[1].astype(jnp.float32)).astype(jnp.bfloat16)
+    dqkv[:, 1536:] = v_part_in[...]
 
     def weight_grads(n, _):
         lhs = normed_t[pl.ds(pl.multiple_of(n * 256, 256), 256), :]
@@ -1051,10 +1103,12 @@
     scatter.finish(near)
     scatter.drain()
     swap.wait_send()
+    for copy in across.values():
+        copy.wait_send()
 
 
 def attend_back(arrays, far_grad, grad_att):
-    blocks = (8, BLOCK, HEAD_DIM)
+    blocks, pairs, split = (8, BLOCK, HEAD_DIM), (4, BLOCK, 2 * HEAD_DIM), (4, BLOCK, HEAD_DIM)
     low, wide = jnp.bfloat16, jnp.float32
     return pl.pallas_call(
         backward_kernel,
@@ -1063,14 +1117,18 @@
         in_specs=[HBM] * (len(arrays) + 2),
         out_specs=[VMEM] * 3,
         scratch_shapes=[pltpu.VMEM(a.shape, a.dtype) for a in arrays]
-        + [pltpu.VMEM(blocks, low)] * 4
+        + [pltpu.VMEM(pairs, low)] * 2
+        + [pltpu.VMEM(split, low)] * 2
         + [
             pltpu.VMEM((8, HEAD_DIM, BLOCK), low),
-            pltpu.VMEM(blocks, wide),
-            pltpu.VMEM(blocks, wide),
+            pltpu.VMEM((4, 2, BLOCK, HEAD_DIM), wide),
+            pltpu.VMEM((4, 2, BLOCK, HEAD_DIM), wide),
+        ]
+        + [pltpu.VMEM(split, low)] * 4
+        + [
             pltpu.VMEM((BLOCK, 1024), low),
-            pltpu.VMEM((2, BLOCK, 512), low),
-            pltpu.VMEM((2, BLOCK, 512), low),
+            pltpu.VMEM((BLOCK, 512), low),
+            pltpu.VMEM((BLOCK, 512), low),
             pltpu.VMEM((BLOCK, 2048), low),
             pltpu.VMEM((D, BLOCK), low),
             pltpu.VMEM((128, D), low),
@@ -1085,8 +1143,8 @@
             pltpu.SemaphoreType.DMA((1,)),
             pltpu.SemaphoreType.DMA((len(arrays),)),
             pltpu.SemaphoreType.DMA((3, 4)),
-            pltpu.SemaphoreType.DMA((4, 8)),
-            pltpu.SemaphoreType.DMA((4, 8)),
+            pltpu.SemaphoreType.DMA((6, 4)),
+            pltpu.SemaphoreType.DMA((6, 4)),
             pltpu.SemaphoreType.DMA((4,)),
         ],
         compiler_params=pltpu.CompilerParams(

time: 224 us -> 208 us (0.929)
  Pallas kernels: 221 us -> 204 us
    pallas_call x1, Pallas kernels: 98.2 us -> 90 us  [attend_back(): pl.pallas_call(backward_kernel, out_shape=[jax.ShapeDtypeStruct((2, 8, w)...]
    pallas_call x1, Pallas kernels: 120 us -> 112 us  [attend(): pl.pallas_call(forward_kernel, out_shape=[jax.ShapeDtypeStruct(whole[NEAR...]
where the time goes in v6:
time: 208 us
  Pallas kernels  204 us (98%)
    pallas_call x1, Pallas kernels, attend(): pl.pallas_call(forward_kernel, out_shape=[jax.ShapeDtypeStruct(whole[NEAR...  112 us
    pallas_call x1, Pallas kernels, attend_back(): pl.pallas_call(backward_kernel, out_shape=[jax.ShapeDtypeStruct((2, 8, w)...  90 us

profile of v6, /device:TPU:1, one launch (start us, length us, event | category | flops | bytes accessed | tf_op | source)
XLA Modules:
  0.0 208.1 jit_solution(1319749676501635261)
XLA Ops:
  2.0 0.7 convert_bitcast_fusion
  2.6 1.0 multiply_sine_fusion
  3.6 112.3 %attend.1 = (bf16[2,4,4,2,2,8,2176]{6,5,4,3,2,1,0:T(8,128)(2,1)}, bf16[2,128,1024]{2,1,0:T(8,128)(2,1)}, f32[2,128,128]{2,1,0:T(8,128)}, bf16[4,256,256]{2,1,0:T...) custom-call(bf16[1,8]{1,0:T(2,128)(2,1)} %bitcast.28, ...), custom_call_target="tpu_custom_call" | custom-call | tf_op jit(solution)/shard_map/attend/pallas_call | solution.py:853
  115.9 90.0 %attend_back.1 = (f32[2,8,2176]{2,1,0:T(8,128)}, f32[2,8,5632]{2,1,0:T(8,128)}, bf16[128,1024]{1,0:T(8,128)(2,1)}) custom-call(bf16[4,256,256]{2,1,0:T(8,128)(2,1)} %get-tuple-element.46.refs_0_, bf16[8,256,128]{2,1,0:T(8,128)(2,1)} %get-tuple-element.47.refs_1_, bf16[8,256,128]{2,1,0:T(8,128)(2,1)} %get-tuple-element.48.refs_2_, ...), custom_call_target="tpu_custom_call" | custom-call | tf_op jit(solution)/shard_map/attend_back/pallas_call | solution.py:1113
  205.9 2.1 %results.1 = (f32[8,2048]{1,0:T(8,128)}, f32[8,1024]{1,0:T(8,128)}, f32[8,1024]{1,0:T(8,128)}, f32[1,8]{1,0:T(1,128)}, f32[1,8]{1,0:T(1,128)}, /*index=5*/f32[1,...) custom-call(f32[2,8,2176]{2,1,0:T(8,128)} %get-tuple-element.62.near, ...), custom_call_target="tpu_custom_call" | custom-call | tf_op jit(solution)/shard_map/results/pallas_call | solution.py:1177
  (1 shorter events, 0.0 us)

commit v7 on v6

--- a/solution.py
+++ b/solution.py
@@ -111,8 +111,8 @@
     return parts_of(NEAR, (6, 6, 5))
 
 
-def far_parts():
-    return parts_of(FAR, (20, 12, 12))
+def far_parts(tiles=(17, 14, 13)):
+    return parts_of(FAR, tiles)
 
 
 def greet(others):
@@ -506,7 +506,7 @@
     return copies
 
 
-FAR_SPANS = ((0, 1024), (1024, 1536), (2560, 1536), (4096, 1536))
+FAR_SPANS = ((3072, 1024), (0, 1536), (1536, 1536), (4096, 1536))
 
 
 def middle_shapes():
@@ -534,7 +534,7 @@
     ]
 
 
-def middle_layer(att, x_ref, g_low, rows, w_far, refs, outs, pair_send, pair_recv, sems, c, sib):
+def middle_layer(gather, far, att, x_ref, g_low, rows, w_far, refs, outs, pair_send, pair_recv, sems, c, sib):
     output, grad_att_out, gmid_out, post_out, dw_out = outs
     (branch, middle, hidden, g_t, hidden_t, grad_act, act, gate_grad, up_grad, grad_hidden,
      down_own, grad_att, dw, out1, in1, out2, in2, out3, in3) = refs
@@ -568,6 +568,7 @@
         branch[:, part(n)] = block
         out1[n] = block.astype(jnp.bfloat16)
         first.append(swap(out1.at[n], in1.at[n]))
+    gather.arrive(far[2:], 2)
     for n in range(6):
         grad_act[:, part(n)] = jnp.dot(g_low, far_cols(3, n), preferred_element_type=jnp.float32)
     for n in range(4):
@@ -579,6 +580,7 @@
     gain = rows[1:2, :]
     scale = rms_scale(middle[...])
     hidden[...] = (middle[...] * scale * gain).astype(jnp.bfloat16)
+    gather.arrive(far[:1], 2)
     for n in range(6):
         gate = jnp.dot(hidden[...], far_cols(1, n), preferred_element_type=jnp.float32)
         up = jnp.dot(hidden[...], far_cols(2, n), preferred_element_type=jnp.float32)
@@ -633,10 +635,10 @@
         ).astype(jnp.bfloat16)
     keep(grad_att, grad_att_out)
     for n in range(4):
-        dw[part(n), :1024] = jnp.dot(
+        dw[part(n), pl.ds(*FAR_SPANS[0])] = jnp.dot(
             branch_t[part(n), :], att[...], preferred_element_type=jnp.float32
         ).astype(jnp.bfloat16)
-    keep(dw.at[:, pl.ds(0, 1024)], dw_out.at[:, pl.ds(0, 1024)])
+    keep(dw.at[:, pl.ds(*FAR_SPANS[0])], dw_out.at[:, pl.ds(*FAR_SPANS[0])])
     third.wait_recv()
     output[...] = (
         middle[own, :] + (down_own[...] + in3[...].astype(jnp.float32))
@@ -669,17 +671,17 @@
             value = jnp.concatenate([value, jnp.zeros((1, TILE - 8), jnp.float32)], axis=1)
             tile = jnp.where(rows == n, value, tile)
     tile = tile.T[:8].astype(jnp.bfloat16)
-    for unit, group, first in ((near_unit, shards[:3], 0), (far_unit, shards[3:], 0)):
-        for shard in group:
-            width = shard.shape[1] // 2
-            for half in range(2):
-                unit[half, :, first : first + width] = shard[:, half * width : (half + 1) * width]
-            first += width
+    places = [(near_unit, 0), (near_unit, 1024), (near_unit, 1536)]
+    places += [(far_unit, first) for first, _ in FAR_SPANS]
+    for shard, (unit, first) in zip(shards, places):
+        width = shard.shape[1] // 2
+        for half in range(2):
+            unit[half, :, first : first + width] = shard[:, half * width : (half + 1) * width]
     near_unit[0, :, 2048:] = tile
     near_unit[1, :, 2048:] = tile
     tab_own[...] = jnp.concatenate([cos_in[...], sin_in[...]], axis=1)
     greet(ring_devices() + [sib])
-    near, far = near_parts(), far_parts()
+    near, far = near_parts(), far_parts((21, 11, 12))
     gather = Gather((near_unit, far_unit), weights, (0, 3 * GATHER_SLOTS), send, recv, own)
     gather.spread(near)
     pairs = []
@@ -695,10 +697,12 @@
     for part in near:
         gather.settle(part)
         gather.direct(part)
+    gather.settle(far[0])
+    gather.begin(far[:1], 1)
     for part in near:
         gather.landed(part)
         gather.begin([part], 2)
-    for part in far:
+    for part in far[1:]:
         gather.settle(part)
         gather.begin([part], 1)
     gather.forward(near, 2)
@@ -788,6 +792,7 @@
     gather.forward(far[:1], 2)
     gather.ring(far[1], 2, 1)
     gather.ring(far[2], 2, 1)
+    gather.forward(far[1:], 2)
     for copy in stores[3:6]:
         copy.start()
     for j in range(8):
@@ -817,7 +822,6 @@
         return 0
 
     lax.fori_loop(0, 3, one_block, 0)
-    gather.forward(far[1:], 2)
     lax.fori_loop(3, 4, one_block, 0)
     leaving = along_x(
         3, lambda t: o_low.at[t], lambda t: att.at[:, columns(t, 2)], head_send, head_recv, local
@@ -826,11 +830,11 @@
     g_low = g_ref[...].reshape(BLOCK, D)
     g_t = middle_refs[3]
     g_t[...] = g_low.T
-    gather.arrive(far, 2)
+    gather.arrive(far[1:2], 2)
     for copy in leaving:
         copy.wait()
     middle_layer(
-        att, x_ref, g_low, rows_ref, w_far, middle_refs, (output, grad_att_out, gmid_out, post_out, dw_out),
+        gather, far, att, x_ref, g_low, rows_ref, w_far, middle_refs, (output, grad_att_out, gmid_out, post_out, dw_out),
         pair_send, pair_recv, own, c, sib,
     )
     gather.drain()
@@ -1016,16 +1020,9 @@
                 )
             copy.start()
             ring_kv.append(copy)
-    arriving_late = ring_q + ring_kv
-    scatter.end(far[:1], 0)
-    scatter.begin(far[:1], 1)
-    scatter.end(far[1:], 0)
-    scatter.begin(far[1:], 1)
     for copy in loads[5:]:
         copy.wait()
     normed_t[...] = normed[...].T
-    for copy in arriving_late:
-        copy.wait()
     cosine, sine = rope_pair(tab)
     gain_q, gain_k = rows[2:3, :HEAD_DIM], rows[3:4, :HEAD_DIM]
 
@@ -1034,31 +1031,42 @@
         grad_in, terms = norm_back(grad, values, rms_scale(values), gain)
         return grad_in.astype(jnp.bfloat16), jnp.sum(terms, axis=0, keepdims=True)
 
+    def weight_grads(first):
+        def one(n, _):
+            lhs = normed_t[pl.ds(pl.multiple_of(n * 256, 256), 256), :]
+            for at in (first, first + 512):
+                block = jnp.dot(lhs, dqkv[:, at : at + 512], preferred_element_type=jnp.float32)
+                near_grad[n // 2, pl.ds(n % 2 * 2, 2), :, :, :, at : at + 512] = block.astype(
+                    jnp.bfloat16
+                ).reshape(2, 4, 2, 16, 512)
+            return 0
+
+        lax.fori_loop(0, 4, one, 0)
+
+    for copy in ring_q:
+        copy.wait()
     q_part = jnp.zeros((1, HEAD_DIM), jnp.float32)
     k_part = jnp.zeros((1, HEAD_DIM), jnp.float32)
     for h in range(8):
         at = slice(h * HEAD_DIM, (h + 1) * HEAD_DIM)
         dqkv[:, at], part = head_back(gq[:, at].astype(jnp.float32), qpre[:, at], gain_q)
         q_part = q_part + part
+    weight_grads(0)
+    scatter.begin(near[:1], 0)
+    scatter.end(far[:1], 0)
+    scatter.begin(far[:1], 1)
+    scatter.end(far[1:], 0)
+    scatter.begin(far[1:], 1)
+    for copy in ring_kv:
+        copy.wait()
     for h in range(4):
         at = slice(h * HEAD_DIM, (h + 1) * HEAD_DIM)
-        grad = k_part_in[:, at].astype(jnp.float32)
         low_at = slice(1024 + h * HEAD_DIM, 1024 + (h + 1) * HEAD_DIM)
-        dqkv[:, low_at], part = head_back(grad, kpre[:, at], gain_k)
+        dqkv[:, low_at], part = head_back(k_part_in[:, at].astype(jnp.float32), kpre[:, at], gain_k)
         k_part = k_part + part
     dqkv[:, 1536:] = v_part_in[...]
-
-    def weight_grads(n, _):
-        lhs = normed_t[pl.ds(pl.multiple_of(n * 256, 256), 256), :]
-        for first in range(0, 2048, 512):
-            block = jnp.dot(lhs, dqkv[:, first : first + 512], preferred_element_type=jnp.float32)
-            near_grad[n // 2, pl.ds(n % 2 * 2, 2), :, :, :, first : first + 512] = block.astype(
-                jnp.bfloat16
-            ).reshape(2, 4, 2, 16, 512)
-        return 0
-
-    lax.fori_loop(0, 4, weight_grads, 0)
-    scatter.begin(near[:2], 0)
+    weight_grads(1024)
+    scatter.begin(near[1:2], 0)
 
     def grad_normed(rows_at):
         return nt(dqkv[rows_at, :], w_near[:, :2048])

time: 208 us -> 204 us (0.981)
  Pallas kernels: 204 us -> 200 us
    pallas_call x1, Pallas kernels: 112 us -> 109 us  [attend(): pl.pallas_call(forward_kernel, out_shape=[jax.ShapeDtypeStruct(whole[NEAR...]
where the time goes in v7:
time: 204 us
  Pallas kernels  200 us (98%)
  between operations  2.05 us (1%)
    pallas_call x1, Pallas kernels, attend(): pl.pallas_call(forward_kernel, out_shape=[jax.ShapeDtypeStruct(whole[NEAR...  109 us
    pallas_call x1, Pallas kernels, attend_back(): pl.pallas_call(backward_kernel, out_shape=[jax.ShapeDtypeStruct((2, 8, w)...  88.3 us

profile of v7, /device:TPU:1, one launch (start us, length us, event | category | flops | bytes accessed | tf_op | source)
XLA Modules:
  0.0 203.6 jit_solution(8331488200715781800)
XLA Ops:
  2.0 0.7 convert_bitcast_fusion
  2.6 1.0 multiply_sine_fusion
  3.6 109.5 %attend.1 = (bf16[2,4,4,2,2,8,2176]{6,5,4,3,2,1,0:T(8,128)(2,1)}, bf16[2,128,1024]{2,1,0:T(8,128)(2,1)}, f32[2,128,128]{2,1,0:T(8,128)}, bf16[4,256,256]{2,1,0:T...) custom-call(bf16[1,8]{1,0:T(2,128)(2,1)} %bitcast.28, ...), custom_call_target="tpu_custom_call" | custom-call | tf_op jit(solution)/shard_map/attend/pallas_call | solution.py:857
  113.1 88.3 %attend_back.1 = (f32[2,8,2176]{2,1,0:T(8,128)}, f32[2,8,5632]{2,1,0:T(8,128)}, bf16[128,1024]{1,0:T(8,128)(2,1)}) custom-call(bf16[4,256,256]{2,1,0:T(8,128)(2,1)} %get-tuple-element.46.refs_0_, bf16[8,256,128]{2,1,0:T(8,128)(2,1)} %get-tuple-element.47.refs_1_, bf16[8,256,128]{2,1,0:T(8,128)(2,1)} %get-tuple-element.48.refs_2_, ...), custom_call_target="tpu_custom_call" | custom-call | tf_op jit(solution)/shard_map/attend_back/pallas_call | solution.py:1121
  201.3 2.1 %results.1 = (f32[8,2048]{1,0:T(8,128)}, f32[8,1024]{1,0:T(8,128)}, f32[8,1024]{1,0:T(8,128)}, f32[1,8]{1,0:T(1,128)}, f32[1,8]{1,0:T(1,128)}, /*index=5*/f32[1,...) custom-call(f32[2,8,2176]{2,1,0:T(8,128)} %get-tuple-element.62.near, ...), custom_call_target="tpu_custom_call" | custom-call | tf_op jit(solution)/shard_map/results/pallas_call | solution.py:1185
  (1 shorter events, 0.0 us)

commit v8 on v7

--- a/solution.py
+++ b/solution.py
@@ -356,9 +356,11 @@
                 copy.start()
                 self.loads[name, half, m] = copy
 
-    def ring(self, part, phase, which):
+    def ring(self, part, phase, which, halves=(0, 1)):
         name = (part.array, part.number)
         for half, way, first, width in part.halves:
+            if half not in halves:
+                continue
             offset, step = ((2, way), (-way, -way))[which]
             self.remote(
                 (name, phase, which, half), part, 6 * phase + 2 * which + half,
@@ -366,11 +368,11 @@
                 ring_device(part.order[2 - phase], step, 0),
             )
 
-    def begin(self, parts, phase):
+    def begin(self, parts, phase, halves=(0, 1)):
         for part in parts:
-            self.ring(part, phase, 0)
+            self.ring(part, phase, 0, halves)
         for part in parts:
-            self.ring(part, phase, 1)
+            self.ring(part, phase, 1, halves)
 
     def middle(self, parts, phase):
         for part in parts:
@@ -492,6 +494,13 @@
 
 
 def along_x(n, source, target, send, recv, local):
+    copies = moves_along_x(n, source, target, send, recv, local)
+    for copy in copies[1:] + copies[:1]:
+        copy.start()
+    return copies
+
+
+def moves_along_x(n, source, target, send, recv, local):
     x = place()[2]
     copies = [pltpu.make_async_copy(source(x), target(x), local.at[n])]
     for step in (1, 2, 3):
@@ -501,8 +510,6 @@
                 device_id=ring_device("x", step, 0),
             )
         )
-    for copy in copies[1:] + copies[:1]:
-        copy.start()
     return copies
 
 
@@ -821,11 +828,12 @@
             lse_ref[n, h] = jnp.log2(total)
         return 0
 
-    lax.fori_loop(0, 3, one_block, 0)
-    lax.fori_loop(3, 4, one_block, 0)
-    leaving = along_x(
+    leaving = moves_along_x(
         3, lambda t: o_low.at[t], lambda t: att.at[:, columns(t, 2)], head_send, head_recv, local
     )
+    for step in (2, 1, 3, 0):
+        one_block((x + step) % 4, 0)
+        leaving[step].start()
     stores[6].start()
     g_low = g_ref[...].reshape(BLOCK, D)
     g_t = middle_refs[3]
@@ -983,10 +991,16 @@
             dq_low[n, :, h * HEAD_DIM : (h + 1) * HEAD_DIM] = (dqt * score_scale).T.astype(jnp.bfloat16)
         return 0
 
-    lax.fori_loop(0, 3, one_block, 0)
+    ring_q = moves_along_x(
+        1, lambda t: dq_low.at[t], lambda t: gq.at[:, columns(t, 2)], head_send, head_recv, head_local
+    )
+    for step in (2, 1, 3):
+        one_block((x + step) % 4, 0)
+        ring_q[step].start()
     scatter.middle(far[:1], 0)
     scatter.middle(far[1:], 0)
-    lax.fori_loop(3, 4, one_block, 0)
+    one_block(x, 0)
+    ring_q[0].start()
     sums = ((dk_acc, dk_low, k_in, k_sum, k_part_in, score_scale), (dv_acc, dv_low, v_in, v_sum, v_part_in, 1.0))
     across = {}
     for n, (acc, low, landing, _, _, scale) in enumerate(sums):
@@ -999,9 +1013,6 @@
             )
             copy.start()
             across[n, step] = copy
-    ring_q = along_x(
-        1, lambda t: dq_low.at[t], lambda t: gq.at[:, columns(t, 2)], head_send, head_recv, head_local
-    )
     ring_kv = []
     for step in (1, 2, 3, 0):
         there = (x + step) % 4
@@ -1067,6 +1078,7 @@
     dqkv[:, 1536:] = v_part_in[...]
     weight_grads(1024)
     scatter.begin(near[1:2], 0)
+    scatter.begin(near[2:], 0, (0,))
 
     def grad_normed(rows_at):
         return nt(dqkv[rows_at, :], w_near[:, :2048])
@@ -1095,7 +1107,7 @@
         [in_part, post[0:1, :], qk[0:2], jnp.zeros((TILE - 4, D), jnp.float32)]
     )
     near_grad[:, :, :, :, :, 2048:] = gain_rows.T.astype(jnp.bfloat16).reshape(2, 4, 4, 2, 16, TILE)
-    scatter.begin(near[2:], 0)
+    scatter.begin(near[2:], 0, (1,))
     scatter.middle(near, 0)
     scatter.middle(far, 1)
     for part in near:

time: 204 us -> 201 us (0.985)
  Pallas kernels: 200 us -> 197 us
where the time goes in v8:
time: 201 us
  Pallas kernels  197 us (98%)
  between operations  2.05 us (1%)
    pallas_call x1, Pallas kernels, attend(): pl.pallas_call(forward_kernel, out_shape=[jax.ShapeDtypeStruct(whole[NEAR...  108 us
    pallas_call x1, Pallas kernels, attend_back(): pl.pallas_call(backward_kernel, out_shape=[jax.ShapeDtypeStruct((2, 8, w)...  87.5 us

profile of v8, /device:TPU:1, one launch (start us, length us, event | category | flops | bytes accessed | tf_op | source)
XLA Modules:
  0.0 201.2 jit_solution(12443299994660290873)
XLA Ops:
  2.0 0.7 convert_bitcast_fusion
  2.6 1.0 multiply_sine_fusion
  3.6 107.8 %attend.1 = (bf16[2,4,4,2,2,8,2176]{6,5,4,3,2,1,0:T(8,128)(2,1)}, bf16[2,128,1024]{2,1,0:T(8,128)(2,1)}, f32[2,128,128]{2,1,0:T(8,128)}, bf16[4,256,256]{2,1,0:T...) custom-call(bf16[1,8]{1,0:T(2,128)(2,1)} %bitcast.28, ...), custom_call_target="tpu_custom_call" | custom-call | tf_op jit(solution)/shard_map/attend/pallas_call | solution.py:865
  111.4 87.5 %attend_back.1 = (f32[2,8,2176]{2,1,0:T(8,128)}, f32[2,8,5632]{2,1,0:T(8,128)}, bf16[128,1024]{1,0:T(8,128)(2,1)}) custom-call(bf16[4,256,256]{2,1,0:T(8,128)(2,1)} %get-tuple-element.46.refs_0_, bf16[8,256,128]{2,1,0:T(8,128)(2,1)} %get-tuple-element.47.refs_1_, bf16[8,256,128]{2,1,0:T(8,128)(2,1)} %get-tuple-element.48.refs_2_, ...), custom_call_target="tpu_custom_call" | custom-call | tf_op jit(solution)/shard_map/attend_back/pallas_call | solution.py:1133
  198.9 2.1 %results.1 = (f32[8,2048]{1,0:T(8,128)}, f32[8,1024]{1,0:T(8,128)}, f32[8,1024]{1,0:T(8,128)}, f32[1,8]{1,0:T(1,128)}, f32[1,8]{1,0:T(1,128)}, /*index=5*/f32[1,...) custom-call(f32[2,8,2176]{2,1,0:T(8,128)} %get-tuple-element.62.near, ...), custom_call_target="tpu_custom_call" | custom-call | tf_op jit(solution)/shard_map/results/pallas_call | solution.py:1197
  (1 shorter events, 0.0 us)

commit v9 on v8

--- a/solution.py
+++ b/solution.py
@@ -119,7 +119,10 @@
     barrier = pltpu.get_barrier_semaphore()
     for other in others:
         pl.semaphore_signal(barrier, inc=1, device_id=other)
-    pl.semaphore_wait(barrier, len(others))
+
+
+def await_greetings(others):
+    pl.semaphore_wait(pltpu.get_barrier_semaphore(), len(others))
 
 
 def ring_device(axis, step, other):
@@ -667,6 +670,8 @@
     weights = (w_near, w_far)
     yh, z, x, yl, c = place()
     sib = sibling()
+    others = ring_devices() + [sib]
+    greet(others)
     lanes = lax.broadcasted_iota(jnp.int32, (TILE, TILE), 1)
     rows = lax.broadcasted_iota(jnp.int32, (TILE, TILE), 0)
     tile = jnp.zeros((TILE, TILE), jnp.float32)
@@ -687,7 +692,7 @@
     near_unit[0, :, 2048:] = tile
     near_unit[1, :, 2048:] = tile
     tab_own[...] = jnp.concatenate([cos_in[...], sin_in[...]], axis=1)
-    greet(ring_devices() + [sib])
+    await_greetings(others)
     near, far = near_parts(), far_parts((21, 11, 12))
     gather = Gather((near_unit, far_unit), weights, (0, 3 * GATHER_SLOTS), send, recv, own)
     gather.spread(near)
@@ -951,6 +956,7 @@
     for n, part in enumerate(far):
         scatter.load(part, far_load.at[n])
     greet(ring_devices() + [sib])
+    await_greetings(ring_devices() + [sib])
     arriving = along_x(
         0, lambda t: do_in.at[:, columns(t, 2)], lambda t: do_ref.at[t], head_send, head_recv, head_local
     )

time: 201 us -> 201 us (level)
  no operation moved by 1% of the time
where the time goes in v9:
time: 201 us
  Pallas kernels  197 us (98%)
  between operations  2.05 us (1%)
    pallas_call x1, Pallas kernels, attend(): pl.pallas_call(forward_kernel, out_shape=[jax.ShapeDtypeStruct(whole[NEAR...  108 us
    pallas_call x1, Pallas kernels, attend_back(): pl.pallas_call(backward_kernel, out_shape=[jax.ShapeDtypeStruct((2, 8, w)...  87.6 us

profile of v9, /device:TPU:1, one launch (start us, length us, event | category | flops | bytes accessed | tf_op | source)
XLA Modules:
  0.0 201.0 jit_solution(3880658978589459935)
XLA Ops:
  2.0 0.7 convert_bitcast_fusion
  2.6 1.0 multiply_sine_fusion
  3.6 107.6 %attend.1 = (bf16[2,4,4,2,2,8,2176]{6,5,4,3,2,1,0:T(8,128)(2,1)}, bf16[2,128,1024]{2,1,0:T(8,128)(2,1)}, f32[2,128,128]{2,1,0:T(8,128)}, bf16[4,256,256]{2,1,0:T...) custom-call(bf16[1,8]{1,0:T(2,128)(2,1)} %bitcast.28, ...), custom_call_target="tpu_custom_call" | custom-call | tf_op jit(solution)/shard_map/attend/pallas_call | solution.py:870
  111.2 87.6 %attend_back.1 = (f32[2,8,2176]{2,1,0:T(8,128)}, f32[2,8,5632]{2,1,0:T(8,128)}, bf16[128,1024]{1,0:T(8,128)(2,1)}) custom-call(bf16[4,256,256]{2,1,0:T(8,128)(2,1)} %get-tuple-element.46.refs_0_, bf16[8,256,128]{2,1,0:T(8,128)(2,1)} %get-tuple-element.47.refs_1_, bf16[8,256,128]{2,1,0:T(8,128)(2,1)} %get-tuple-element.48.refs_2_, ...), custom_call_target="tpu_custom_call" | custom-call | tf_op jit(solution)/shard_map/attend_back/pallas_call | solution.py:1139
  198.8 2.1 %results.1 = (f32[8,2048]{1,0:T(8,128)}, f32[8,1024]{1,0:T(8,128)}, f32[8,1024]{1,0:T(8,128)}, f32[1,8]{1,0:T(1,128)}, f32[1,8]{1,0:T(1,128)}, /*index=5*/f32[1,...) custom-call(f32[2,8,2176]{2,1,0:T(8,128)} %get-tuple-element.62.near, ...), custom_call_target="tpu_custom_call" | custom-call | tf_op jit(solution)/shard_map/results/pallas_call | solution.py:1203
  (1 shorter events, 0.0 us)
